TPU v7x, 128 devices: a whole 4x4x4 slice. The times are simulated.
128 devices in a mesh: coil: 4 (over z), slab: 32 (over x, y, core).
Axes of the slice: x: 4, y: 4, z: 4, core: 2. Of those that a mesh axis runs over, the one named last changes fastest.
Arguments:
- image: float32 [2, 256, 256, 128], P(None, 'slab'), may hold values from -6 to 6
- sensitivity: bfloat16 [16, 2, 256, 256, 128], P('coil', None, 'slab'), may hold values from -5 to 5
- blocks: bfloat16 [32, 24, 128, 512], P('slab'), may hold values from -0.25 to 0.25
- samples: bfloat16 [32, 24, 128, 16, 2, 128], P('slab', None, None, 'coil'), may hold values from -6 to 6
- offsets: int32 [32, 24], P('slab'), may hold values from 0 to 192
- counts: int32 [32], P('slab'), may hold values from 1 to 24, as said below
- auxiliary: float32 [2, 256, 256, 128], P(None, 'slab', 'coil'), may hold values from -4 to 4
- scaled_dual: float32 [2, 256, 256, 128], P(None, 'slab', 'coil'), may hold values from -3 to 3
Outputs:
- image_next: float32 [2, 256, 256, 128], P(None, 'slab', 'coil')
- auxiliary_next: float32 [2, 256, 256, 128], P(None, 'slab', 'coil')
- dual_next: float32 [2, 256, 256, 128], P(None, 'slab', 'coil')
Inputs may be any that keep to these rules, and one draw needn't show every extreme that they name: Each tile's live groups are its first counts slots; some tile holds 24 live groups.
All inputs are finite; a program needn't handle non-finite values.
Results may differ from a plain program's by a relative error of at most 0.014.
Values may be sent and summed in bfloat16 or wider, within the bound.
No kernel may reach another device: no remote copies, remote signals or barrier semaphores. Data moves between devices by JAX's collectives and lax.ppermute only.
A program may use at most 128 MiB of HBM per device.

v0:
```python
import math

import jax
import jax.numpy as jnp
import numpy as np
import ml_dtypes
from jax import lax
from jax.experimental import pallas as pl
from jax.experimental.pallas import tpu as pltpu
from jax.sharding import PartitionSpec as P

N = 256
Z = 128
WIN = 64
P_SIZE = 128
CH = 24
KYD = 8
TILES = 32
CELLS = WIN * KYD
ROWS = N * KYD
NCOIL = 4

step_size = 0.5
penalty = 1.0
threshold = 0.3

BF = jnp.bfloat16
F32 = jnp.float32


def dft_parts():
    index = np.arange(N)
    angle = (index[:, None] * index[None, :] % N).astype(np.float32) * np.float32(2.0 * math.pi / N)
    factor = np.float32(1.0 / math.sqrt(N))
    re = (np.cos(angle) * factor).astype(ml_dtypes.bfloat16)
    im = (-np.sin(angle) * factor).astype(ml_dtypes.bfloat16)
    return re, im


def real_tables():
    re, im = dft_parts()
    along_y = np.stack(
        [np.concatenate([re, -im], 1), np.concatenate([im, re], 1)], 1
    ).reshape(2 * N, 2 * N)
    re_c = re.reshape(N, TILES, KYD)
    im_c = im.reshape(N, TILES, KYD)
    along_x = np.stack(
        [np.stack([re_c, -im_c], 2), np.stack([im_c, re_c], 2)], 0
    ).reshape(2 * N, 2 * N)
    return along_y, along_x


def coil_kernel(table_ref, sens_ref, image_ref, out_ref, spread):
    step = pl.program_id(0)
    parts = []
    for i in range(2):
        s_re = sens_ref[0, 0, i].astype(F32)
        s_im = sens_ref[0, 1, i].astype(F32)
        m_re = image_ref[0, i]
        m_im = image_ref[1, i]
        c_re = (s_re * m_re - s_im * m_im).astype(BF)
        c_im = (s_re * m_im + s_im * m_re).astype(BF)
        parts.append(jnp.concatenate([c_re, c_im], 0))
    data = jnp.concatenate(parts, 1)
    result = jnp.dot(table_ref[...], data, preferred_element_type=F32)
    for i in range(2):
        spread[pl.ds(2 * step + i, 2 * N, stride=KYD), :] = result[:, i * Z : (i + 1) * Z]

    @pl.when(step == 3)
    def _():
        out_ref[...] = spread[...].astype(BF)


def coil_forward(coil, table, sensitivity, image):
    return pl.pallas_call(
        coil_kernel,
        out_shape=jax.ShapeDtypeStruct((TILES * 128, Z), BF),
        grid=(4,),
        in_specs=[
            pl.BlockSpec((2 * N, 2 * N), lambda i: (0, 0)),
            pl.BlockSpec((1, 2, 2, N, Z), lambda i: (coil, 0, i, 0, 0)),
            pl.BlockSpec((2, 2, N, Z), lambda i: (0, i, 0, 0)),
        ],
        out_specs=pl.BlockSpec((TILES * 128, Z), lambda i: (0, 0)),
        scratch_shapes=[pltpu.VMEM((TILES * 128, Z), F32)],
        compiler_params=pltpu.CompilerParams(vmem_limit_bytes=32 << 20),
        name=f"coil_forward_{coil}",
    )(table, sensitivity, image)


def grid_kernel(
    coil,
    offsets_ref,
    counts_ref,
    piece_ref,
    forward_ref,
    inverse_ref,
    blocks_hbm,
    turned_hbm,
    samples_hbm,
    out_ref,
    blocks,
    turned,
    samples,
    cells,
    window,
    total,
    sems,
):
    count = counts_ref[0]

    def copies(j):
        return (
            pltpu.make_async_copy(blocks_hbm.at[j], blocks.at[j], sems.at[0, j]),
            pltpu.make_async_copy(turned_hbm.at[j], turned.at[j], sems.at[1, j]),
            pltpu.make_async_copy(samples_hbm.at[coil, j], samples.at[j], sems.at[2, j]),
        )

    def start(j, carry):
        for copy in copies(j):
            copy.start()
        return carry

    lax.fori_loop(0, count, start, 0)

    for pair in range(KYD // 2):
        data = jnp.concatenate(
            [piece_ref[:, 2 * pair + i].reshape(2 * N, Z) for i in range(2)], 1
        )
        result = jnp.dot(forward_ref[...], data, preferred_element_type=F32)
        for i in range(2):
            for part in range(2):
                cells[part, pl.ds(2 * pair + i, N, stride=KYD), :] = result[
                    part * N : (part + 1) * N, i * Z : (i + 1) * Z
                ]
    for part in range(2):
        cells[part, ROWS : ROWS + KYD, :] = jnp.zeros((KYD, Z), F32)
        window[0, :, part * Z : (part + 1) * Z] = cells[part, 0:ROWS, :].astype(BF)
        window[1, :, part * Z : (part + 1) * Z] = cells[part, KYD : ROWS + KYD, :].astype(BF)
    total[...] = jnp.zeros_like(total)

    def group(j, carry):
        for copy in copies(j):
            copy.wait()
        first = offsets_ref[0, j]
        row = pl.multiple_of((first // 2) * (2 * KYD), 2 * KYD)
        view = window[first % 2, pl.ds(row, CELLS), :]
        predicted = jnp.dot(blocks[j], view, preferred_element_type=F32)
        misfit = (predicted - samples[j].astype(F32)).astype(BF)
        update = jnp.dot(turned[j], misfit, preferred_element_type=F32)
        spot = pl.ds(pl.multiple_of(first * KYD, KYD), CELLS)
        for part in range(2):
            total[part, spot, :] = total[part, spot, :] + update[:, part * Z : (part + 1) * Z]
        return carry

    lax.fori_loop(0, count, group, 0)

    for pair in range(KYD // 2):
        sides = []
        for i in range(2):
            ky = 2 * pair + i
            sides.append(
                jnp.concatenate(
                    [
                        total[part, pl.ds(ky, N, stride=KYD), :].astype(BF)
                        for part in range(2)
                    ],
                    0,
                )
            )
        data = jnp.concatenate(sides, 1)
        result = jnp.dot(inverse_ref[...], data, preferred_element_type=F32).astype(BF)
        for i in range(2):
            out_ref[:, 2 * pair + i] = result[:, i * Z : (i + 1) * Z].reshape(TILES, 16, Z)


def grid_tile(coil, offsets, counts, piece, forward, inverse, blocks, turned, samples):
    vmem = pl.BlockSpec(memory_space=pltpu.VMEM)
    smem = pl.BlockSpec(memory_space=pltpu.SMEM)
    hbm = pl.BlockSpec(memory_space=pl.ANY)

    def kernel(*refs):
        grid_kernel(coil, *refs)

    return pl.pallas_call(
        kernel,
        out_shape=jax.ShapeDtypeStruct((TILES, KYD, 16, Z), BF),
        in_specs=[smem, smem, vmem, vmem, vmem, hbm, hbm, hbm],
        out_specs=vmem,
        scratch_shapes=[
            pltpu.VMEM((CH, P_SIZE, CELLS), BF),
            pltpu.VMEM((CH, CELLS, P_SIZE), BF),
            pltpu.VMEM((CH, P_SIZE, 2 * Z), BF),
            pltpu.VMEM((2, ROWS + KYD, Z), F32),
            pltpu.VMEM((2, ROWS, 2 * Z), BF),
            pltpu.VMEM((2, ROWS, Z), F32),
            pltpu.SemaphoreType.DMA((3, CH)),
        ],
        compiler_params=pltpu.CompilerParams(vmem_limit_bytes=48 << 20),
        name=f"grid_tile_{coil}",
    )(offsets, counts, piece, forward, inverse, blocks, turned, samples)


def gradient_kernel(first, last, table_ref, piece_ref, sens_ref, *rest):
    if first:
        (out_ref, spread) = rest
    else:
        (before_ref, out_ref, spread) = rest
    step = pl.program_id(0)

    @pl.when(step == 0)
    def _():
        spread[...] = piece_ref[...].astype(F32)

    data = jnp.concatenate(
        [spread[pl.ds(2 * step + i, 2 * N, stride=KYD), :].astype(BF) for i in range(2)], 1
    )
    result = jnp.dot(table_ref[...], data, preferred_element_type=F32).astype(BF).astype(F32)
    for i in range(2):
        a_re = result[:N, i * Z : (i + 1) * Z]
        a_im = result[N:, i * Z : (i + 1) * Z]
        s_re = sens_ref[0, 0, i].astype(F32)
        s_im = sens_ref[0, 1, i].astype(F32)
        g_re = s_re * a_re + s_im * a_im
        g_im = s_re * a_im - s_im * a_re
        if not first:
            g_re = g_re + before_ref[0, i]
            g_im = g_im + before_ref[1, i]
        if last:
            out_ref[:, 0, i] = g_re.astype(BF).reshape(NCOIL, N // NCOIL, Z)
            out_ref[:, 1, i] = g_im.astype(BF).reshape(NCOIL, N // NCOIL, Z)
        else:
            out_ref[0, i] = g_re
            out_ref[1, i] = g_im


def gradient_step(coil, table, piece, sensitivity, before):
    first = before is None
    last = coil == NCOIL - 1
    whole = pl.BlockSpec((2, 2, N, Z), lambda i: (0, i, 0, 0))
    if last:
        out_shape = jax.ShapeDtypeStruct((NCOIL, 2, KYD, N // NCOIL, Z), BF)
        out_spec = pl.BlockSpec((NCOIL, 2, 2, N // NCOIL, Z), lambda i: (0, 0, i, 0, 0))
    else:
        out_shape = jax.ShapeDtypeStruct((2, KYD, N, Z), F32)
        out_spec = whole

    def kernel(*refs):
        gradient_kernel(first, last, *refs)

    return pl.pallas_call(
        kernel,
        out_shape=out_shape,
        grid=(4,),
        in_specs=[
            pl.BlockSpec((2 * N, 2 * N), lambda i: (0, 0)),
            pl.BlockSpec((TILES * 128, Z), lambda i: (0, 0)),
            pl.BlockSpec((1, 2, 2, N, Z), lambda i: (coil, 0, i, 0, 0)),
        ]
        + ([] if first else [whole]),
        out_specs=out_spec,
        scratch_shapes=[pltpu.VMEM((TILES * 128, Z), F32)],
        compiler_params=pltpu.CompilerParams(vmem_limit_bytes=32 << 20),
        name=f"gradient_{coil}",
    )(*([table, piece, sensitivity] + ([] if first else [before])))


def haar_rows(top, low):
    add = (top + low) * 0.5
    sub = (top - low) * 0.5
    cols = top.shape[0]
    odd = lax.broadcasted_iota(jnp.int32, top.shape, 0) % 2 == 1

    def pairs(v):
        ahead = pltpu.roll(v, cols - 1, 0)
        behind = pltpu.roll(v, 1, 0)
        return jnp.where(odd, behind - v, v + ahead)

    return pairs(add), pairs(sub)


def target_kernel(image_ref, aux_ref, dual_ref, out_ref):
    for part in range(2):
        for m in range(KYD // 2):
            rows = haar_rows(
                aux_ref[part, 2 * m] - dual_ref[part, 2 * m],
                aux_ref[part, 2 * m + 1] - dual_ref[part, 2 * m + 1],
            )
            for i in range(2):
                current = image_ref[part, 2 * m + i]
                out_ref[part, 2 * m + i] = current - step_size * penalty * (current - rows[i])


def target_step(position, image, auxiliary, scaled_dual):
    vmem = pl.BlockSpec((2, KYD, N // NCOIL, Z), lambda i, s: (0, 0, 0, 0))
    return pl.pallas_call(
        lambda s, *refs: target_kernel(*refs),
        out_shape=jax.ShapeDtypeStruct(auxiliary.shape, F32),
        grid_spec=pltpu.PrefetchScalarGridSpec(
            num_scalar_prefetch=1,
            grid=(1,),
            in_specs=[
                pl.BlockSpec((2, KYD, N // NCOIL, Z), lambda i, s: (0, 0, s[0], 0)),
                vmem,
                vmem,
            ],
            out_specs=vmem,
        ),
        name="target",
    )(position, image, auxiliary, scaled_dual)


def update_kernel(base_ref, pieces_ref, dual_ref, image_out, aux_out, dual_out):
    for m in range(KYD // 2):
        coeffs = []
        for part in range(2):
            rows = []
            for i in range(2):
                x = 2 * m + i
                gradient = pieces_ref[0, part, x].astype(F32)
                for k in range(1, NCOIL):
                    gradient = gradient + pieces_ref[k, part, x].astype(F32)
                value = base_ref[part, x] - step_size * gradient
                image_out[part, x] = value
                rows.append(value)
            top, low = haar_rows(*rows)
            coeffs.append((top + dual_ref[part, 2 * m], low + dual_ref[part, 2 * m + 1]))
        for i in range(2):
            x = 2 * m + i
            c_re = coeffs[0][i]
            c_im = coeffs[1][i]
            magnitude = jnp.sqrt(c_re * c_re + c_im * c_im)
            factor = jnp.maximum(1.0 - threshold / jnp.maximum(magnitude, threshold), 0.0)
            for part, c in enumerate((c_re, c_im)):
                kept = c * factor
                aux_out[part, x] = kept
                dual_out[part, x] = c - kept


def update_step(base, pieces, scaled_dual):
    vmem = pl.BlockSpec(memory_space=pltpu.VMEM)
    shape = jax.ShapeDtypeStruct(scaled_dual.shape, F32)
    return pl.pallas_call(
        update_kernel,
        out_shape=(shape, shape, shape),
        in_specs=[vmem, vmem, vmem],
        out_specs=(vmem, vmem, vmem),
        name="update",
    )(base, pieces, scaled_dual)


def body(image, sensitivity, blocks, samples, offsets, counts, auxiliary, scaled_dual):
    along_y, along_x = real_tables()
    y_forward = jnp.asarray(along_y)
    y_inverse = jnp.asarray(np.ascontiguousarray(along_y.T))
    x_forward = jnp.asarray(along_x)
    x_inverse = jnp.asarray(np.ascontiguousarray(along_x.T))

    turned = jnp.swapaxes(blocks[0], 1, 2)
    by_coil = jnp.transpose(samples[0], (2, 0, 1, 3, 4)).reshape(NCOIL, CH, P_SIZE, 2 * Z)

    pieces = []
    for coil in range(NCOIL):
        half = coil_forward(coil, y_forward, sensitivity, image).reshape(TILES, KYD, 16, Z)
        pieces.append(lax.all_to_all(half, "slab", 0, 0, tiled=True))
    position = lax.axis_index("coil").reshape(1)
    base = target_step(position, image, auxiliary, scaled_dual)
    backs = []
    for coil in range(NCOIL):
        back = grid_tile(
            coil, offsets, counts, pieces[coil], x_forward, x_inverse, blocks[0], turned, by_coil
        )
        backs.append(lax.all_to_all(back, "slab", 0, 0, tiled=True))
    total = None
    for coil in range(NCOIL):
        total = gradient_step(coil, y_inverse, backs[coil].reshape(TILES * 128, Z), sensitivity, total)
    shares = lax.all_to_all(total, "coil", 0, 0, tiled=True)
    return update_step(base, shares, scaled_dual)


def solution(mesh):
    return jax.shard_map(
        body,
        mesh=mesh,
        in_specs=(
            P(None, "slab", None, None),
            P("coil", None, "slab", None, None),
            P("slab", None, None, None),
            P("slab", None, None, "coil", None, None),
            P("slab", None),
            P("slab"),
            P(None, "slab", "coil", None),
            P(None, "slab", "coil", None),
        ),
        out_specs=(
            P(None, "slab", "coil", None),
            P(None, "slab", "coil", None),
            P(None, "slab", "coil", None),
        ),
        check_vma=False,
    )
```

profile of v0, /device:TPU:0, one launch (start us, length us, event | category | flops | bytes accessed | tf_op | source)
XLA Modules:
  0.0 236.2 jit_solution(15308494704832676661)
XLA Ops:
  0.6 0.0 copy-start
  0.6 2.2 copy-done
  2.8 1.6 copy-done.6
  4.4 1.0 copy-done.11
  5.5 1.7 coil_forward_0.1
  7.2 0.0 copy-start.23
  7.2 1.0 copy-done.23
  8.2 7.5 %all-to-all-start.6 = ((bf16[32,8,16,128]{3,2,1,0:T(8,128)(2,1)}), bf16[32,8,16,128]{3,2,1,0:T(8,128)(2,1)}, u32[]{:S(2)}, u32[]{:S(2)}) async-start(bf16[32,8,16,128]{3,2,1,0:T(8,128)(2,1)} %bitcast.22), calls=%async_computation.6 | async-start | bytes 2097152 | tf_op jit(solution)/shard_map/all_to_all | solution.py:365
  15.8 0.0 copy-start.1
  15.8 2.2 copy-done.1
  18.0 1.7 coil_forward_1.1
  19.7 0.0 copy-start.22
  19.7 1.0 copy-done.22
  20.7 11.8 %all-to-all-done.6.refs_2_ = bf16[32,8,16,128]{3,2,1,0:T(8,128)(2,1)} async-done(((bf16[32,8,16,128]{3,2,1,0:T(8,128)(2,1)}), bf16[32,8,16,128]{3,2,1,0:T(8,128)(2,1)}, u32[]{:S(2)}, u32[]{:S(2)}) %all-to-all-start.6) | async-done | bytes 1048608 | tf_op jit(solution)/shard_map/all_to_all | solution.py:365
  32.5 4.7 %all-to-all-start.4 = ((bf16[32,8,16,128]{3,2,1,0:T(8,128)(2,1)}), bf16[32,8,16,128]{3,2,1,0:T(8,128)(2,1)}, u32[]{:S(2)}, u32[]{:S(2)}) async-start(bf16[32,8,16,128]{3,2,1,0:T(8,128)(2,1)} %bitcast.21), calls=%async_computation.4 | async-start | bytes 2097152 | tf_op jit(solution)/shard_map/all_to_all | solution.py:365
  37.2 0.0 copy-start.2
  37.2 2.2 copy-done.2
  39.4 1.7 coil_forward_2.1
  41.2 0.0 copy-start.21
  41.2 1.0 copy-done.21
  42.1 11.8 %all-to-all-done.4.refs_2_ = bf16[32,8,16,128]{3,2,1,0:T(8,128)(2,1)} async-done(((bf16[32,8,16,128]{3,2,1,0:T(8,128)(2,1)}), bf16[32,8,16,128]{3,2,1,0:T(8,128)(2,1)}, u32[]{:S(2)}, u32[]{:S(2)}) %all-to-all-start.4) | async-done | bytes 1048608 | tf_op jit(solution)/shard_map/all_to_all | solution.py:365
  54.0 4.7 %all-to-all-start.2 = ((bf16[32,8,16,128]{3,2,1,0:T(8,128)(2,1)}), bf16[32,8,16,128]{3,2,1,0:T(8,128)(2,1)}, u32[]{:S(2)}, u32[]{:S(2)}) async-start(bf16[32,8,16,128]{3,2,1,0:T(8,128)(2,1)} %bitcast.20), calls=%async_computation.2 | async-start | bytes 2097152 | tf_op jit(solution)/shard_map/all_to_all | solution.py:365
  58.6 0.0 copy-start.3
  58.7 2.2 copy-done.3
  60.8 1.8 coil_forward_3.1
  62.6 0.0 copy-start.17
  62.6 1.0 copy-done.17
  63.6 11.8 %all-to-all-done.2.refs_2_ = bf16[32,8,16,128]{3,2,1,0:T(8,128)(2,1)} async-done(((bf16[32,8,16,128]{3,2,1,0:T(8,128)(2,1)}), bf16[32,8,16,128]{3,2,1,0:T(8,128)(2,1)}, u32[]{:S(2)}, u32[]{:S(2)}) %all-to-all-start.2) | async-done | bytes 1048608 | tf_op jit(solution)/shard_map/all_to_all | solution.py:365
  75.4 4.0 %all-to-all-start = ((bf16[32,8,16,128]{3,2,1,0:T(8,128)(2,1)}), bf16[32,8,16,128]{3,2,1,0:T(8,128)(2,1)S(1)}, u32[]{:S(2)}, u32[]{:S(2)}) async-start(bf16[32,8,16,128]{3,2,1,0:T(8,128)(2,1)} %bitcast.19), calls=%async_computation | async-start | bytes 2097152 | tf_op jit(solution)/shard_map/all_to_all | solution.py:365
  79.5 10.8 %reshape.46 = bf16[4,24,128,256]{3,0,2,1:T(4,128)(2,1)} reshape(bf16[4,24,128,2,128]{4,3,0,2,1:T(2,128)(2,1)} %bitcast.31) | data formatting | bytes 12582912 | tf_op jit(solution)/shard_map/reshape | solution.py:360
  90.3 6.6 %copy.22.refs_7_ = bf16[4,24,128,256]{3,2,1,0:T(8,128)(2,1)} copy(bf16[4,24,128,256]{3,0,2,1:T(4,128)(2,1)} %reshape.46) | data formatting | bytes 12582912 | tf_op jit(solution)/shard_map/reshape | solution.py:360
  96.9 4.7 %copy.15 = bf16[1,24,128,512]{2,3,1,0:T(8,128)(2,1)} copy(bf16[1,24,128,512]{3,2,1,0:T(8,128)(2,1)} %param.14) | data formatting | bytes 6291456 | tf_op args[2]
  102.4 4.3 %grid_tile_0.1 = bf16[32,8,16,128]{3,2,1,0:T(8,128)(2,1)S(1)} custom-call(s32[1,24]{1,0:T(1,128)S(1)} %copy-done.24, s32[1]{0:T(128)S(6)} %copy.23.refs_1_, bf16[32,8,16,128]{3,2,1,0:T(8,128)(2,1)} %all-to-all-done.6.refs_2_, bf16[512,512]{1,0:T(8,128)(2,1)S(1)} %copy-done.8, bf16[512,512]{1,0:T(8,128)(2,1)S(1)} %copy-done.9, ...), custom_call_target="tpu_custom_call" | custom-call | tf_op jit(solution)/shard_map/grid_tile_0/pallas_call | solution.py:185
  106.7 1.0 copy-done.19
  107.7 0.0 all-to-all-done.refs_2_
  107.7 15.9 %all-to-all-start.7 = ((bf16[32,8,16,128]{3,2,1,0:T(8,128)(2,1)}), bf16[32,8,16,128]{3,2,1,0:T(8,128)(2,1)S(1)}, u32[]{:S(2)}, u32[]{:S(2)}) async-start(bf16[32,8,16,128]{3,2,1,0:T(8,128)(2,1)} %copy-done.19), calls=%async_computation.7 | async-start | bytes 2097152 | tf_op jit(solution)/shard_map/all_to_all | solution.py:373
  123.6 4.3 %grid_tile_1.1 = bf16[32,8,16,128]{3,2,1,0:T(8,128)(2,1)S(1)} custom-call(s32[1,24]{1,0:T(1,128)S(1)} %copy-done.24, s32[1]{0:T(128)S(6)} %copy.23.refs_1_, bf16[32,8,16,128]{3,2,1,0:T(8,128)(2,1)} %all-to-all-done.4.refs_2_, bf16[512,512]{1,0:T(8,128)(2,1)S(1)} %copy-done.8, bf16[512,512]{1,0:T(8,128)(2,1)S(1)} %copy-done.9, ...), custom_call_target="tpu_custom_call" | custom-call | tf_op jit(solution)/shard_map/grid_tile_1/pallas_call | solution.py:185
  128.0 1.0 copy-done.20
  129.0 11.5 %all-to-all-done.7 = bf16[32,8,16,128]{3,2,1,0:T(8,128)(2,1)S(1)} async-done(((bf16[32,8,16,128]{3,2,1,0:T(8,128)(2,1)}), bf16[32,8,16,128]{3,2,1,0:T(8,128)(2,1)S(1)}, u32[]{:S(2)}, u32[]{:S(2)}) %all-to-all-start.7) | async-done | bytes 1048608 | tf_op jit(solution)/shard_map/all_to_all | solution.py:373
  140.4 4.7 %all-to-all-start.5 = ((bf16[32,8,16,128]{3,2,1,0:T(8,128)(2,1)}), bf16[32,8,16,128]{3,2,1,0:T(8,128)(2,1)}, u32[]{:S(2)}, u32[]{:S(2)}) async-start(bf16[32,8,16,128]{3,2,1,0:T(8,128)(2,1)} %copy-done.20), calls=%async_computation.5 | async-start | bytes 2097152 | tf_op jit(solution)/shard_map/all_to_all | solution.py:373
  145.1 4.5 %grid_tile_2.1 = bf16[32,8,16,128]{3,2,1,0:T(8,128)(2,1)S(1)} custom-call(s32[1,24]{1,0:T(1,128)S(1)} %copy-done.24, s32[1]{0:T(128)S(6)} %copy.23.refs_1_, bf16[32,8,16,128]{3,2,1,0:T(8,128)(2,1)} %all-to-all-done.2.refs_2_, bf16[512,512]{1,0:T(8,128)(2,1)S(1)} %copy-done.8, bf16[512,512]{1,0:T(8,128)(2,1)S(1)} %copy-done.9, ...), custom_call_target="tpu_custom_call" | custom-call | tf_op jit(solution)/shard_map/grid_tile_2/pallas_call | solution.py:185
  149.7 1.0 copy-done.18
  150.6 11.3 %all-to-all-done.5 = bf16[32,8,16,128]{3,2,1,0:T(8,128)(2,1)} async-done(((bf16[32,8,16,128]{3,2,1,0:T(8,128)(2,1)}), bf16[32,8,16,128]{3,2,1,0:T(8,128)(2,1)}, u32[]{:S(2)}, u32[]{:S(2)}) %all-to-all-start.5) | async-done | bytes 1048608 | tf_op jit(solution)/shard_map/all_to_all | solution.py:373
  161.9 4.7 %all-to-all-start.3 = ((bf16[32,8,16,128]{3,2,1,0:T(8,128)(2,1)}), bf16[32,8,16,128]{3,2,1,0:T(8,128)(2,1)}, u32[]{:S(2)}, u32[]{:S(2)}) async-start(bf16[32,8,16,128]{3,2,1,0:T(8,128)(2,1)} %copy-done.18), calls=%async_computation.3 | async-start | bytes 2097152 | tf_op jit(solution)/shard_map/all_to_all | solution.py:373
  166.6 0.0 copy-start.10
  166.6 3.6 %grid_tile_3.1 = bf16[32,8,16,128]{3,2,1,0:T(8,128)(2,1)S(1)} custom-call(s32[1,24]{1,0:T(1,128)S(1)} %copy-done.24, s32[1]{0:T(128)S(6)} %copy.23.refs_1_, bf16[32,8,16,128]{3,2,1,0:T(8,128)(2,1)S(1)} %all-to-all-done.refs_2_, bf16[512,512]{1,0:T(8,128)(2,1)S(1)} %copy-done.8, bf16[512,512]{1,0:T(8,128)(2,1)S(1)} %copy-done.9, ...), custom_call_target="tpu_custom_call" | custom-call | tf_op jit(solution)/shard_map/grid_tile_3/pallas_call | solution.py:185
  170.2 1.0 copy-done.15
  171.2 12.1 %all-to-all-done.3 = bf16[32,8,16,128]{3,2,1,0:T(8,128)(2,1)} async-done(((bf16[32,8,16,128]{3,2,1,0:T(8,128)(2,1)}), bf16[32,8,16,128]{3,2,1,0:T(8,128)(2,1)}, u32[]{:S(2)}, u32[]{:S(2)}) %all-to-all-start.3) | async-done | bytes 1048608 | tf_op jit(solution)/shard_map/all_to_all | solution.py:373
  183.3 4.7 %all-to-all-start.1 = ((bf16[32,8,16,128]{3,2,1,0:T(8,128)(2,1)}), bf16[32,8,16,128]{3,2,1,0:T(8,128)(2,1)}, u32[]{:S(2)}, u32[]{:S(2)}) async-start(bf16[32,8,16,128]{3,2,1,0:T(8,128)(2,1)} %copy-done.15), calls=%async_computation.1 | async-start | bytes 2097152 | tf_op jit(solution)/shard_map/all_to_all | solution.py:373
  188.0 0.0 copy-start.4
  188.0 2.2 copy-done.4
  190.2 1.2 copy-done.14
  191.4 1.9 gradient_0.1.refs_3_
  193.4 3.3 %gradient_1.1.refs_3_ = f32[2,8,256,128]{3,2,1,0:T(8,128)S(1)} custom-call(bf16[512,512]{1,0:T(8,128)(2,1)S(1)} %copy-done.10, bf16[4096,128]{1,0:T(8,128)(2,1)} %bitcast.13.refs_1_, bf16[4,2,8,256,128]{4,3,2,1,0:T(8,128)(2,1)S(1)} %copy-done.4, f32[2,8,256,128]{3,2,1,0:T(8,128)S(1)} %gradient_0.1.refs_3_), custom_call_target="tpu_custom_call" | custom-call | tf_op jit(solution)/shard_map/gradient_1/pallas_call | solution.py:251
  196.7 3.3 %gradient_2.1.refs_3_ = f32[2,8,256,128]{3,2,1,0:T(8,128)S(1)} custom-call(bf16[512,512]{1,0:T(8,128)(2,1)S(1)} %copy-done.10, bf16[4096,128]{1,0:T(8,128)(2,1)} %bitcast.11.refs_1_, bf16[4,2,8,256,128]{4,3,2,1,0:T(8,128)(2,1)S(1)} %copy-done.4, f32[2,8,256,128]{3,2,1,0:T(8,128)S(1)} %gradient_1.1.refs_3_), custom_call_target="tpu_custom_call" | custom-call | tf_op jit(solution)/shard_map/gradient_2/pallas_call | solution.py:251
  200.0 4.8 %all-to-all-done.1 = bf16[32,8,16,128]{3,2,1,0:T(8,128)(2,1)} async-done(((bf16[32,8,16,128]{3,2,1,0:T(8,128)(2,1)}), bf16[32,8,16,128]{3,2,1,0:T(8,128)(2,1)}, u32[]{:S(2)}, u32[]{:S(2)}) %all-to-all-start.1) | async-done | bytes 1048608 | tf_op jit(solution)/shard_map/all_to_all | solution.py:373
  204.8 2.2 copy-done.5
  207.0 3.2 %gradient_3.1 = bf16[4,2,8,64,128]{4,3,2,1,0:T(8,128)(2,1)S(1)} custom-call(bf16[512,512]{1,0:T(8,128)(2,1)S(1)} %copy-done.10, bf16[4096,128]{1,0:T(8,128)(2,1)} %bitcast.7.refs_1_, bf16[4,2,8,256,128]{4,3,2,1,0:T(8,128)(2,1)S(1)} %copy-done.5, f32[2,8,256,128]{3,2,1,0:T(8,128)S(1)} %gradient_2.1.refs_3_), custom_call_target="tpu_custom_call" | custom-call | tf_op jit(solution)/shard_map/gradient_3/pallas_call | solution.py:251
  210.2 1.0 copy-done.16
  211.2 5.3 %all-to-all-start.8 = ((bf16[4,2,8,64,128]{4,3,2,1,0:T(8,128)(2,1)}), bf16[4,2,8,64,128]{4,3,2,1,0:T(8,128)(2,1)S(1)}, u32[]{:S(2)}, u32[]{:S(2)}) async-start(bf16[4,2,8,64,128]{4,3,2,1,0:T(8,128)(2,1)} %copy-done.16), calls=%async_computation.8 | async-start | bytes 2097152 | tf_op jit(solution)/shard_map/all_to_all | solution.py:377
  216.5 2.4 %target.1.base_ref = f32[2,8,64,128]{3,2,1,0:T(8,128)} custom-call(s32[1]{0:T(128)} %bitcast.s, f32[2,8,256,128]{3,2,1,0:T(8,128)} %image_ref.7, f32[2,8,64,128]{3,2,1,0:T(8,128)} %refs_1_.5, f32[2,8,64,128]{3,2,1,0:T(8,128)} %dual_ref.1), custom_call_target="tpu_custom_call" | custom-call | tf_op jit(solution)/shard_map/target/pallas_call | solution.py:296
  218.9 13.2 %all-to-all-done.8.pieces_ref = bf16[4,2,8,64,128]{4,3,2,1,0:T(8,128)(2,1)S(1)} async-done(((bf16[4,2,8,64,128]{4,3,2,1,0:T(8,128)(2,1)}), bf16[4,2,8,64,128]{4,3,2,1,0:T(8,128)(2,1)S(1)}, u32[]{:S(2)}, u32[]{:S(2)}) %all-to-all-start.8) | async-done | bytes 1048608 | tf_op jit(solution)/shard_map/all_to_all | solution.py:377
  232.1 1.0 copy-done.25
  233.1 3.1 %update.1 = (f32[2,8,64,128]{3,2,1,0:T(8,128)}, f32[2,8,64,128]{3,2,1,0:T(8,128)}, f32[2,8,64,128]{3,2,1,0:T(8,128)}) custom-call(f32[2,8,64,128]{3,2,1,0:T(8,128)} %target.1.base_ref, bf16[4,2,8,64,128]{4,3,2,1,0:T(8,128)(2,1)} %copy-done.25, f32[2,8,64,128]{3,2,1,0:T(8,128)} %dual_ref.1), custom_call_target="tpu_custom_call" | custom-call | tf_op jit(solution)/shard_map/update/pallas_call | solution.py:343
  (23 shorter events, 0.0 us)
Async XLA Ops:
  0.6 2.2 copy-start
  2.8 1.6 copy-start.6
  4.4 1.0 copy-start.11
  5.5 10.3 %copy-start.7 = (f32[2,8,256,128]{3,2,1,0:T(8,128)S(1)}, f32[2,8,256,128]{3,2,1,0:T(8,128)}, u32[]{:S(2)}) copy-start(f32[2,8,256,128]{3,2,1,0:T(8,128)} %image_ref.7) | copy-start | bytes 6291460
  5.5 10.3 %copy-start.12 = (bf16[512,512]{1,0:T(8,128)(2,1)S(1)}, bf16[512,512]{1,0:T(8,128)(2,1)}, u32[]{:S(2)}) copy-start(bf16[512,512]{1,0:T(8,128)(2,1)} %constant.14.clone.table_ref) | copy-start | bytes 1572868
  7.2 1.0 copy-start.23
  8.2 24.3 %all-to-all-start.6 = ((bf16[32,8,16,128]{3,2,1,0:T(8,128)(2,1)}), bf16[32,8,16,128]{3,2,1,0:T(8,128)(2,1)}, u32[]{:S(2)}, u32[]{:S(2)}) async-start(bf16[32,8,16,128]{3,2,1,0:T(8,128)(2,1)} %bitcast.22), calls=%async_computation.6 | async-start | bytes 2097152 | tf_op jit(solution)/shard_map/all_to_all | solution.py:365
  15.8 2.2 copy-start.1
  19.7 1.0 copy-start.22
  32.5 21.4 %all-to-all-start.4 = ((bf16[32,8,16,128]{3,2,1,0:T(8,128)(2,1)}), bf16[32,8,16,128]{3,2,1,0:T(8,128)(2,1)}, u32[]{:S(2)}, u32[]{:S(2)}) async-start(bf16[32,8,16,128]{3,2,1,0:T(8,128)(2,1)} %bitcast.21), calls=%async_computation.4 | async-start | bytes 2097152 | tf_op jit(solution)/shard_map/all_to_all | solution.py:365
  37.2 2.2 copy-start.2
  41.2 1.0 copy-start.21
  54.0 21.4 %all-to-all-start.2 = ((bf16[32,8,16,128]{3,2,1,0:T(8,128)(2,1)}), bf16[32,8,16,128]{3,2,1,0:T(8,128)(2,1)}, u32[]{:S(2)}, u32[]{:S(2)}) async-start(bf16[32,8,16,128]{3,2,1,0:T(8,128)(2,1)} %bitcast.20), calls=%async_computation.2 | async-start | bytes 2097152 | tf_op jit(solution)/shard_map/all_to_all | solution.py:365
  58.6 2.2 copy-start.3
  62.6 1.0 copy-start.17
  75.4 32.3 %all-to-all-start = ((bf16[32,8,16,128]{3,2,1,0:T(8,128)(2,1)}), bf16[32,8,16,128]{3,2,1,0:T(8,128)(2,1)S(1)}, u32[]{:S(2)}, u32[]{:S(2)}) async-start(bf16[32,8,16,128]{3,2,1,0:T(8,128)(2,1)} %bitcast.19), calls=%async_computation | async-start | bytes 2097152 | tf_op jit(solution)/shard_map/all_to_all | solution.py:365
  96.9 5.4 %copy-start.8 = (bf16[512,512]{1,0:T(8,128)(2,1)S(1)}, bf16[512,512]{1,0:T(8,128)(2,1)}, u32[]{:S(2)}) copy-start(bf16[512,512]{1,0:T(8,128)(2,1)} %constant.16.clone.refs_3_) | copy-start | bytes 1572868
  96.9 5.4 %copy-start.9 = (bf16[512,512]{1,0:T(8,128)(2,1)S(1)}, bf16[512,512]{1,0:T(8,128)(2,1)}, u32[]{:S(2)}) copy-start(bf16[512,512]{1,0:T(8,128)(2,1)} %constant.17.clone.refs_4_) | copy-start | bytes 1572868
  96.9 5.4 %copy-start.24 = (s32[1,24]{1,0:T(1,128)S(1)}, s32[1,24]{1,0:T(1,128)}, u32[]{:S(2)}) copy-start(s32[1,24]{1,0:T(1,128)} %refs_0_.13) | copy-start | bytes 292
  106.7 1.0 copy-start.19
  107.7 32.7 %all-to-all-start.7 = ((bf16[32,8,16,128]{3,2,1,0:T(8,128)(2,1)}), bf16[32,8,16,128]{3,2,1,0:T(8,128)(2,1)S(1)}, u32[]{:S(2)}, u32[]{:S(2)}) async-start(bf16[32,8,16,128]{3,2,1,0:T(8,128)(2,1)} %copy-done.19), calls=%async_computation.7 | async-start | bytes 2097152 | tf_op jit(solution)/shard_map/all_to_all | solution.py:373
  128.0 1.0 copy-start.20
  140.4 9.2 %copy-start.13 = (bf16[32,8,16,128]{3,2,1,0:T(8,128)(2,1)}, bf16[32,8,16,128]{3,2,1,0:T(8,128)(2,1)S(1)}, u32[]{:S(2)}) copy-start(bf16[32,8,16,128]{3,2,1,0:T(8,128)(2,1)S(1)} %all-to-all-done.7) | copy-start | bytes 3145732
  140.4 21.4 %all-to-all-start.5 = ((bf16[32,8,16,128]{3,2,1,0:T(8,128)(2,1)}), bf16[32,8,16,128]{3,2,1,0:T(8,128)(2,1)}, u32[]{:S(2)}, u32[]{:S(2)}) async-start(bf16[32,8,16,128]{3,2,1,0:T(8,128)(2,1)} %copy-done.20), calls=%async_computation.5 | async-start | bytes 2097152 | tf_op jit(solution)/shard_map/all_to_all | solution.py:373
  149.6 1.0 copy-start.18
  161.9 21.5 %all-to-all-start.3 = ((bf16[32,8,16,128]{3,2,1,0:T(8,128)(2,1)}), bf16[32,8,16,128]{3,2,1,0:T(8,128)(2,1)}, u32[]{:S(2)}, u32[]{:S(2)}) async-start(bf16[32,8,16,128]{3,2,1,0:T(8,128)(2,1)} %copy-done.18), calls=%async_computation.3 | async-start | bytes 2097152 | tf_op jit(solution)/shard_map/all_to_all | solution.py:373
  166.6 21.5 %copy-start.10 = (bf16[512,512]{1,0:T(8,128)(2,1)S(1)}, bf16[512,512]{1,0:T(8,128)(2,1)}, u32[]{:S(2)}) copy-start(bf16[512,512]{1,0:T(8,128)(2,1)} %constant.15.clone.refs_0_) | copy-start | bytes 1572868
  170.2 1.0 copy-start.15
  183.3 21.4 %all-to-all-start.1 = ((bf16[32,8,16,128]{3,2,1,0:T(8,128)(2,1)}), bf16[32,8,16,128]{3,2,1,0:T(8,128)(2,1)}, u32[]{:S(2)}, u32[]{:S(2)}) async-start(bf16[32,8,16,128]{3,2,1,0:T(8,128)(2,1)} %copy-done.15), calls=%async_computation.1 | async-start | bytes 2097152 | tf_op jit(solution)/shard_map/all_to_all | solution.py:373
  188.0 2.2 copy-start.4
  190.2 1.2 copy-start.14
  204.8 2.2 copy-start.5
  210.2 1.0 copy-start.16
  211.2 20.9 %all-to-all-start.8 = ((bf16[4,2,8,64,128]{4,3,2,1,0:T(8,128)(2,1)}), bf16[4,2,8,64,128]{4,3,2,1,0:T(8,128)(2,1)S(1)}, u32[]{:S(2)}, u32[]{:S(2)}) async-start(bf16[4,2,8,64,128]{4,3,2,1,0:T(8,128)(2,1)} %copy-done.16), calls=%async_computation.8 | async-start | bytes 2097152 | tf_op jit(solution)/shard_map/all_to_all | solution.py:377
  232.1 1.0 copy-start.25
where the time goes:
time: 238 us; the launch traced here: 236 us
  waiting for transfers between devices  88.4 us (37%)
  starting transfers between devices  56.1 us (24%)
  local copies, waits for them, and re-layouts  49 us (21%)
  Pallas kernels  41.1 us (17%)
    all_to_all x4, waiting for transfers between devices, body(): backs.append(lax.all_to_all(back, 'slab', 0, 0, tiled=True))  39.6 us
    all_to_all x4, waiting for transfers between devices, body(): pieces.append(lax.all_to_all(half, 'slab', 0, 0, tiled=True))  35.5 us
    unnamed x53, local copies, waits for them, and re-layouts  31.6 us
    all_to_all x4, starting transfers between devices, body(): backs.append(lax.all_to_all(back, 'slab', 0, 0, tiled=True))  29.9 us
    all_to_all x4, starting transfers between devices, body(): pieces.append(lax.all_to_all(half, 'slab', 0, 0, tiled=True))  20.9 us
    reshape x2, local copies, waits for them, and re-layouts, body(): jnp.transpose(samples[0], (2, 0, 1, 3, 4)).reshape(NCOIL, CH, P_SIZE, 2 * Z)  17.5 us
    pallas_call x4, Pallas kernels, grid_tile(): pl.pallas_call(kernel, out_shape=jax.ShapeDtypeStruct((TILES, KYD, 16, Z)...  16.9 us
    all_to_all x1, waiting for transfers between devices, body(): shares = lax.all_to_all(total, 'coil', 0, 0, tiled=True)  13.2 us
  transfers between devices with their start and end apart: 9, of which 8 were waited for; matrix products, arithmetic and copies ran while one was open for 9% of the time, Pallas kernels for 14%

commit v1 on v0

v1 whole, which is shorter than its diff:
```python
import math

import jax
import jax.numpy as jnp
import numpy as np
import ml_dtypes
from jax import lax
from jax.experimental import pallas as pl
from jax.experimental.pallas import tpu as pltpu
from jax.sharding import PartitionSpec as P

N = 256
Z = 128
WIN = 64
P_SIZE = 128
CH = 24
KYD = 8
TILES = 32
CELLS = WIN * KYD
ROWS = N * KYD
NCOIL = 4
PER = 2

step_size = 0.5
penalty = 1.0
threshold = 0.3

BF = jnp.bfloat16
F32 = jnp.float32


def dft_parts():
    index = np.arange(N)
    angle = (index[:, None] * index[None, :] % N).astype(np.float32) * np.float32(2.0 * math.pi / N)
    factor = np.float32(1.0 / math.sqrt(N))
    re = (np.cos(angle) * factor).astype(ml_dtypes.bfloat16)
    im = (-np.sin(angle) * factor).astype(ml_dtypes.bfloat16)
    return re, im


def real_tables():
    re, im = dft_parts()
    along_y = np.stack(
        [np.concatenate([re, -im], 1), np.concatenate([im, re], 1)], 1
    ).reshape(2 * N, 2 * N)
    re_c = re.reshape(N, TILES, KYD)
    im_c = im.reshape(N, TILES, KYD)
    along_x = np.stack(
        [np.stack([re_c, -im_c], 2), np.stack([im_c, re_c], 2)], 0
    ).reshape(2 * N, 2 * N)
    return along_y, along_x


def hbm(shape, dtype):
    return pltpu.HBM(shape, dtype)


def in_hbm(x):
    return pltpu.with_memory_space_constraint(x, pltpu.HBM)


def coil_kernel(table_ref, sens_ref, image_ref, out_ref, spread):
    step = pl.program_id(1)
    parts = []
    for i in range(2):
        s_re = sens_ref[0, 0, i].astype(F32)
        s_im = sens_ref[0, 1, i].astype(F32)
        m_re = image_ref[0, i]
        m_im = image_ref[1, i]
        c_re = (s_re * m_re - s_im * m_im).astype(BF)
        c_im = (s_re * m_im + s_im * m_re).astype(BF)
        parts.append(jnp.concatenate([c_re, c_im], 0))
    data = jnp.concatenate(parts, 1)
    result = jnp.dot(table_ref[...], data, preferred_element_type=F32)
    for i in range(2):
        spread[pl.ds(2 * step + i, 2 * N, stride=KYD), :] = result[:, i * Z : (i + 1) * Z]

    @pl.when(step == 3)
    def _():
        out_ref[:, 0] = spread[...].astype(BF).reshape(TILES, 128, Z)


def coil_forward(chunk, table, sensitivity, image):
    first = chunk * PER
    return pl.pallas_call(
        coil_kernel,
        out_shape=hbm((TILES, PER, 128, Z), BF),
        grid=(PER, 4),
        in_specs=[
            pl.BlockSpec((2 * N, 2 * N), lambda c, i: (0, 0)),
            pl.BlockSpec((1, 2, 2, N, Z), lambda c, i: (first + c, 0, i, 0, 0)),
            pl.BlockSpec((2, 2, N, Z), lambda c, i: (0, i, 0, 0)),
        ],
        out_specs=pl.BlockSpec((TILES, 1, 128, Z), lambda c, i: (0, c, 0, 0)),
        scratch_shapes=[pltpu.VMEM((TILES * 128, Z), F32)],
        compiler_params=pltpu.CompilerParams(vmem_limit_bytes=32 << 20),
        name=f"coil_forward_{chunk}",
    )(table, sensitivity, image)


def samples_kernel(counts_ref, samples_ref, out_ref, spread):
    @pl.when(pl.program_id(0) < counts_ref[0])
    def _():
        spread[...] = samples_ref[0].astype(F32).reshape(P_SIZE * 8, Z)
        for coil in range(NCOIL):
            for part in range(2):
                out_ref[coil, 0, :, part * Z : (part + 1) * Z] = spread[
                    pl.ds(2 * coil + part, P_SIZE, stride=8), :
                ].astype(BF)


def samples_by_coil(counts, samples):
    last = lambda i, n: jnp.minimum(i, n[0] - 1)
    return pl.pallas_call(
        samples_kernel,
        out_shape=hbm((NCOIL, CH, P_SIZE, 2 * Z), BF),
        grid_spec=pltpu.PrefetchScalarGridSpec(
            num_scalar_prefetch=1,
            grid=(CH,),
            in_specs=[pl.BlockSpec((1, P_SIZE, 8, Z), lambda i, n: (last(i, n), 0, 0, 0))],
            out_specs=pl.BlockSpec((NCOIL, 1, P_SIZE, 2 * Z), lambda i, n: (0, last(i, n), 0, 0)),
            scratch_shapes=[pltpu.VMEM((P_SIZE * 8, Z), F32)],
        ),
        name="samples_by_coil",
    )(counts, samples)


def grid_kernel(
    chunk,
    offsets_ref,
    counts_ref,
    piece_ref,
    forward_ref,
    inverse_ref,
    blocks_hbm,
    turned_hbm,
    samples_hbm,
    out_ref,
    blocks,
    turned,
    samples,
    cells,
    window,
    total,
    sems,
):
    count = counts_ref[0]

    def copies(j):
        return [
            pltpu.make_async_copy(blocks_hbm.at[j], blocks.at[j], sems.at[0, j]),
            pltpu.make_async_copy(turned_hbm.at[j], turned.at[j], sems.at[1, j]),
        ] + [
            pltpu.make_async_copy(
                samples_hbm.at[chunk * PER + c, j],
                samples.at[j, :, pl.ds(2 * Z * c, 2 * Z)],
                sems.at[2 + c, j],
            )
            for c in range(PER)
        ]

    def start(j, carry):
        for copy in copies(j):
            copy.start()
        return carry

    lax.fori_loop(0, count, start, 0)

    for ky in range(KYD):
        data = jnp.concatenate(
            [piece_ref[:, c, ky].reshape(2 * N, Z) for c in range(PER)], 1
        )
        result = jnp.dot(forward_ref[...], data, preferred_element_type=F32)
        for c in range(PER):
            for part in range(2):
                cells[2 * c + part, pl.ds(ky, N, stride=KYD), :] = result[
                    part * N : (part + 1) * N, c * Z : (c + 1) * Z
                ]
    for s in range(2 * PER):
        lanes = slice(s * Z, (s + 1) * Z)
        cells[s, ROWS : ROWS + KYD, :] = jnp.zeros((KYD, Z), F32)
        window[0, :, lanes] = cells[s, 0:ROWS, :].astype(BF)
        window[1, :, lanes] = cells[s, KYD : ROWS + KYD, :].astype(BF)
    total[...] = jnp.zeros_like(total)

    def arrive(j):
        for copy in copies(j):
            copy.wait()

    def predict(j):
        first = offsets_ref[0, j]
        row = pl.multiple_of((first // 2) * (2 * KYD), 2 * KYD)
        view = window[first % 2, pl.ds(row, CELLS), :]
        predicted = jnp.dot(blocks[j], view, preferred_element_type=F32)
        return (predicted - samples[j].astype(F32)).astype(BF)

    def add_back(j, misfit):
        update = jnp.dot(turned[j], misfit, preferred_element_type=F32)
        spot = pl.ds(pl.multiple_of(offsets_ref[0, j] * KYD, KYD), CELLS)
        for s in range(2 * PER):
            total[s, spot, :] = total[s, spot, :] + update[:, s * Z : (s + 1) * Z]

    arrive(0)
    samples[0] = predict(0)

    def group(j, carry):
        arrive(j)
        before = samples[j - 1]
        misfit = predict(j)
        add_back(j - 1, before)
        samples[j] = misfit
        return carry

    lax.fori_loop(1, count, group, 0)
    add_back(count - 1, samples[count - 1])

    for ky in range(KYD):
        data = jnp.concatenate(
            [
                jnp.concatenate(
                    [
                        total[2 * c + part, pl.ds(ky, N, stride=KYD), :].astype(BF)
                        for part in range(2)
                    ],
                    0,
                )
                for c in range(PER)
            ],
            1,
        )
        result = jnp.dot(inverse_ref[...], data, preferred_element_type=F32).astype(BF)
        for c in range(PER):
            out_ref[:, c, ky] = result[:, c * Z : (c + 1) * Z].reshape(TILES, 16, Z)


def grid_tile(chunk, offsets, counts, piece, forward, inverse, blocks, turned, samples):
    vmem = pl.BlockSpec(memory_space=pltpu.VMEM)
    smem = pl.BlockSpec(memory_space=pltpu.SMEM)
    far = pl.BlockSpec(memory_space=pltpu.HBM)

    def kernel(*refs):
        grid_kernel(chunk, *refs)

    return pl.pallas_call(
        kernel,
        out_shape=jax.ShapeDtypeStruct((TILES, PER, KYD, 16, Z), BF),
        in_specs=[smem, smem, vmem, vmem, vmem, far, far, far],
        out_specs=vmem,
        scratch_shapes=[
            pltpu.VMEM((CH, P_SIZE, CELLS), BF),
            pltpu.VMEM((CH, CELLS, P_SIZE), BF),
            pltpu.VMEM((CH, P_SIZE, 2 * Z * PER), BF),
            pltpu.VMEM((2 * PER, ROWS + KYD, Z), F32),
            pltpu.VMEM((2, ROWS, 2 * Z * PER), BF),
            pltpu.VMEM((2 * PER, ROWS, Z), F32),
            pltpu.SemaphoreType.DMA((2 + PER, CH)),
        ],
        compiler_params=pltpu.CompilerParams(vmem_limit_bytes=48 << 20),
        name=f"grid_tile_{chunk}",
    )(offsets, counts, piece, forward, inverse, blocks, turned, samples)


def gradient_kernel(first, last, table_ref, piece_ref, sens_ref, *rest):
    if first:
        (out_ref, spread) = rest
    else:
        (before_ref, out_ref, spread) = rest
    step = pl.program_id(0)

    @pl.when(step == 0)
    def _():
        for c in range(PER):
            spread[c] = piece_ref[:, c].astype(F32).reshape(TILES * 128, Z)

    data = jnp.concatenate(
        [
            spread[c, pl.ds(2 * step + i, 2 * N, stride=KYD), :].astype(BF)
            for c in range(PER)
            for i in range(2)
        ],
        1,
    )
    result = jnp.dot(table_ref[...], data, preferred_element_type=F32).astype(BF).astype(F32)
    for i in range(2):
        g_re = None if first else before_ref[0, i]
        g_im = None if first else before_ref[1, i]
        for c in range(PER):
            lanes = slice((2 * c + i) * Z, (2 * c + i + 1) * Z)
            a_re = result[:N, lanes]
            a_im = result[N:, lanes]
            s_re = sens_ref[c, 0, i].astype(F32)
            s_im = sens_ref[c, 1, i].astype(F32)
            t_re = s_re * a_re + s_im * a_im
            t_im = s_re * a_im - s_im * a_re
            g_re = t_re if g_re is None else g_re + t_re
            g_im = t_im if g_im is None else g_im + t_im
        if last:
            out_ref[:, 0, i] = g_re.astype(BF).reshape(NCOIL, N // NCOIL, Z)
            out_ref[:, 1, i] = g_im.astype(BF).reshape(NCOIL, N // NCOIL, Z)
        else:
            out_ref[0, i] = g_re
            out_ref[1, i] = g_im


def gradient_step(chunk, table, piece, sensitivity, before):
    first = before is None
    last = chunk == NCOIL // PER - 1
    whole = pl.BlockSpec((2, 2, N, Z), lambda i: (0, i, 0, 0))
    if last:
        out_shape = hbm((NCOIL, 2, KYD, N // NCOIL, Z), BF)
        out_spec = pl.BlockSpec((NCOIL, 2, 2, N // NCOIL, Z), lambda i: (0, 0, i, 0, 0))
    else:
        out_shape = hbm((2, KYD, N, Z), F32)
        out_spec = whole

    def kernel(*refs):
        gradient_kernel(first, last, *refs)

    return pl.pallas_call(
        kernel,
        out_shape=out_shape,
        grid=(4,),
        in_specs=[
            pl.BlockSpec((2 * N, 2 * N), lambda i: (0, 0)),
            pl.BlockSpec((TILES, PER, 128, Z), lambda i: (0, 0, 0, 0)),
            pl.BlockSpec((PER, 2, 2, N, Z), lambda i: (chunk, 0, i, 0, 0)),
        ]
        + ([] if first else [whole]),
        out_specs=out_spec,
        scratch_shapes=[pltpu.VMEM((PER, TILES * 128, Z), F32)],
        compiler_params=pltpu.CompilerParams(vmem_limit_bytes=32 << 20),
        name=f"gradient_{chunk}",
    )(*([table, piece, sensitivity] + ([] if first else [before])))


def haar_rows(top, low):
    add = (top + low) * 0.5
    sub = (top - low) * 0.5
    cols = top.shape[0]
    odd = lax.broadcasted_iota(jnp.int32, top.shape, 0) % 2 == 1

    def pairs(v):
        ahead = pltpu.roll(v, cols - 1, 0)
        behind = pltpu.roll(v, 1, 0)
        return jnp.where(odd, behind - v, v + ahead)

    return pairs(add), pairs(sub)


def target_kernel(image_ref, aux_ref, dual_ref, out_ref):
    for part in range(2):
        rows = haar_rows(
            aux_ref[part, 0] - dual_ref[part, 0],
            aux_ref[part, 1] - dual_ref[part, 1],
        )
        for i in range(2):
            current = image_ref[part, i]
            out_ref[part, i] = current - step_size * penalty * (current - rows[i])


def target_step(position, image, auxiliary, scaled_dual):
    pair = pl.BlockSpec((2, 2, N // NCOIL, Z), lambda i, s: (0, i, 0, 0))
    return pl.pallas_call(
        lambda s, *refs: target_kernel(*refs),
        out_shape=hbm(auxiliary.shape, F32),
        grid_spec=pltpu.PrefetchScalarGridSpec(
            num_scalar_prefetch=1,
            grid=(KYD // 2,),
            in_specs=[
                pl.BlockSpec((2, 2, N // NCOIL, Z), lambda i, s: (0, i, s[0], 0)),
                pair,
                pair,
            ],
            out_specs=pair,
        ),
        name="target",
    )(position, image, auxiliary, scaled_dual)


def update_kernel(base_ref, pieces_ref, dual_ref, image_out, aux_out, dual_out):
    coeffs = []
    for part in range(2):
        rows = []
        for x in range(2):
            gradient = pieces_ref[0, part, x].astype(F32)
            for k in range(1, NCOIL):
                gradient = gradient + pieces_ref[k, part, x].astype(F32)
            value = base_ref[part, x] - step_size * gradient
            image_out[part, x] = value
            rows.append(value)
        top, low = haar_rows(*rows)
        coeffs.append((top + dual_ref[part, 0], low + dual_ref[part, 1]))
    for x in range(2):
        c_re = coeffs[0][x]
        c_im = coeffs[1][x]
        magnitude = jnp.sqrt(c_re * c_re + c_im * c_im)
        factor = jnp.maximum(1.0 - threshold / jnp.maximum(magnitude, threshold), 0.0)
        for part, c in enumerate((c_re, c_im)):
            kept = c * factor
            aux_out[part, x] = kept
            dual_out[part, x] = c - kept


def update_step(base, pieces, scaled_dual):
    pair = pl.BlockSpec((2, 2, N // NCOIL, Z), lambda i: (0, i, 0, 0))
    shape = hbm(scaled_dual.shape, F32)
    return pl.pallas_call(
        update_kernel,
        out_shape=(shape, shape, shape),
        grid=(KYD // 2,),
        in_specs=[
            pair,
            pl.BlockSpec((NCOIL, 2, 2, N // NCOIL, Z), lambda i: (0, 0, i, 0, 0)),
            pair,
        ],
        out_specs=(pair, pair, pair),
        name="update",
    )(base, pieces, scaled_dual)


def body(image, sensitivity, blocks, samples, offsets, counts, auxiliary, scaled_dual):
    along_y, along_x = real_tables()
    y_forward, x_forward = lax.optimization_barrier((jnp.asarray(along_y), jnp.asarray(along_x)))
    y_inverse = y_forward.T
    x_inverse = x_forward.T

    image, sensitivity, auxiliary, scaled_dual = (
        in_hbm(v) for v in (image, sensitivity, auxiliary, scaled_dual)
    )
    turned = jnp.swapaxes(blocks[0], 1, 2)
    by_coil = samples_by_coil(counts, in_hbm(samples.reshape(CH, P_SIZE, 2 * NCOIL, Z)))

    chunks = range(NCOIL // PER)
    pieces = []
    for chunk in chunks:
        half = coil_forward(chunk, in_hbm(y_forward), sensitivity, image)
        piece = lax.all_to_all(half, "slab", 0, 0, tiled=True)
        pieces.append(piece.reshape(TILES, PER, KYD, 16, Z))
    position = lax.axis_index("coil").reshape(1)
    base = target_step(position, image, auxiliary, scaled_dual)
    backs = []
    for chunk in chunks:
        back = grid_tile(
            chunk, offsets, counts, pieces[chunk], x_forward, x_inverse, blocks[0], turned, by_coil
        )
        backs.append(lax.all_to_all(back, "slab", 0, 0, tiled=True))
    total = None
    for chunk in chunks:
        piece = in_hbm(backs[chunk].reshape(TILES, PER, 128, Z))
        total = gradient_step(chunk, in_hbm(y_inverse), piece, sensitivity, total)
    shares = in_hbm(lax.all_to_all(total, "coil", 0, 0, tiled=True))
    return update_step(base, shares, scaled_dual)


def solution(mesh):
    return jax.shard_map(
        body,
        mesh=mesh,
        in_specs=(
            P(None, "slab", None, None),
            P("coil", None, "slab", None, None),
            P("slab", None, None, None),
            P("slab", None, None, "coil", None, None),
            P("slab", None),
            P("slab"),
            P(None, "slab", "coil", None),
            P(None, "slab", "coil", None),
        ),
        out_specs=(
            P(None, "slab", "coil", None),
            P(None, "slab", "coil", None),
            P(None, "slab", "coil", None),
        ),
        check_vma=False,
    )
```

time: 238 us -> 194 us (0.82)
  local copies, waits for them, and re-layouts: 49 us -> 16.7 us
  starting transfers between devices: 56.1 us -> 36 us
  Pallas kernels: 41.1 us -> 50 us
    reshape x2 -> x0, local copies, waits for them, and re-layouts: 17.5 us -> none  [body(): jnp.transpose(samples[0], (2, 0, 1, 3, 4)).reshape(NCOIL, CH, P_SIZE, 2 * Z)]
    unnamed x53 -> x19, local copies, waits for them, and re-layouts: 31.6 us -> 14.4 us
    all_to_all x4 -> x2, starting transfers between devices: 29.9 us -> 19.3 us  [body(): backs.append(lax.all_to_all(back, 'slab', 0, 0, tiled=True))]
    all_to_all x5 -> x3, starting transfers between devices: 26.2 us -> 16.7 us  [the longest x2 11.4 us: body(): piece = lax.all_to_all(half, 'slab', 0, 0, tiled=True)]
    pallas_call x10 -> x7, Pallas kernels: 29.3 us -> 37.8 us  [the longest x2 16.7 us: coil_forward(): pl.pallas_call(coil_kernel, out_shape=hbm((TILES, PER, 128, Z), BF), grid...]
    all_to_all x4 -> x2, waiting for transfers between devices: 39.6 us -> 44.8 us  [body(): backs.append(lax.all_to_all(back, 'slab', 0, 0, tiled=True))]
    all_to_all x5 -> x3, waiting for transfers between devices: 48.7 us -> 43.9 us  [the longest x2 32.5 us: body(): piece = lax.all_to_all(half, 'slab', 0, 0, tiled=True)]
    pallas_call x4 -> x2, Pallas kernels: 11.7 us -> 12.2 us  [gradient_step(): pl.pallas_call(kernel, out_shape=out_shape, grid=(4,), in_specs=[pl.Block...]
  transfers between devices with their start and end apart: 9 -> 5, of which waited for: 8 -> 5; matrix products, arithmetic and copies ran while one was open for 9% -> 3% of each run, Pallas kernels for 14% -> 16%
where the time goes in v1:
time: 194 us; the launch traced here: 193 us
  waiting for transfers between devices  88.7 us (46%)
  Pallas kernels  50 us (26%)
  starting transfers between devices  36 us (19%)
  local copies, waits for them, and re-layouts  16.7 us (9%)
    all_to_all x2, waiting for transfers between devices, body(): backs.append(lax.all_to_all(back, 'slab', 0, 0, tiled=True))  44.8 us
    all_to_all x2, waiting for transfers between devices, body(): piece = lax.all_to_all(half, 'slab', 0, 0, tiled=True)  32.5 us
    all_to_all x2, starting transfers between devices, body(): backs.append(lax.all_to_all(back, 'slab', 0, 0, tiled=True))  19.3 us
    pallas_call x2, Pallas kernels, coil_forward(): pl.pallas_call(coil_kernel, out_shape=hbm((TILES, PER, 128, Z), BF), grid...  16.7 us
    unnamed x19, local copies, waits for them, and re-layouts  14.4 us
    pallas_call x2, Pallas kernels, gradient_step(): pl.pallas_call(kernel, out_shape=out_shape, grid=(4,), in_specs=[pl.Block...  12.2 us
    all_to_all x2, starting transfers between devices, body(): piece = lax.all_to_all(half, 'slab', 0, 0, tiled=True)  11.4 us
    all_to_all x1, waiting for transfers between devices, body(): shares = in_hbm(lax.all_to_all(total, 'coil', 0, 0, tiled=True))  11.4 us
  transfers between devices with their start and end apart: 5, of which 5 were waited for; matrix products, arithmetic and copies ran while one was open for 3% of the time, Pallas kernels for 16%

profile of v1, /device:TPU:0, one launch (start us, length us, event | category | flops | bytes accessed | tf_op | source)
XLA Modules:
  0.0 192.8 jit_solution(13123903514279560363)
XLA Ops:
  0.6 2.1 %copy.13.table_ref = bf16[512,512]{1,0:T(8,128)(2,1)} copy(bf16[512,512]{0,1:T(8,128)(2,1)} %constant.10.clone) | data formatting | bytes 1048576 | tf_op jit(solution)/shard_map/optimization_barrier | solution.py:423
  2.7 8.3 %coil_forward_0.1 = bf16[32,2,128,128]{3,2,1,0:T(8,128)(2,1)} custom-call(bf16[512,512]{1,0:T(8,128)(2,1)} %copy.13.table_ref, bf16[4,2,8,256,128]{4,3,2,1,0:T(8,128)(2,1)} %refs_2_.5, f32[2,8,256,128]{3,2,1,0:T(8,128)} %image_ref.3), custom_call_target="tpu_custom_call" | custom-call | tf_op jit(solution)/shard_map/coil_forward_0/pallas_call | solution.py:85
  11.0 7.4 %all-to-all-start.2 = ((bf16[32,2,128,128]{3,2,1,0:T(8,128)(2,1)}), bf16[32,2,128,128]{3,2,1,0:T(8,128)(2,1)S(1)}, u32[]{:S(2)}, u32[]{:S(2)}) async-start(bf16[32,2,128,128]{3,2,1,0:T(8,128)(2,1)} %coil_forward_0.1), calls=%async_computation.2 | async-start | bytes 4194304 | tf_op jit(solution)/shard_map/all_to_all | solution.py:437
  18.4 8.4 %coil_forward_1.1 = bf16[32,2,128,128]{3,2,1,0:T(8,128)(2,1)} custom-call(bf16[512,512]{1,0:T(8,128)(2,1)} %copy.13.table_ref, bf16[4,2,8,256,128]{4,3,2,1,0:T(8,128)(2,1)} %refs_2_.5, f32[2,8,256,128]{3,2,1,0:T(8,128)} %image_ref.3), custom_call_target="tpu_custom_call" | custom-call | tf_op jit(solution)/shard_map/coil_forward_1/pallas_call | solution.py:85
  26.8 0.0 copy-start.5
  26.8 20.5 %all-to-all-done.2 = bf16[32,2,128,128]{3,2,1,0:T(8,128)(2,1)S(1)} async-done(((bf16[32,2,128,128]{3,2,1,0:T(8,128)(2,1)}), bf16[32,2,128,128]{3,2,1,0:T(8,128)(2,1)S(1)}, u32[]{:S(2)}, u32[]{:S(2)}) %all-to-all-start.2) | async-done | bytes 2097184 | tf_op jit(solution)/shard_map/all_to_all | solution.py:437
  47.3 0.0 copy-start.1
  47.3 1.4 copy-done.1
  48.8 4.0 %all-to-all-start = ((bf16[32,2,128,128]{3,2,1,0:T(8,128)(2,1)}), bf16[32,2,128,128]{3,2,1,0:T(8,128)(2,1)S(1)}, u32[]{:S(2)}, u32[]{:S(2)}) async-start(bf16[32,2,128,128]{3,2,1,0:T(8,128)(2,1)} %coil_forward_1.1), calls=%async_computation | async-start | bytes 4194304 | tf_op jit(solution)/shard_map/all_to_all | solution.py:437
  53.4 0.0 copy-done.5
  53.4 0.2 copy.15.refs_3_
  53.7 4.7 %copy.14 = bf16[1,24,128,512]{2,3,1,0:T(8,128)(2,1)} copy(bf16[1,24,128,512]{3,2,1,0:T(8,128)(2,1)} %param.12) | data formatting | bytes 6291456 | tf_op args[2]
  58.4 0.0 copy-start.6
  58.4 2.8 %samples_by_coil.1.refs_7_ = bf16[4,24,128,256]{3,2,1,0:T(8,128)(2,1)} custom-call(s32[1]{0:T(128)S(6)} %copy.21.counts_ref.refs_1_, bf16[24,128,8,128]{3,2,1,0:T(8,128)(2,1)} %bitcast.21), custom_call_target="tpu_custom_call" | custom-call | tf_op jit(solution)/shard_map/samples_by_coil/pallas_call | solution.py:114
  61.1 0.0 copy-done.6
  61.1 0.0 copy-start.2
  61.1 1.6 copy-done.2
  62.7 5.5 %grid_tile_0.1 = bf16[32,2,8,16,128]{4,3,2,1,0:T(8,128)(2,1)S(1)} custom-call(s32[1,24]{1,0:T(1,128)S(1)} %copy-done.6, s32[1]{0:T(128)S(6)} %copy.21.counts_ref.refs_1_, bf16[32,2,8,16,128]{4,3,2,1,0:T(8,128)(2,1)S(1)} %bitcast.13, bf16[512,512]{1,0:T(8,128)(2,1)S(1)} %copy.15.refs_3_, bf16[512,512]{1,0:T(8,128)(2,1)S(1)} %bitcast.14, ...), custom_call_target="tpu_custom_call" | custom-call | tf_op jit(solution)/shard_map/grid_tile_0/pallas_call | solution.py:244
  68.2 0.0 copy-start.3
  68.2 1.4 copy-done.3
  69.6 12.0 %all-to-all-done = bf16[32,2,128,128]{3,2,1,0:T(8,128)(2,1)S(1)} async-done(((bf16[32,2,128,128]{3,2,1,0:T(8,128)(2,1)}), bf16[32,2,128,128]{3,2,1,0:T(8,128)(2,1)S(1)}, u32[]{:S(2)}, u32[]{:S(2)}) %all-to-all-start) | async-done | bytes 2097184 | tf_op jit(solution)/shard_map/all_to_all | solution.py:437
  81.7 15.3 %all-to-all-start.3 = ((bf16[32,2,8,16,128]{4,3,2,1,0:T(8,128)(2,1)}), bf16[32,2,8,16,128]{4,3,2,1,0:T(8,128)(2,1)}, u32[]{:S(2)}, u32[]{:S(2)}) async-start(bf16[32,2,8,16,128]{4,3,2,1,0:T(8,128)(2,1)} %copy-done.3), calls=%async_computation.3 | async-start | bytes 4194304 | tf_op jit(solution)/shard_map/all_to_all | solution.py:446
  97.0 5.5 %grid_tile_1.1 = bf16[32,2,8,16,128]{4,3,2,1,0:T(8,128)(2,1)S(1)} custom-call(s32[1,24]{1,0:T(1,128)S(1)} %copy-done.6, s32[1]{0:T(128)S(6)} %copy.21.counts_ref.refs_1_, bf16[32,2,8,16,128]{4,3,2,1,0:T(8,128)(2,1)S(1)} %bitcast.12, bf16[512,512]{1,0:T(8,128)(2,1)S(1)} %copy.15.refs_3_, bf16[512,512]{1,0:T(8,128)(2,1)S(1)} %bitcast.15, ...), custom_call_target="tpu_custom_call" | custom-call | tf_op jit(solution)/shard_map/grid_tile_1/pallas_call | solution.py:244
  102.5 0.0 copy-start.4
  102.5 1.3 copy-done.4
  103.8 22.1 %all-to-all-done.3 = bf16[32,2,8,16,128]{4,3,2,1,0:T(8,128)(2,1)} async-done(((bf16[32,2,8,16,128]{4,3,2,1,0:T(8,128)(2,1)}), bf16[32,2,8,16,128]{4,3,2,1,0:T(8,128)(2,1)}, u32[]{:S(2)}, u32[]{:S(2)}) %all-to-all-start.3) | async-done | bytes 2097184 | tf_op jit(solution)/shard_map/all_to_all | solution.py:446
  125.9 4.0 %all-to-all-start.1 = ((bf16[32,2,8,16,128]{4,3,2,1,0:T(8,128)(2,1)}), bf16[32,2,8,16,128]{4,3,2,1,0:T(8,128)(2,1)S(1)}, u32[]{:S(2)}, u32[]{:S(2)}) async-start(bf16[32,2,8,16,128]{4,3,2,1,0:T(8,128)(2,1)} %copy-done.4), calls=%async_computation.1 | async-start | bytes 4194304 | tf_op jit(solution)/shard_map/all_to_all | solution.py:446
  129.9 6.2 %gradient_0.1.refs_3_ = f32[2,8,256,128]{3,2,1,0:T(8,128)} custom-call(bf16[512,512]{1,0:T(8,128)(2,1)} %bitcast.22, bf16[32,2,128,128]{3,2,1,0:T(8,128)(2,1)} %bitcast.11.refs_1_, bf16[4,2,8,256,128]{4,3,2,1,0:T(8,128)(2,1)} %refs_2_.5), custom_call_target="tpu_custom_call" | custom-call | tf_op jit(solution)/shard_map/gradient_0/pallas_call | solution.py:319
  136.1 22.7 %all-to-all-done.1 = bf16[32,2,8,16,128]{4,3,2,1,0:T(8,128)(2,1)S(1)} async-done(((bf16[32,2,8,16,128]{4,3,2,1,0:T(8,128)(2,1)}), bf16[32,2,8,16,128]{4,3,2,1,0:T(8,128)(2,1)S(1)}, u32[]{:S(2)}, u32[]{:S(2)}) %all-to-all-start.1) | async-done | bytes 2097184 | tf_op jit(solution)/shard_map/all_to_all | solution.py:446
  158.8 0.0 copy-start.7
  158.8 1.3 copy-done.7
  160.1 0.0 copy-start
  160.1 1.6 copy-done
  161.7 6.0 %gradient_1.1 = bf16[4,2,8,64,128]{4,3,2,1,0:T(8,128)(2,1)} custom-call(bf16[512,512]{1,0:T(8,128)(2,1)} %bitcast.23, bf16[32,2,128,128]{3,2,1,0:T(8,128)(2,1)} %bitcast.20, bf16[4,2,8,256,128]{4,3,2,1,0:T(8,128)(2,1)} %refs_2_.5, f32[2,8,256,128]{3,2,1,0:T(8,128)S(1)} %copy-done), custom_call_target="tpu_custom_call" | custom-call | tf_op jit(solution)/shard_map/gradient_1/pallas_call | solution.py:319
  167.7 5.3 %all-to-all-start.4 = ((bf16[4,2,8,64,128]{4,3,2,1,0:T(8,128)(2,1)}), bf16[4,2,8,64,128]{4,3,2,1,0:T(8,128)(2,1)S(1)}, u32[]{:S(2)}, u32[]{:S(2)}) async-start(bf16[4,2,8,64,128]{4,3,2,1,0:T(8,128)(2,1)} %gradient_1.1), calls=%async_computation.4 | async-start | bytes 2097152 | tf_op jit(solution)/shard_map/all_to_all | solution.py:451
  173.1 3.5 %target.1.base_ref = f32[2,8,64,128]{3,2,1,0:T(8,128)} custom-call(s32[1]{0:T(128)} %bitcast.s, f32[2,8,256,128]{3,2,1,0:T(8,128)} %image_ref.3, f32[2,8,64,128]{3,2,1,0:T(8,128)} %refs_1_.3, f32[2,8,64,128]{3,2,1,0:T(8,128)} %dual_ref.1), custom_call_target="tpu_custom_call" | custom-call | tf_op jit(solution)/shard_map/target/pallas_call | solution.py:363
  176.6 11.4 %all-to-all-done.4.pieces_ref = bf16[4,2,8,64,128]{4,3,2,1,0:T(8,128)(2,1)S(1)} async-done(((bf16[4,2,8,64,128]{4,3,2,1,0:T(8,128)(2,1)}), bf16[4,2,8,64,128]{4,3,2,1,0:T(8,128)(2,1)S(1)}, u32[]{:S(2)}, u32[]{:S(2)}) %all-to-all-start.4) | async-done | bytes 1048608 | tf_op jit(solution)/shard_map/all_to_all | solution.py:451
  188.0 0.0 copy-start.8
  188.0 1.0 copy-done.8
  188.9 3.9 %update.1 = (f32[2,8,64,128]{3,2,1,0:T(8,128)}, f32[2,8,64,128]{3,2,1,0:T(8,128)}, f32[2,8,64,128]{3,2,1,0:T(8,128)}) custom-call(f32[2,8,64,128]{3,2,1,0:T(8,128)} %target.1.base_ref, bf16[4,2,8,64,128]{4,3,2,1,0:T(8,128)(2,1)} %copy-done.8, f32[2,8,64,128]{3,2,1,0:T(8,128)} %dual_ref.1), custom_call_target="tpu_custom_call" | custom-call | tf_op jit(solution)/shard_map/update/pallas_call | solution.py:407
Async XLA Ops:
  11.0 36.3 %all-to-all-start.2 = ((bf16[32,2,128,128]{3,2,1,0:T(8,128)(2,1)}), bf16[32,2,128,128]{3,2,1,0:T(8,128)(2,1)S(1)}, u32[]{:S(2)}, u32[]{:S(2)}) async-start(bf16[32,2,128,128]{3,2,1,0:T(8,128)(2,1)} %coil_forward_0.1), calls=%async_computation.2 | async-start | bytes 4194304 | tf_op jit(solution)/shard_map/all_to_all | solution.py:437
  26.8 26.6 %copy-start.5 = (bf16[512,512]{0,1:T(8,128)(2,1)S(1)}, bf16[512,512]{0,1:T(8,128)(2,1)}, u32[]{:S(2)}) copy-start(bf16[512,512]{0,1:T(8,128)(2,1)} %constant.11.clone) | copy-start | bytes 1572868
  47.3 1.5 copy-start.1
  48.8 32.9 %all-to-all-start = ((bf16[32,2,128,128]{3,2,1,0:T(8,128)(2,1)}), bf16[32,2,128,128]{3,2,1,0:T(8,128)(2,1)S(1)}, u32[]{:S(2)}, u32[]{:S(2)}) async-start(bf16[32,2,128,128]{3,2,1,0:T(8,128)(2,1)} %coil_forward_1.1), calls=%async_computation | async-start | bytes 4194304 | tf_op jit(solution)/shard_map/all_to_all | solution.py:437
  58.4 2.8 %copy-start.6 = (s32[1,24]{1,0:T(1,128)S(1)}, s32[1,24]{1,0:T(1,128)}, u32[]{:S(2)}) copy-start(s32[1,24]{1,0:T(1,128)} %refs_0_.5) | copy-start | bytes 292
  61.1 1.6 copy-start.2
  68.2 1.5 copy-start.3
  81.7 44.2 %all-to-all-start.3 = ((bf16[32,2,8,16,128]{4,3,2,1,0:T(8,128)(2,1)}), bf16[32,2,8,16,128]{4,3,2,1,0:T(8,128)(2,1)}, u32[]{:S(2)}, u32[]{:S(2)}) async-start(bf16[32,2,8,16,128]{4,3,2,1,0:T(8,128)(2,1)} %copy-done.3), calls=%async_computation.3 | async-start | bytes 4194304 | tf_op jit(solution)/shard_map/all_to_all | solution.py:446
  102.5 1.3 copy-start.4
  125.9 32.9 %all-to-all-start.1 = ((bf16[32,2,8,16,128]{4,3,2,1,0:T(8,128)(2,1)}), bf16[32,2,8,16,128]{4,3,2,1,0:T(8,128)(2,1)S(1)}, u32[]{:S(2)}, u32[]{:S(2)}) async-start(bf16[32,2,8,16,128]{4,3,2,1,0:T(8,128)(2,1)} %copy-done.4), calls=%async_computation.1 | async-start | bytes 4194304 | tf_op jit(solution)/shard_map/all_to_all | solution.py:446
  158.8 1.3 copy-start.7
  160.1 1.6 copy-start
  167.7 20.2 %all-to-all-start.4 = ((bf16[4,2,8,64,128]{4,3,2,1,0:T(8,128)(2,1)}), bf16[4,2,8,64,128]{4,3,2,1,0:T(8,128)(2,1)S(1)}, u32[]{:S(2)}, u32[]{:S(2)}) async-start(bf16[4,2,8,64,128]{4,3,2,1,0:T(8,128)(2,1)} %gradient_1.1), calls=%async_computation.4 | async-start | bytes 2097152 | tf_op jit(solution)/shard_map/all_to_all | solution.py:451
  188.0 1.0 copy-start.8

commit v2 on v1

v2 whole, which is shorter than its diff:
```python
import math

import jax
import jax.numpy as jnp
import numpy as np
import ml_dtypes
from jax import lax
from jax.experimental import pallas as pl
from jax.experimental.pallas import tpu as pltpu
from jax.sharding import PartitionSpec as P

N = 256
Z = 128
WIN = 64
P_SIZE = 128
CH = 24
KYD = 8
TILES = 32
CELLS = WIN * KYD
ROWS = N * KYD
NCOIL = 4
PER = 2

step_size = 0.5
penalty = 1.0
threshold = 0.3

BF = jnp.bfloat16
F32 = jnp.float32


def dft_parts():
    index = np.arange(N)
    angle = (index[:, None] * index[None, :] % N).astype(np.float32) * np.float32(2.0 * math.pi / N)
    factor = np.float32(1.0 / math.sqrt(N))
    re = (np.cos(angle) * factor).astype(ml_dtypes.bfloat16)
    im = (-np.sin(angle) * factor).astype(ml_dtypes.bfloat16)
    return re, im


def real_tables():
    re, im = dft_parts()
    along_y = np.stack(
        [np.concatenate([re, -im], 1), np.concatenate([im, re], 1)], 1
    ).reshape(2 * N, 2 * N)
    re_c = re.reshape(N, TILES, KYD)
    im_c = im.reshape(N, TILES, KYD)
    along_x = np.stack(
        [np.stack([re_c, -im_c], 2), np.stack([im_c, re_c], 2)], 0
    ).reshape(2 * N, 2 * N)
    return along_y, along_x


def hbm(shape, dtype):
    return pltpu.HBM(shape, dtype)


def in_hbm(x):
    return pltpu.with_memory_space_constraint(x, pltpu.HBM)


VMEM = pl.BlockSpec(memory_space=pltpu.VMEM)
SMEM = pl.BlockSpec(memory_space=pltpu.SMEM)
HBM = pl.BlockSpec(memory_space=pltpu.HBM)
DMA = pltpu.SemaphoreType.DMA


def coil_kernel(
    chunk, table_hbm, sens_hbm, image_hbm, out_hbm, table, sens, image, spread, out, sems, done
):
    def copies(step):
        rows = pl.ds(2 * step, 2)
        return [
            pltpu.make_async_copy(image_hbm.at[:, rows], image.at[:, rows], sems.at[PER, step])
        ] + [
            pltpu.make_async_copy(
                sens_hbm.at[chunk * PER + c, :, rows], sens.at[c, :, rows], sems.at[c, step]
            )
            for c in range(PER)
        ]

    whole = pltpu.make_async_copy(table_hbm, table, done.at[PER])
    whole.start()
    pending = [copies(step) for step in range(4)]
    for step in range(4):
        for copy in pending[step][:2]:
            copy.start()
    for step in range(4):
        for copy in pending[step][2:]:
            copy.start()
    whole.wait()

    def leave(c):
        return pltpu.make_async_copy(out.at[:, c], out_hbm.at[:, c], done.at[c])

    def one_coil(c, carry):
        for step in range(4):

            @pl.when(c == 0)
            def _():
                pending[step][0].wait()

            arrival = pltpu.make_async_copy(
                sens_hbm.at[chunk * PER + c, :, pl.ds(2 * step, 2)],
                sens.at[c, :, pl.ds(2 * step, 2)],
                sems.at[c, step],
            )
            arrival.wait()
            parts = []
            for x in (2 * step, 2 * step + 1):
                s_re = sens[c, 0, x].astype(F32)
                s_im = sens[c, 1, x].astype(F32)
                m_re = image[0, x]
                m_im = image[1, x]
                c_re = (s_re * m_re - s_im * m_im).astype(BF)
                c_im = (s_re * m_im + s_im * m_re).astype(BF)
                parts.append(jnp.concatenate([c_re, c_im], 0))
            data = jnp.concatenate(parts, 1)
            result = jnp.dot(table[...], data, preferred_element_type=F32)
            for i in range(2):
                spread[pl.ds(2 * step + i, 2 * N, stride=KYD), :] = result[:, i * Z : (i + 1) * Z]
        out[:, c] = spread[...].astype(BF).reshape(TILES, 128, Z)
        leave(c).start()
        return carry

    lax.fori_loop(0, PER, one_coil, 0)
    for c in range(PER):
        leave(c).wait()


def coil_forward(chunk, table, sensitivity, image):
    def kernel(*refs):
        coil_kernel(chunk, *refs)

    return pl.pallas_call(
        kernel,
        out_shape=hbm((TILES, PER, 128, Z), BF),
        in_specs=[HBM, HBM, HBM],
        out_specs=HBM,
        scratch_shapes=[
            pltpu.VMEM((2 * N, 2 * N), BF),
            pltpu.VMEM((PER, 2, KYD, N, Z), BF),
            pltpu.VMEM((2, KYD, N, Z), F32),
            pltpu.VMEM((TILES * 128, Z), F32),
            pltpu.VMEM((TILES, PER, 128, Z), BF),
            DMA((PER + 1, 4)),
            DMA((PER + 1,)),
        ],
        compiler_params=pltpu.CompilerParams(vmem_limit_bytes=18 << 20),
        name=f"coil_forward_{chunk}",
    )(table, sensitivity, image)


def samples_kernel(counts_ref, samples_hbm, out_hbm, samples, spread, out, arrive, leave):
    count = counts_ref[0]

    def into(j):
        return pltpu.make_async_copy(samples_hbm.at[j], samples.at[j], arrive.at[j])

    def back(j):
        return pltpu.make_async_copy(out.at[:, j], out_hbm.at[:, j], leave.at[j])

    def start(j, carry):
        into(j).start()
        return carry

    def group(j, carry):
        into(j).wait()
        slot = j % 2
        spread[slot] = samples[j].astype(F32).reshape(P_SIZE * 8, Z)
        for coil in range(NCOIL):
            for part in range(2):
                out[coil, j, :, part * Z : (part + 1) * Z] = spread[
                    slot, pl.ds(2 * coil + part, P_SIZE, stride=8), :
                ].astype(BF)
        back(j).start()
        return carry

    def finish(j, carry):
        back(j).wait()
        return carry

    lax.fori_loop(0, count, start, 0)
    lax.fori_loop(0, count, group, 0)
    lax.fori_loop(0, count, finish, 0)


def samples_by_coil(counts, samples):
    return pl.pallas_call(
        samples_kernel,
        out_shape=hbm((NCOIL, CH, P_SIZE, 2 * Z), BF),
        in_specs=[SMEM, HBM],
        out_specs=HBM,
        scratch_shapes=[
            pltpu.VMEM((CH, P_SIZE, 8, Z), BF),
            pltpu.VMEM((2, P_SIZE * 8, Z), F32),
            pltpu.VMEM((NCOIL, CH, P_SIZE, 2 * Z), BF),
            DMA((CH,)),
            DMA((CH,)),
        ],
        compiler_params=pltpu.CompilerParams(vmem_limit_bytes=18 << 20),
        name="samples_by_coil",
    )(counts, samples)


def grid_kernel(
    chunk,
    offsets_ref,
    counts_ref,
    piece_hbm,
    forward_ref,
    inverse_ref,
    blocks_hbm,
    turned_hbm,
    samples_hbm,
    out_hbm,
    piece,
    blocks,
    turned,
    samples,
    window,
    total,
    out,
    sems,
    leave,
):
    count = counts_ref[0]
    arrival = pltpu.make_async_copy(piece_hbm, piece, leave.at[PER])
    arrival.start()

    def copies(j):
        return [
            pltpu.make_async_copy(blocks_hbm.at[j], blocks.at[j], sems.at[0, j]),
            pltpu.make_async_copy(turned_hbm.at[j], turned.at[j], sems.at[1, j]),
        ] + [
            pltpu.make_async_copy(
                samples_hbm.at[chunk * PER + c, j],
                samples.at[j, :, pl.ds(2 * Z * c, 2 * Z)],
                sems.at[2 + c, j],
            )
            for c in range(PER)
        ]

    def start(j, carry):
        for copy in copies(j):
            copy.start()
        return carry

    lax.fori_loop(0, count, start, 0)

    arrival.wait()

    def forward_row(ky, carry):
        data = jnp.concatenate(
            [piece[:, c, ky].reshape(2 * N, Z) for c in range(PER)], 1
        )
        result = jnp.dot(forward_ref[...], data, preferred_element_type=F32)
        for c in range(PER):
            for part in range(2):
                total[2 * c + part, pl.ds(ky, N, stride=KYD), :] = result[
                    part * N : (part + 1) * N, c * Z : (c + 1) * Z
                ]
        return carry

    lax.fori_loop(0, KYD, forward_row, 0)
    for s in range(2 * PER):
        lanes = slice(s * Z, (s + 1) * Z)
        total[s, ROWS : ROWS + KYD, :] = jnp.zeros((KYD, Z), F32)
        window[0, :, lanes] = total[s, 0:ROWS, :].astype(BF)
        window[1, :, lanes] = total[s, KYD : ROWS + KYD, :].astype(BF)
    total[...] = jnp.zeros_like(total)

    def arrive(j):
        for copy in copies(j):
            copy.wait()

    def predict(j):
        first = offsets_ref[0, j]
        row = pl.multiple_of((first // 2) * (2 * KYD), 2 * KYD)
        view = window[first % 2, pl.ds(row, CELLS), :]
        predicted = jnp.dot(blocks[j], view, preferred_element_type=F32)
        return (predicted - samples[j].astype(F32)).astype(BF)

    def add_back(j, misfit):
        update = jnp.dot(turned[j], misfit, preferred_element_type=F32)
        spot = pl.ds(pl.multiple_of(offsets_ref[0, j] * KYD, KYD), CELLS)
        for s in range(2 * PER):
            total[s, spot, :] = total[s, spot, :] + update[:, s * Z : (s + 1) * Z]

    arrive(0)
    samples[0] = predict(0)

    def group(j, carry):
        arrive(j)
        before = samples[j - 1]
        misfit = predict(j)
        add_back(j - 1, before)
        samples[j] = misfit
        return carry

    lax.fori_loop(1, count, group, 0)
    add_back(count - 1, samples[count - 1])

    leaving = []
    for c in range(PER):

        def inverse_rows(pair, carry):
            data = jnp.concatenate(
                [
                    jnp.concatenate(
                        [
                            total[2 * c + part, pl.ds(2 * pair + i, N, stride=KYD), :].astype(BF)
                            for part in range(2)
                        ],
                        0,
                    )
                    for i in range(2)
                ],
                1,
            )
            result = jnp.dot(inverse_ref[...], data, preferred_element_type=F32).astype(BF)
            for i in range(2):
                out[:, c, 2 * pair + i] = result[:, i * Z : (i + 1) * Z].reshape(TILES, 16, Z)
            return carry

        lax.fori_loop(0, KYD // 2, inverse_rows, 0)
        copy = pltpu.make_async_copy(out.at[:, c], out_hbm.at[:, c], leave.at[c])
        copy.start()
        leaving.append(copy)
    for copy in leaving:
        copy.wait()


def grid_tile(chunk, offsets, counts, piece, forward, inverse, blocks, turned, samples):
    def kernel(*refs):
        grid_kernel(chunk, *refs)

    return pl.pallas_call(
        kernel,
        out_shape=hbm((TILES, PER, KYD, 16, Z), BF),
        in_specs=[SMEM, SMEM, HBM, VMEM, VMEM, HBM, HBM, HBM],
        out_specs=HBM,
        scratch_shapes=[
            pltpu.VMEM((TILES, PER, KYD, 16, Z), BF),
            pltpu.VMEM((CH, P_SIZE, CELLS), BF),
            pltpu.VMEM((CH, CELLS, P_SIZE), BF),
            pltpu.VMEM((CH, P_SIZE, 2 * Z * PER), BF),
            pltpu.VMEM((2, ROWS, 2 * Z * PER), BF),
            pltpu.VMEM((2 * PER, ROWS + KYD, Z), F32),
            pltpu.VMEM((TILES, PER, KYD, 16, Z), BF),
            DMA((2 + PER, CH)),
            DMA((PER + 1,)),
        ],
        compiler_params=pltpu.CompilerParams(vmem_limit_bytes=30 << 20),
        name=f"grid_tile_{chunk}",
    )(offsets, counts, piece, forward, inverse, blocks, turned, samples)


def gradient_kernel(chunk, table_ref, piece_hbm, sens_hbm, *rest):
    first = chunk == 0
    last = chunk == NCOIL // PER - 1
    rest = list(rest)
    before_ref = None if first else rest.pop(0)
    out_ref = rest.pop(0)
    piece, sens, spread, sems, arrive = rest[:5]
    if last:
        out, leave = rest[5:]
    half = TILES // 2

    def sens_copy(step):
        rows = pl.ds(2 * step, 2)
        return pltpu.make_async_copy(
            sens_hbm.at[pl.ds(chunk * PER, PER), :, rows], sens.at[:, :, rows], sems.at[step]
        )

    def leave_copy(step):
        rows = pl.ds(2 * step, 2)
        return pltpu.make_async_copy(out.at[:, :, rows], out_ref.at[:, :, rows], leave.at[step])

    arrivals = []
    for c in range(PER):
        for h in range(2):
            tiles = pl.ds(h * half, half)
            copy = pltpu.make_async_copy(
                piece_hbm.at[tiles, c], piece.at[tiles, c], arrive.at[c, h]
            )
            copy.start()
            arrivals.append((c, h, copy))
    for step in range(4):
        sens_copy(step).start()
    for c, h, copy in arrivals:
        copy.wait()
        spread[c, h * half * 128 : (h + 1) * half * 128, :] = (
            piece[h * half : (h + 1) * half, c].astype(F32).reshape(half * 128, Z)
        )

    def rows_pair(step, carry):
        sens_copy(step).wait()
        for i in range(2):
            x = 2 * step + i
            data = jnp.concatenate(
                [spread[c, pl.ds(x, 2 * N, stride=KYD), :].astype(BF) for c in range(PER)], 1
            )
            result = jnp.dot(table_ref[...], data, preferred_element_type=F32)
            result = result.astype(BF).astype(F32)
            g_re = None if first else before_ref[0, x]
            g_im = None if first else before_ref[1, x]
            for c in range(PER):
                lanes = slice(c * Z, (c + 1) * Z)
                a_re = result[:N, lanes]
                a_im = result[N:, lanes]
                s_re = sens[c, 0, x].astype(F32)
                s_im = sens[c, 1, x].astype(F32)
                t_re = s_re * a_re + s_im * a_im
                t_im = s_re * a_im - s_im * a_re
                g_re = t_re if g_re is None else g_re + t_re
                g_im = t_im if g_im is None else g_im + t_im
            if last:
                out[:, 0, x] = g_re.astype(BF).reshape(NCOIL, N // NCOIL, Z)
                out[:, 1, x] = g_im.astype(BF).reshape(NCOIL, N // NCOIL, Z)
            else:
                out_ref[0, x] = g_re
                out_ref[1, x] = g_im
        if last:
            leave_copy(step).start()
        return carry

    lax.fori_loop(0, 4, rows_pair, 0)
    if last:
        for step in range(4):
            leave_copy(step).wait()


def gradient_step(chunk, table, piece, sensitivity, before):
    first = chunk == 0
    last = chunk == NCOIL // PER - 1

    def kernel(*refs):
        gradient_kernel(chunk, *refs)

    shares = (NCOIL, 2, KYD, N // NCOIL, Z)
    return pl.pallas_call(
        kernel,
        out_shape=hbm(shares, BF) if last else jax.ShapeDtypeStruct((2, KYD, N, Z), F32),
        in_specs=[VMEM, HBM, HBM] + ([] if first else [VMEM]),
        out_specs=HBM if last else VMEM,
        scratch_shapes=[
            pltpu.VMEM((TILES, PER, 128, Z), BF),
            pltpu.VMEM((PER, 2, KYD, N, Z), BF),
            pltpu.VMEM((PER, TILES * 128, Z), F32),
            DMA((4,)),
            DMA((PER, 2)),
        ]
        + ([pltpu.VMEM(shares, BF), DMA((4,))] if last else []),
        compiler_params=pltpu.CompilerParams(vmem_limit_bytes=18 << 20),
        name=f"gradient_{chunk}",
    )(*([table, piece, sensitivity] + ([] if first else [before])))


def haar_rows(top, low):
    add = (top + low) * 0.5
    sub = (top - low) * 0.5
    cols = top.shape[0]
    odd = lax.broadcasted_iota(jnp.int32, top.shape, 0) % 2 == 1

    def pairs(v):
        ahead = pltpu.roll(v, cols - 1, 0)
        behind = pltpu.roll(v, 1, 0)
        return jnp.where(odd, behind - v, v + ahead)

    return pairs(add), pairs(sub)


def target_kernel(position_ref, image_hbm, aux_ref, dual_ref, out_ref, image, sem):
    share = N // NCOIL
    columns = pl.ds(pl.multiple_of(position_ref[0] * share, share), share)
    copy = pltpu.make_async_copy(image_hbm.at[:, :, columns], image, sem)
    copy.start()
    copy.wait()
    for m in range(KYD // 2):
        for part in range(2):
            rows = haar_rows(
                *(aux_ref[part, 2 * m + i] - dual_ref[part, 2 * m + i] for i in range(2))
            )
            for i in range(2):
                current = image[part, 2 * m + i]
                out_ref[part, 2 * m + i] = current - step_size * penalty * (current - rows[i])


def target_step(position, image, auxiliary, scaled_dual):
    return pl.pallas_call(
        target_kernel,
        out_shape=jax.ShapeDtypeStruct(auxiliary.shape, F32),
        in_specs=[SMEM, HBM, VMEM, VMEM],
        out_specs=VMEM,
        scratch_shapes=[pltpu.VMEM(auxiliary.shape, F32), DMA],
        compiler_params=pltpu.CompilerParams(vmem_limit_bytes=6 << 20),
        name="target",
    )(position, image, auxiliary, scaled_dual)


def update_kernel(
    base_ref, pieces_ref, dual_ref, image_hbm, aux_hbm, dual_hbm, image, aux, dual, sems
):
    leaving = []
    for m in range(KYD // 2):
        coeffs = []
        for part in range(2):
            rows = []
            for x in (2 * m, 2 * m + 1):
                gradient = pieces_ref[0, part, x].astype(F32)
                for k in range(1, NCOIL):
                    gradient = gradient + pieces_ref[k, part, x].astype(F32)
                value = base_ref[part, x] - step_size * gradient
                image[part, x] = value
                rows.append(value)
            top, low = haar_rows(*rows)
            coeffs.append((top + dual_ref[part, 2 * m], low + dual_ref[part, 2 * m + 1]))
        for i in range(2):
            c_re = coeffs[0][i]
            c_im = coeffs[1][i]
            magnitude = jnp.sqrt(c_re * c_re + c_im * c_im)
            factor = jnp.maximum(1.0 - threshold / jnp.maximum(magnitude, threshold), 0.0)
            for part, value in enumerate((c_re, c_im)):
                kept = value * factor
                aux[part, 2 * m + i] = kept
                dual[part, 2 * m + i] = value - kept
        pair = pl.ds(2 * m, 2)
        for k, (near, far) in enumerate(((image, image_hbm), (aux, aux_hbm), (dual, dual_hbm))):
            copy = pltpu.make_async_copy(near.at[:, pair], far.at[:, pair], sems.at[k, m])
            copy.start()
            leaving.append(copy)
    for copy in leaving:
        copy.wait()


def update_step(base, pieces, scaled_dual):
    shape = hbm(scaled_dual.shape, F32)
    return pl.pallas_call(
        update_kernel,
        out_shape=(shape, shape, shape),
        in_specs=[VMEM, VMEM, VMEM],
        out_specs=(HBM, HBM, HBM),
        scratch_shapes=[pltpu.VMEM(scaled_dual.shape, F32)] * 3 + [DMA((3, KYD // 2))],
        compiler_params=pltpu.CompilerParams(vmem_limit_bytes=8 << 20),
        name="update",
    )(base, pieces, scaled_dual)


def body(image, sensitivity, blocks, samples, offsets, counts, auxiliary, scaled_dual):
    along_y, along_x = real_tables()
    y_forward, x_forward = jnp.asarray(along_y), jnp.asarray(along_x)
    y_kept, x_kept = lax.optimization_barrier((y_forward, x_forward))
    y_inverse = y_kept.T
    x_inverse = x_kept.T

    image, sensitivity = in_hbm(image), in_hbm(sensitivity)
    y_forward = in_hbm(y_forward)
    turned = jnp.swapaxes(blocks[0], 1, 2)
    by_coil = samples_by_coil(counts, in_hbm(samples.reshape(CH, P_SIZE, 2 * NCOIL, Z)))

    chunks = range(NCOIL // PER)
    pieces = []
    for chunk in chunks:
        half = coil_forward(chunk, y_forward, sensitivity, image)
        if chunk == 1:
            half, turned, by_coil, y_inverse, x_inverse = lax.optimization_barrier(
                (half, turned, by_coil, y_inverse, x_inverse)
            )
        piece = lax.all_to_all(half, "slab", 0, 0, tiled=True)
        pieces.append(piece.reshape(TILES, PER, KYD, 16, Z))
    position = lax.axis_index("coil").reshape(1)
    base = target_step(position, image, auxiliary, scaled_dual)
    backs = []
    for chunk in chunks:
        back = grid_tile(
            chunk,
            offsets,
            counts,
            in_hbm(pieces[chunk]),
            x_forward,
            x_inverse,
            in_hbm(blocks[0]),
            in_hbm(turned),
            in_hbm(by_coil),
        )
        backs.append(lax.all_to_all(back, "slab", 0, 0, tiled=True))
    total = None
    for chunk in chunks:
        piece = in_hbm(backs[chunk].reshape(TILES, PER, 128, Z))
        total = gradient_step(chunk, y_inverse, piece, sensitivity, total)
    shares = lax.all_to_all(total, "coil", 0, 0, tiled=True)
    return update_step(base, shares, scaled_dual)


def solution(mesh):
    return jax.shard_map(
        body,
        mesh=mesh,
        in_specs=(
            P(None, "slab", None, None),
            P("coil", None, "slab", None, None),
            P("slab", None, None, None),
            P("slab", None, None, "coil", None, None),
            P("slab", None),
            P("slab"),
            P(None, "slab", "coil", None),
            P(None, "slab", "coil", None),
        ),
        out_specs=(
            P(None, "slab", "coil", None),
            P(None, "slab", "coil", None),
            P(None, "slab", "coil", None),
        ),
        check_vma=False,
    )
```

time: 194 us -> 173 us (0.89)
  local copies, waits for them, and re-layouts: 16.7 us -> 4.24 us
  starting transfers between devices: 36 us -> 26.5 us
    unnamed x19 -> x17, local copies, waits for them, and re-layouts: 14.4 us -> 4.24 us
    all_to_all x2, starting transfers between devices: 19.3 us -> 9.53 us  [body(): backs.append(lax.all_to_all(back, 'slab', 0, 0, tiled=True))]
    all_to_all x2, waiting for transfers between devices: 44.8 us -> 42.4 us  [body(): backs.append(lax.all_to_all(back, 'slab', 0, 0, tiled=True))]
    optimization_barrier x2 -> x0, local copies, waits for them, and re-layouts: 2.26 us -> none  [body(): lax.optimization_barrier((jnp.asarray(along_y), jnp.asarray(along_x)))]
    all_to_all x1, waiting for transfers between devices: 11.4 us -> 13.6 us  [body(): shares = lax.all_to_all(total, 'coil', 0, 0, tiled=True)]
  transfers between devices with their start and end apart: 5 -> 5, of which waited for: 5 -> 5; matrix products, arithmetic and copies ran while one was open for 3% -> 2% of each run, Pallas kernels for 16% -> 21%
where the time goes in v2:
time: 173 us
  waiting for transfers between devices  89.9 us (52%)
  Pallas kernels  50.5 us (29%)
  starting transfers between devices  26.5 us (15%)
  local copies, waits for them, and re-layouts  4.24 us (2%)
    all_to_all x2, waiting for transfers between devices, body(): backs.append(lax.all_to_all(back, 'slab', 0, 0, tiled=True))  42.4 us
    all_to_all x2, waiting for transfers between devices, body(): piece = lax.all_to_all(half, 'slab', 0, 0, tiled=True)  33.9 us
    pallas_call x2, Pallas kernels, grid_tile(): pl.pallas_call(kernel, out_shape=hbm((TILES, PER, KYD, 16, Z), BF), in_sp...  21.6 us
    pallas_call x2, Pallas kernels, coil_forward(): pl.pallas_call(kernel, out_shape=hbm((TILES, PER, 128, Z), BF), in_specs=...  14.3 us
    all_to_all x1, waiting for transfers between devices, body(): shares = lax.all_to_all(total, 'coil', 0, 0, tiled=True)  13.6 us
    all_to_all x2, starting transfers between devices, body(): piece = lax.all_to_all(half, 'slab', 0, 0, tiled=True)  11.6 us
    pallas_call x2, Pallas kernels, gradient_step(): pl.pallas_call(kernel, out_shape=hbm(shares, BF) if last else jax.ShapeDt...  9.78 us
    all_to_all x2, starting transfers between devices, body(): backs.append(lax.all_to_all(back, 'slab', 0, 0, tiled=True))  9.53 us
  transfers between devices with their start and end apart: 5, of which 5 were waited for; matrix products, arithmetic and copies ran while one was open for 2% of the time, Pallas kernels for 21%

profile of v2, /device:TPU:0, one launch (start us, length us, event | category | flops | bytes accessed | tf_op | source)
XLA Modules:
  0.0 172.6 jit_solution(13277852571534026043)
XLA Ops:
  0.6 7.1 %coil_forward_0.1 = bf16[32,2,128,128]{3,2,1,0:T(8,128)(2,1)} custom-call(bf16[512,512]{1,0:T(8,128)(2,1)} %constant.20.refs_0_, bf16[4,2,8,256,128]{4,3,2,1,0:T(8,128)(2,1)} %refs_2_.7, f32[2,8,256,128]{3,2,1,0:T(8,128)} %refs_2_.5), custom_call_target="tpu_custom_call" | custom-call | tf_op jit(solution)/shard_map/coil_forward_0/pallas_call | solution.py:135
  7.7 7.5 %all-to-all-start.2 = ((bf16[32,2,128,128]{3,2,1,0:T(8,128)(2,1)}), bf16[32,2,128,128]{3,2,1,0:T(8,128)(2,1)}, u32[]{:S(2)}, u32[]{:S(2)}) async-start(bf16[32,2,128,128]{3,2,1,0:T(8,128)(2,1)} %coil_forward_0.1), calls=%async_computation.2 | async-start | bytes 4194304 | tf_op jit(solution)/shard_map/all_to_all | solution.py:570
  15.3 0.0 copy-start.6
  15.3 7.2 %coil_forward_1.1 = bf16[32,2,128,128]{3,2,1,0:T(8,128)(2,1)} custom-call(bf16[512,512]{1,0:T(8,128)(2,1)} %constant.20.refs_0_, bf16[4,2,8,256,128]{4,3,2,1,0:T(8,128)(2,1)} %refs_2_.7, f32[2,8,256,128]{3,2,1,0:T(8,128)} %refs_2_.5), custom_call_target="tpu_custom_call" | custom-call | tf_op jit(solution)/shard_map/coil_forward_1/pallas_call | solution.py:135
  23.2 0.0 copy-done.6
  23.2 2.9 %copy.14 = bf16[1,24,128,512]{2,3,1,0:T(8,128)(2,1)} copy(bf16[1,24,128,512]{3,2,1,0:T(8,128)(2,1)S(1)} %copy-done.6) | data formatting | bytes 6291456 | tf_op args[2]
  26.0 2.2 %samples_by_coil.1.refs_7_ = bf16[4,24,128,256]{3,2,1,0:T(8,128)(2,1)} custom-call(s32[1]{0:T(128)S(6)} %copy.21.counts_ref.refs_1_, bf16[24,128,8,128]{3,2,1,0:T(8,128)(2,1)} %bitcast.21), custom_call_target="tpu_custom_call" | custom-call | tf_op jit(solution)/shard_map/samples_by_coil/pallas_call | solution.py:189
  28.3 0.0 copy-start.1
  28.3 0.0 copy-start.2
  28.3 0.0 copy-start.5
  28.3 15.8 %all-to-all-done.2 = bf16[32,2,128,128]{3,2,1,0:T(8,128)(2,1)} async-done(((bf16[32,2,128,128]{3,2,1,0:T(8,128)(2,1)}), bf16[32,2,128,128]{3,2,1,0:T(8,128)(2,1)}, u32[]{:S(2)}, u32[]{:S(2)}) %all-to-all-start.2) | async-done | bytes 2097184 | tf_op jit(solution)/shard_map/all_to_all | solution.py:570
  44.2 4.0 %all-to-all-start = ((bf16[32,2,128,128]{3,2,1,0:T(8,128)(2,1)}), bf16[32,2,128,128]{3,2,1,0:T(8,128)(2,1)S(1)}, u32[]{:S(2)}, u32[]{:S(2)}) async-start(bf16[32,2,128,128]{3,2,1,0:T(8,128)(2,1)} %coil_forward_1.1), calls=%async_computation | async-start | bytes 4194304 | tf_op jit(solution)/shard_map/all_to_all | solution.py:570
  48.2 0.0 copy-done.1
  48.2 0.0 copy-done.2
  48.2 0.0 copy-done.5
  48.2 10.8 %grid_tile_0.1 = bf16[32,2,8,16,128]{4,3,2,1,0:T(8,128)(2,1)} custom-call(s32[1,24]{1,0:T(1,128)S(1)} %copy-done.5, s32[1]{0:T(128)S(6)} %copy.21.counts_ref.refs_1_, bf16[32,2,8,16,128]{4,3,2,1,0:T(8,128)(2,1)} %bitcast.9.refs_2_, bf16[512,512]{1,0:T(8,128)(2,1)S(1)} %copy-done.2, bf16[512,512]{1,0:T(8,128)(2,1)S(1)} %bitcast.14, ...), custom_call_target="tpu_custom_call" | custom-call | tf_op jit(solution)/shard_map/grid_tile_0/pallas_call | solution.py:338
  59.0 18.1 %all-to-all-done = bf16[32,2,128,128]{3,2,1,0:T(8,128)(2,1)S(1)} async-done(((bf16[32,2,128,128]{3,2,1,0:T(8,128)(2,1)}), bf16[32,2,128,128]{3,2,1,0:T(8,128)(2,1)S(1)}, u32[]{:S(2)}, u32[]{:S(2)}) %all-to-all-start) | async-done | bytes 2097184 | tf_op jit(solution)/shard_map/all_to_all | solution.py:570
  77.1 0.0 copy-start.7
  77.1 1.3 copy-done.7
  78.4 4.8 %all-to-all-start.3 = ((bf16[32,2,8,16,128]{4,3,2,1,0:T(8,128)(2,1)}), bf16[32,2,8,16,128]{4,3,2,1,0:T(8,128)(2,1)}, u32[]{:S(2)}, u32[]{:S(2)}) async-start(bf16[32,2,8,16,128]{4,3,2,1,0:T(8,128)(2,1)} %grid_tile_0.1), calls=%async_computation.3 | async-start | bytes 4194304 | tf_op jit(solution)/shard_map/all_to_all | solution.py:587
  83.2 10.8 %grid_tile_1.1 = bf16[32,2,8,16,128]{4,3,2,1,0:T(8,128)(2,1)} custom-call(s32[1,24]{1,0:T(1,128)S(1)} %copy-done.5, s32[1]{0:T(128)S(6)} %copy.21.counts_ref.refs_1_, bf16[32,2,8,16,128]{4,3,2,1,0:T(8,128)(2,1)} %bitcast.20, bf16[512,512]{1,0:T(8,128)(2,1)S(1)} %copy-done.2, bf16[512,512]{1,0:T(8,128)(2,1)S(1)} %bitcast.15, bf16[24,128,512]{2,1,0:T(8,128)(2,1)} %bitcast.17, ...), custom_call_target="tpu_custom_call" | custom-call | tf_op jit(solution)/shard_map/grid_tile_1/pallas_call | solution.py:338
  94.0 0.0 copy-start
  94.0 18.1 %all-to-all-done.3 = bf16[32,2,8,16,128]{4,3,2,1,0:T(8,128)(2,1)} async-done(((bf16[32,2,8,16,128]{4,3,2,1,0:T(8,128)(2,1)}), bf16[32,2,8,16,128]{4,3,2,1,0:T(8,128)(2,1)}, u32[]{:S(2)}, u32[]{:S(2)}) %all-to-all-start.3) | async-done | bytes 2097184 | tf_op jit(solution)/shard_map/all_to_all | solution.py:587
  112.0 4.8 %all-to-all-start.1 = ((bf16[32,2,8,16,128]{4,3,2,1,0:T(8,128)(2,1)}), bf16[32,2,8,16,128]{4,3,2,1,0:T(8,128)(2,1)}, u32[]{:S(2)}, u32[]{:S(2)}) async-start(bf16[32,2,8,16,128]{4,3,2,1,0:T(8,128)(2,1)} %grid_tile_1.1), calls=%async_computation.1 | async-start | bytes 4194304 | tf_op jit(solution)/shard_map/all_to_all | solution.py:587
  116.8 0.0 copy-done
  116.8 4.6 %gradient_0.1.refs_3_ = f32[2,8,256,128]{3,2,1,0:T(8,128)S(1)} custom-call(bf16[512,512]{1,0:T(8,128)(2,1)S(1)} %bitcast.12, bf16[32,2,128,128]{3,2,1,0:T(8,128)(2,1)} %bitcast.10.refs_1_, bf16[4,2,8,256,128]{4,3,2,1,0:T(8,128)(2,1)} %refs_2_.7), custom_call_target="tpu_custom_call" | custom-call | tf_op jit(solution)/shard_map/gradient_0/pallas_call | solution.py:442
  121.4 24.3 %all-to-all-done.1 = bf16[32,2,8,16,128]{4,3,2,1,0:T(8,128)(2,1)} async-done(((bf16[32,2,8,16,128]{4,3,2,1,0:T(8,128)(2,1)}), bf16[32,2,8,16,128]{4,3,2,1,0:T(8,128)(2,1)}, u32[]{:S(2)}, u32[]{:S(2)}) %all-to-all-start.1) | async-done | bytes 2097184 | tf_op jit(solution)/shard_map/all_to_all | solution.py:587
  145.7 5.2 %gradient_1.1 = bf16[4,2,8,64,128]{4,3,2,1,0:T(8,128)(2,1)} custom-call(bf16[512,512]{1,0:T(8,128)(2,1)S(1)} %bitcast.13, bf16[32,2,128,128]{3,2,1,0:T(8,128)(2,1)} %bitcast.8.refs_1_, bf16[4,2,8,256,128]{4,3,2,1,0:T(8,128)(2,1)} %refs_2_.7, f32[2,8,256,128]{3,2,1,0:T(8,128)S(1)} %gradient_0.1.refs_3_), custom_call_target="tpu_custom_call" | custom-call | tf_op jit(solution)/shard_map/gradient_1/pallas_call | solution.py:442
  150.9 0.0 copy-start.3
  150.9 0.0 copy-start.4
  151.0 5.5 %all-to-all-start.4 = ((bf16[4,2,8,64,128]{4,3,2,1,0:T(8,128)(2,1)}), bf16[4,2,8,64,128]{4,3,2,1,0:T(8,128)(2,1)S(1)}, u32[]{:S(2)}, u32[]{:S(2)}) async-start(bf16[4,2,8,64,128]{4,3,2,1,0:T(8,128)(2,1)} %gradient_1.1), calls=%async_computation.4 | async-start | bytes 2097152 | tf_op jit(solution)/shard_map/all_to_all | solution.py:592
  156.4 0.0 copy-done.3
  156.4 0.0 copy-done.4
  156.4 1.3 target.1.base_ref
  157.7 13.6 %all-to-all-done.4.pieces_ref = bf16[4,2,8,64,128]{4,3,2,1,0:T(8,128)(2,1)S(1)} async-done(((bf16[4,2,8,64,128]{4,3,2,1,0:T(8,128)(2,1)}), bf16[4,2,8,64,128]{4,3,2,1,0:T(8,128)(2,1)S(1)}, u32[]{:S(2)}, u32[]{:S(2)}) %all-to-all-start.4) | async-done | bytes 1048608 | tf_op jit(solution)/shard_map/all_to_all | solution.py:592
  171.3 1.3 update.1
Async XLA Ops:
  7.7 36.5 %all-to-all-start.2 = ((bf16[32,2,128,128]{3,2,1,0:T(8,128)(2,1)}), bf16[32,2,128,128]{3,2,1,0:T(8,128)(2,1)}, u32[]{:S(2)}, u32[]{:S(2)}) async-start(bf16[32,2,128,128]{3,2,1,0:T(8,128)(2,1)} %coil_forward_0.1), calls=%async_computation.2 | async-start | bytes 4194304 | tf_op jit(solution)/shard_map/all_to_all | solution.py:570
  15.3 7.9 %copy-start.6 = (bf16[1,24,128,512]{3,2,1,0:T(8,128)(2,1)S(1)}, bf16[1,24,128,512]{3,2,1,0:T(8,128)(2,1)}, u32[]{:S(2)}) copy-start(bf16[1,24,128,512]{3,2,1,0:T(8,128)(2,1)} %param.12) | copy-start | bytes 9437188
  28.3 19.9 %copy-start.1 = (bf16[512,512]{0,1:T(8,128)(2,1)S(1)}, bf16[512,512]{0,1:T(8,128)(2,1)}, u32[]{:S(2)}) copy-start(bf16[512,512]{0,1:T(8,128)(2,1)} %constant.11.clone) | copy-start | bytes 1572868
  28.3 19.9 %copy-start.2 = (bf16[512,512]{1,0:T(8,128)(2,1)S(1)}, bf16[512,512]{1,0:T(8,128)(2,1)}, u32[]{:S(2)}) copy-start(bf16[512,512]{1,0:T(8,128)(2,1)} %constant.21.refs_3_) | copy-start | bytes 1572868
  28.3 19.9 %copy-start.5 = (s32[1,24]{1,0:T(1,128)S(1)}, s32[1,24]{1,0:T(1,128)}, u32[]{:S(2)}) copy-start(s32[1,24]{1,0:T(1,128)} %refs_0_.5) | copy-start | bytes 292
  44.2 32.9 %all-to-all-start = ((bf16[32,2,128,128]{3,2,1,0:T(8,128)(2,1)}), bf16[32,2,128,128]{3,2,1,0:T(8,128)(2,1)S(1)}, u32[]{:S(2)}, u32[]{:S(2)}) async-start(bf16[32,2,128,128]{3,2,1,0:T(8,128)(2,1)} %coil_forward_1.1), calls=%async_computation | async-start | bytes 4194304 | tf_op jit(solution)/shard_map/all_to_all | solution.py:570
  77.1 1.3 copy-start.7
  78.4 33.6 %all-to-all-start.3 = ((bf16[32,2,8,16,128]{4,3,2,1,0:T(8,128)(2,1)}), bf16[32,2,8,16,128]{4,3,2,1,0:T(8,128)(2,1)}, u32[]{:S(2)}, u32[]{:S(2)}) async-start(bf16[32,2,8,16,128]{4,3,2,1,0:T(8,128)(2,1)} %grid_tile_0.1), calls=%async_computation.3 | async-start | bytes 4194304 | tf_op jit(solution)/shard_map/all_to_all | solution.py:587
  94.0 22.9 %copy-start = (bf16[512,512]{0,1:T(8,128)(2,1)S(1)}, bf16[512,512]{0,1:T(8,128)(2,1)}, u32[]{:S(2)}) copy-start(bf16[512,512]{0,1:T(8,128)(2,1)} %constant.10.clone) | copy-start | bytes 1572868
  112.0 33.7 %all-to-all-start.1 = ((bf16[32,2,8,16,128]{4,3,2,1,0:T(8,128)(2,1)}), bf16[32,2,8,16,128]{4,3,2,1,0:T(8,128)(2,1)}, u32[]{:S(2)}, u32[]{:S(2)}) async-start(bf16[32,2,8,16,128]{4,3,2,1,0:T(8,128)(2,1)} %grid_tile_1.1), calls=%async_computation.1 | async-start | bytes 4194304 | tf_op jit(solution)/shard_map/all_to_all | solution.py:587
  150.9 5.5 %copy-start.3 = (f32[2,8,64,128]{3,2,1,0:T(8,128)S(1)}, f32[2,8,64,128]{3,2,1,0:T(8,128)}, u32[]{:S(2)}) copy-start(f32[2,8,64,128]{3,2,1,0:T(8,128)} %dual_ref.3) | copy-start | bytes 1572868
  150.9 5.5 %copy-start.4 = (f32[2,8,64,128]{3,2,1,0:T(8,128)S(1)}, f32[2,8,64,128]{3,2,1,0:T(8,128)}, u32[]{:S(2)}) copy-start(f32[2,8,64,128]{3,2,1,0:T(8,128)} %aux_ref.1) | copy-start | bytes 1572868
  151.0 20.4 %all-to-all-start.4 = ((bf16[4,2,8,64,128]{4,3,2,1,0:T(8,128)(2,1)}), bf16[4,2,8,64,128]{4,3,2,1,0:T(8,128)(2,1)S(1)}, u32[]{:S(2)}, u32[]{:S(2)}) async-start(bf16[4,2,8,64,128]{4,3,2,1,0:T(8,128)(2,1)} %gradient_1.1), calls=%async_computation.4 | async-start | bytes 2097152 | tf_op jit(solution)/shard_map/all_to_all | solution.py:592

commit v3 on v2

--- a/solution.py
+++ b/solution.py
@@ -66,66 +66,84 @@
 
 
 def coil_kernel(
-    chunk, table_hbm, sens_hbm, image_hbm, out_hbm, table, sens, image, spread, out, sems, done
+    chunk, table_hbm, sens_hbm, image_hbm, out_hbm, table, sens, image, spread, out, sems, leave
 ):
-    def copies(step):
-        rows = pl.ds(2 * step, 2)
-        return [
-            pltpu.make_async_copy(image_hbm.at[:, rows], image.at[:, rows], sems.at[PER, step])
-        ] + [
-            pltpu.make_async_copy(
-                sens_hbm.at[chunk * PER + c, :, rows], sens.at[c, :, rows], sems.at[c, step]
+    stages = 2
+    span = KYD // stages
+    group = TILES // stages
+
+    def sens_copy(c, stage):
+        rows = pl.ds(stage * span, span)
+        return pltpu.make_async_copy(
+            sens_hbm.at[chunk * PER + c, :, rows], sens.at[c, :, rows], sems.at[c, stage]
+        )
+
+    def image_copy(stage):
+        rows = pl.ds(stage * span, span)
+        return pltpu.make_async_copy(image_hbm.at[:, rows], image.at[:, rows], sems.at[PER, stage])
+
+    def leave_copy(c, stage):
+        tiles = pl.ds(stage * group, group)
+        return pltpu.make_async_copy(out.at[tiles, c], out_hbm.at[tiles, c], leave.at[c, stage])
+
+    whole = pltpu.make_async_copy(table_hbm, table, leave.at[PER, 0])
+    whole.start()
+    for stage in range(stages):
+        image_copy(stage).start()
+        sens_copy(0, stage).start()
+    for c in range(1, PER):
+        for stage in range(stages):
+            sens_copy(c, stage).start()
+    whole.wait()
+
+    def one_coil(c, arrive):
+        for stage in range(stages):
+            arrive(c, stage)
+            for pair in range(span // 2):
+                first = stage * span + 2 * pair
+                parts = []
+                for x in (first, first + 1):
+                    s_re = sens[c, 0, x].astype(F32)
+                    s_im = sens[c, 1, x].astype(F32)
+                    m_re = image[0, x]
+                    m_im = image[1, x]
+                    c_re = (s_re * m_re - s_im * m_im).astype(BF)
+                    c_im = (s_re * m_im + s_im * m_re).astype(BF)
+                    parts.append(jnp.concatenate([c_re, c_im], 0))
+                data = jnp.concatenate(parts, 1)
+                result = jnp.dot(table[...], data, preferred_element_type=F32)
+                for i in range(2):
+                    spread[c, pl.ds(first + i, 2 * N, stride=KYD), :] = result[
+                        :, i * Z : (i + 1) * Z
+                    ]
+        for stage in range(stages):
+            rows = slice(stage * group * 128, (stage + 1) * group * 128)
+            out[stage * group : (stage + 1) * group, c] = (
+                spread[c, rows].astype(BF).reshape(group, 128, Z)
             )
-            for c in range(PER)
-        ]
-
-    whole = pltpu.make_async_copy(table_hbm, table, done.at[PER])
-    whole.start()
-    pending = [copies(step) for step in range(4)]
-    for step in range(4):
-        for copy in pending[step][:2]:
-            copy.start()
-    for step in range(4):
-        for copy in pending[step][2:]:
-            copy.start()
-    whole.wait()
-
-    def leave(c):
-        return pltpu.make_async_copy(out.at[:, c], out_hbm.at[:, c], done.at[c])
-
-    def one_coil(c, carry):
-        for step in range(4):
-
-            @pl.when(c == 0)
-            def _():
-                pending[step][0].wait()
-
-            arrival = pltpu.make_async_copy(
-                sens_hbm.at[chunk * PER + c, :, pl.ds(2 * step, 2)],
-                sens.at[c, :, pl.ds(2 * step, 2)],
-                sems.at[c, step],
-            )
-            arrival.wait()
-            parts = []
-            for x in (2 * step, 2 * step + 1):
-                s_re = sens[c, 0, x].astype(F32)
-                s_im = sens[c, 1, x].astype(F32)
-                m_re = image[0, x]
-                m_im = image[1, x]
-                c_re = (s_re * m_re - s_im * m_im).astype(BF)
-                c_im = (s_re * m_im + s_im * m_re).astype(BF)
-                parts.append(jnp.concatenate([c_re, c_im], 0))
-            data = jnp.concatenate(parts, 1)
-            result = jnp.dot(table[...], data, preferred_element_type=F32)
-            for i in range(2):
-                spread[pl.ds(2 * step + i, 2 * N, stride=KYD), :] = result[:, i * Z : (i + 1) * Z]
-        out[:, c] = spread[...].astype(BF).reshape(TILES, 128, Z)
-        leave(c).start()
-        return carry
-
-    lax.fori_loop(0, PER, one_coil, 0)
+            leave_copy(c, stage).start()
+
+    def arrive_staged(c, stage):
+        if c == 0:
+            image_copy(stage).wait()
+        sens_copy(c, stage).wait()
+
+    if chunk == 0:
+        for c in range(PER):
+            one_coil(c, arrive_staged)
+    else:
+        for stage in range(stages):
+            for c in range(PER):
+                arrive_staged(c, stage)
+
+        def rolled(c, carry):
+            one_coil(c, lambda c, stage: None)
+            return carry
+
+        lax.fori_loop(0, PER, rolled, 0)
     for c in range(PER):
-        leave(c).wait()
+        for stage in range(stages):
+            leave_copy(c, stage).wait()
 
 
 def coil_forward(chunk, table, sensitivity, image):
@@ -141,10 +159,10 @@
             pltpu.VMEM((2 * N, 2 * N), BF),
             pltpu.VMEM((PER, 2, KYD, N, Z), BF),
             pltpu.VMEM((2, KYD, N, Z), F32),
-            pltpu.VMEM((TILES * 128, Z), F32),
+            pltpu.VMEM((PER, TILES * 128, Z), F32),
             pltpu.VMEM((TILES, PER, 128, Z), BF),
-            DMA((PER + 1, 4)),
-            DMA((PER + 1,)),
+            DMA((PER + 1, 2)),
+            DMA((PER + 1, 2)),
         ],
         compiler_params=pltpu.CompilerParams(vmem_limit_bytes=18 << 20),
         name=f"coil_forward_{chunk}",
@@ -225,8 +243,11 @@
     leave,
 ):
     count = counts_ref[0]
-    arrival = pltpu.make_async_copy(piece_hbm, piece, leave.at[PER])
-    arrival.start()
+    if chunk == 0:
+        arrival = pltpu.make_async_copy(piece_hbm, piece, leave.at[PER])
+        arrival.start()
+    else:
+        piece = piece_hbm
 
     def copies(j):
         return [
@@ -248,7 +269,8 @@
 
     lax.fori_loop(0, count, start, 0)
 
-    arrival.wait()
+    if chunk == 0:
+        arrival.wait()
 
     def forward_row(ky, carry):
         data = jnp.concatenate(
@@ -338,10 +360,10 @@
     return pl.pallas_call(
         kernel,
         out_shape=hbm((TILES, PER, KYD, 16, Z), BF),
-        in_specs=[SMEM, SMEM, HBM, VMEM, VMEM, HBM, HBM, HBM],
+        in_specs=[SMEM, SMEM, HBM if chunk == 0 else VMEM, VMEM, VMEM, HBM, HBM, HBM],
         out_specs=HBM,
         scratch_shapes=[
-            pltpu.VMEM((TILES, PER, KYD, 16, Z), BF),
+            pltpu.VMEM((TILES, PER, KYD, 16, Z) if chunk == 0 else (16, Z), BF),
             pltpu.VMEM((CH, P_SIZE, CELLS), BF),
             pltpu.VMEM((CH, CELLS, P_SIZE), BF),
             pltpu.VMEM((CH, P_SIZE, 2 * Z * PER), BF),
@@ -356,105 +378,129 @@
     )(offsets, counts, piece, forward, inverse, blocks, turned, samples)
 
 
-def gradient_kernel(chunk, table_ref, piece_hbm, sens_hbm, *rest):
-    first = chunk == 0
-    last = chunk == NCOIL // PER - 1
-    rest = list(rest)
-    before_ref = None if first else rest.pop(0)
-    out_ref = rest.pop(0)
-    piece, sens, spread, sems, arrive = rest[:5]
-    if last:
-        out, leave = rest[5:]
-    half = TILES // 2
-
-    def sens_copy(step):
-        rows = pl.ds(2 * step, 2)
-        return pltpu.make_async_copy(
-            sens_hbm.at[pl.ds(chunk * PER, PER), :, rows], sens.at[:, :, rows], sems.at[step]
-        )
-
-    def leave_copy(step):
-        rows = pl.ds(2 * step, 2)
-        return pltpu.make_async_copy(out.at[:, :, rows], out_ref.at[:, :, rows], leave.at[step])
-
-    arrivals = []
+def combine(adjoint, sens, x, before):
+    g_re, g_im = before
     for c in range(PER):
-        for h in range(2):
-            tiles = pl.ds(h * half, half)
-            copy = pltpu.make_async_copy(
-                piece_hbm.at[tiles, c], piece.at[tiles, c], arrive.at[c, h]
-            )
-            copy.start()
-            arrivals.append((c, h, copy))
-    for step in range(4):
-        sens_copy(step).start()
-    for c, h, copy in arrivals:
-        copy.wait()
-        spread[c, h * half * 128 : (h + 1) * half * 128, :] = (
-            piece[h * half : (h + 1) * half, c].astype(F32).reshape(half * 128, Z)
-        )
-
-    def rows_pair(step, carry):
-        sens_copy(step).wait()
-        for i in range(2):
-            x = 2 * step + i
-            data = jnp.concatenate(
-                [spread[c, pl.ds(x, 2 * N, stride=KYD), :].astype(BF) for c in range(PER)], 1
-            )
-            result = jnp.dot(table_ref[...], data, preferred_element_type=F32)
-            result = result.astype(BF).astype(F32)
-            g_re = None if first else before_ref[0, x]
-            g_im = None if first else before_ref[1, x]
-            for c in range(PER):
-                lanes = slice(c * Z, (c + 1) * Z)
-                a_re = result[:N, lanes]
-                a_im = result[N:, lanes]
-                s_re = sens[c, 0, x].astype(F32)
-                s_im = sens[c, 1, x].astype(F32)
-                t_re = s_re * a_re + s_im * a_im
-                t_im = s_re * a_im - s_im * a_re
-                g_re = t_re if g_re is None else g_re + t_re
-                g_im = t_im if g_im is None else g_im + t_im
-            if last:
-                out[:, 0, x] = g_re.astype(BF).reshape(NCOIL, N // NCOIL, Z)
-                out[:, 1, x] = g_im.astype(BF).reshape(NCOIL, N // NCOIL, Z)
-            else:
-                out_ref[0, x] = g_re
-                out_ref[1, x] = g_im
-        if last:
-            leave_copy(step).start()
+        lanes = slice(c * Z, (c + 1) * Z)
+        a_re = adjoint[:N, lanes]
+        a_im = adjoint[N:, lanes]
+        s_re = sens[c, 0, x].astype(F32)
+        s_im = sens[c, 1, x].astype(F32)
+        t_re = s_re * a_re + s_im * a_im
+        t_im = s_re * a_im - s_im * a_re
+        g_re = t_re if g_re is None else g_re + t_re
+        g_im = t_im if g_im is None else g_im + t_im
+    return g_re, g_im
+
+
+def adjoint_row(table_ref, spread, x):
+    data = jnp.concatenate(
+        [spread[c, pl.ds(x, 2 * N, stride=KYD), :].astype(BF) for c in range(PER)], 1
+    )
+    return jnp.dot(table_ref[...], data, preferred_element_type=F32).astype(BF).astype(F32)
+
+
+def gradient_first_kernel(table_ref, piece_hbm, sens_hbm, out_ref, piece, sens, spread, sems):
+    copies = [
+        pltpu.make_async_copy(piece_hbm, piece, sems.at[0]),
+        pltpu.make_async_copy(sens_hbm.at[pl.ds(0, PER)], sens, sems.at[1]),
+    ]
+    for copy in copies:
+        copy.start()
+    copies[0].wait()
+    for c in range(PER):
+        spread[c] = piece[:, c].astype(F32).reshape(TILES * 128, Z)
+    copies[1].wait()
+
+    def row(x, carry):
+        g_re, g_im = combine(adjoint_row(table_ref, spread, x), sens, x, (None, None))
+        out_ref[0, x] = g_re
+        out_ref[1, x] = g_im
         return carry
 
-    lax.fori_loop(0, 4, rows_pair, 0)
-    if last:
-        for step in range(4):
-            leave_copy(step).wait()
-
-
-def gradient_step(chunk, table, piece, sensitivity, before):
-    first = chunk == 0
-    last = chunk == NCOIL // PER - 1
-
-    def kernel(*refs):
-        gradient_kernel(chunk, *refs)
-
-    shares = (NCOIL, 2, KYD, N // NCOIL, Z)
+    lax.fori_loop(0, KYD, row, 0)
+
+
+def gradient_first(table, piece, sensitivity):
     return pl.pallas_call(
-        kernel,
-        out_shape=hbm(shares, BF) if last else jax.ShapeDtypeStruct((2, KYD, N, Z), F32),
-        in_specs=[VMEM, HBM, HBM] + ([] if first else [VMEM]),
-        out_specs=HBM if last else VMEM,
+        gradient_first_kernel,
+        out_shape=jax.ShapeDtypeStruct((2, KYD, N, Z), F32),
+        in_specs=[VMEM, HBM, HBM],
+        out_specs=VMEM,
         scratch_shapes=[
             pltpu.VMEM((TILES, PER, 128, Z), BF),
             pltpu.VMEM((PER, 2, KYD, N, Z), BF),
             pltpu.VMEM((PER, TILES * 128, Z), F32),
-            DMA((4,)),
-            DMA((PER, 2)),
-        ]
-        + ([pltpu.VMEM(shares, BF), DMA((4,))] if last else []),
+            DMA((2,)),
+        ],
         compiler_params=pltpu.CompilerParams(vmem_limit_bytes=18 << 20),
-        name=f"gradient_{chunk}",
-    )(*([table, piece, sensitivity] + ([] if first else [before])))
+        name="gradient_first",
+    )(table, piece, sensitivity)
+
+
+def gradient_last_kernel(position_ref, table_ref, piece_hbm, sens_hbm, before_ref, *rest):
+    shares = rest[:NCOIL]
+    piece, sens, spread, out, arrive, sems = rest[NCOIL:]
+    position = position_ref[0]
+    span = KYD // 2
+
+    def sens_copy(stage):
+        rows = pl.ds(stage * span, span)
+        return pltpu.make_async_copy(
+            sens_hbm.at[pl.ds(PER, PER), :, rows], sens.at[:, :, rows], arrive.at[stage]
+        )
+
+    def leave(k, stage):
+        rows = pl.ds(stage * span, span)
+        target = lax.rem(position + k, NCOIL)
+        return pltpu.make_async_copy(
+            out.at[target, :, rows], shares[k].at[:, rows], sems.at[k, stage]
+        )
+
+    arrivals = [
+        pltpu.make_async_copy(piece_hbm.at[:, c], piece.at[:, c], arrive.at[2 + c])
+        for c in range(PER)
+    ]
+    for copy in arrivals:
+        copy.start()
+    for stage in range(2):
+        sens_copy(stage).start()
+    for c in range(PER):
+        arrivals[c].wait()
+        spread[c] = piece[:, c].astype(F32).reshape(TILES * 128, Z)
+    for stage in range(2):
+        sens_copy(stage).wait()
+        for x in range(stage * span, (stage + 1) * span):
+            g_re, g_im = combine(
+                adjoint_row(table_ref, spread, x), sens, x, (before_ref[0, x], before_ref[1, x])
+            )
+            out[:, 0, x] = g_re.astype(BF).reshape(NCOIL, N // NCOIL, Z)
+            out[:, 1, x] = g_im.astype(BF).reshape(NCOIL, N // NCOIL, Z)
+        for k in range(NCOIL):
+            leave(k, stage).start()
+    for stage in range(2):
+        for k in range(NCOIL):
+            leave(k, stage).wait()
+
+
+def gradient_last(position, table, piece, sens, before):
+    share = (2, KYD, N // NCOIL, Z)
+    return pl.pallas_call(
+        gradient_last_kernel,
+        out_shape=(hbm(share, BF),) * NCOIL,
+        in_specs=[SMEM, VMEM, HBM, HBM, VMEM],
+        out_specs=(HBM,) * NCOIL,
+        scratch_shapes=[
+            pltpu.VMEM((TILES, PER, 128, Z), BF),
+            pltpu.VMEM((PER, 2, KYD, N, Z), BF),
+            pltpu.VMEM((PER, TILES * 128, Z), F32),
+            pltpu.VMEM((NCOIL,) + share, BF),
+            DMA((2 + PER,)),
+            DMA((NCOIL, 2)),
+        ],
+        compiler_params=pltpu.CompilerParams(vmem_limit_bytes=16 << 20),
+        name="gradient_last",
+    )(position, table, piece, sens, before)
 
 
 def haar_rows(top, low):
@@ -500,7 +546,7 @@
 
 
 def update_kernel(
-    base_ref, pieces_ref, dual_ref, image_hbm, aux_hbm, dual_hbm, image, aux, dual, sems
+    base_ref, s0, s1, s2, s3, dual_ref, image_hbm, aux_hbm, dual_hbm, image, aux, dual, sems
 ):
     leaving = []
     for m in range(KYD // 2):
@@ -508,9 +554,9 @@
         for part in range(2):
             rows = []
             for x in (2 * m, 2 * m + 1):
-                gradient = pieces_ref[0, part, x].astype(F32)
-                for k in range(1, NCOIL):
-                    gradient = gradient + pieces_ref[k, part, x].astype(F32)
+                gradient = s0[part, x].astype(F32)
+                for share in (s1, s2, s3):
+                    gradient = gradient + share[part, x].astype(F32)
                 value = base_ref[part, x] - step_size * gradient
                 image[part, x] = value
                 rows.append(value)
@@ -534,17 +580,17 @@
         copy.wait()
 
 
-def update_step(base, pieces, scaled_dual):
+def update_step(base, shares, scaled_dual):
     shape = hbm(scaled_dual.shape, F32)
     return pl.pallas_call(
         update_kernel,
         out_shape=(shape, shape, shape),
-        in_specs=[VMEM, VMEM, VMEM],
+        in_specs=[VMEM] * (NCOIL + 2),
         out_specs=(HBM, HBM, HBM),
         scratch_shapes=[pltpu.VMEM(scaled_dual.shape, F32)] * 3 + [DMA((3, KYD // 2))],
         compiler_params=pltpu.CompilerParams(vmem_limit_bytes=8 << 20),
         name="update",
-    )(base, pieces, scaled_dual)
+    )(base, *shares, scaled_dual)
 
 
 def body(image, sensitivity, blocks, samples, offsets, counts, auxiliary, scaled_dual):
@@ -577,7 +623,7 @@
             chunk,
             offsets,
             counts,
-            in_hbm(pieces[chunk]),
+            in_hbm(pieces[chunk]) if chunk == 0 else pieces[chunk],
             x_forward,
             x_inverse,
             in_hbm(blocks[0]),
@@ -585,11 +631,13 @@
             in_hbm(by_coil),
         )
         backs.append(lax.all_to_all(back, "slab", 0, 0, tiled=True))
-    total = None
-    for chunk in chunks:
-        piece = in_hbm(backs[chunk].reshape(TILES, PER, 128, Z))
-        total = gradient_step(chunk, y_inverse, piece, sensitivity, total)
-    shares = lax.all_to_all(total, "coil", 0, 0, tiled=True)
+    first, last = (back.reshape(TILES, PER, 128, Z) for back in backs)
+    before = gradient_first(y_inverse, in_hbm(first), sensitivity)
+    own, *others = gradient_last(position, y_inverse, in_hbm(last), sensitivity, before)
+    shares = [own]
+    for k in (2, 1, 3):
+        ring = [(i, (i + k) % NCOIL) for i in range(NCOIL)]
+        shares.append(lax.ppermute(others[k - 1], "coil", ring))
     return update_step(base, shares, scaled_dual)
 
 

time: 173 us -> 167 us (0.965)
  Pallas kernels: 50.5 us -> 46.4 us
  waiting for transfers between devices: 89.9 us -> 86.4 us
  starting transfers between devices: 26.5 us -> 28.5 us
    all_to_all x1 -> x0, waiting for transfers between devices: 13.6 us -> none  [body(): shares = lax.all_to_all(total, 'coil', 0, 0, tiled=True)]
    ppermute x0 -> x3, waiting for transfers between devices: none -> 8.19 us  [body(): shares.append(lax.ppermute(others[k - 1], 'coil', ring))]
    ppermute x0 -> x3, starting transfers between devices: none -> 7.19 us  [body(): shares.append(lax.ppermute(others[k - 1], 'coil', ring))]
    all_to_all x1 -> x0, starting transfers between devices: 5.45 us -> none  [body(): shares = lax.all_to_all(total, 'coil', 0, 0, tiled=True)]
    pallas_call x2, Pallas kernels: 14.3 us -> 11 us  [coil_forward(): pl.pallas_call(kernel, out_shape=hbm((TILES, PER, 128, Z), BF), in_specs=...]
    all_to_all x2, waiting for transfers between devices: 33.9 us -> 35.7 us  [body(): piece = lax.all_to_all(half, 'slab', 0, 0, tiled=True)]
  transfers between devices with their start and end apart: 5 -> 7, of which waited for: 5 -> 7; matrix products, arithmetic and copies ran while one was open for 2% -> 2% of each run, Pallas kernels for 21% -> 21%
where the time goes in v3:
time: 167 us; the launch traced here: 166 us
  waiting for transfers between devices  86.4 us (52%)
  Pallas kernels  46.4 us (28%)
  starting transfers between devices  28.5 us (17%)
  local copies, waits for them, and re-layouts  2.94 us (2%)
    all_to_all x2, waiting for transfers between devices, body(): backs.append(lax.all_to_all(back, 'slab', 0, 0, tiled=True))  42.6 us
    all_to_all x2, waiting for transfers between devices, body(): piece = lax.all_to_all(half, 'slab', 0, 0, tiled=True)  35.7 us
    pallas_call x2, Pallas kernels, grid_tile(): pl.pallas_call(kernel, out_shape=hbm((TILES, PER, KYD, 16, Z), BF), in_sp...  20 us
    all_to_all x2, starting transfers between devices, body(): piece = lax.all_to_all(half, 'slab', 0, 0, tiled=True)  11.6 us
    pallas_call x2, Pallas kernels, coil_forward(): pl.pallas_call(kernel, out_shape=hbm((TILES, PER, 128, Z), BF), in_specs=...  11 us
    all_to_all x2, starting transfers between devices, body(): backs.append(lax.all_to_all(back, 'slab', 0, 0, tiled=True))  9.71 us
    ppermute x3, waiting for transfers between devices, body(): shares.append(lax.ppermute(others[k - 1], 'coil', ring))  8.19 us
    ppermute x3, starting transfers between devices, body(): shares.append(lax.ppermute(others[k - 1], 'coil', ring))  7.19 us
  transfers between devices with their start and end apart: 7, of which 7 were waited for; matrix products, arithmetic and copies ran while one was open for 2% of the time, Pallas kernels for 21%

profile of v3, /device:TPU:0, one launch (start us, length us, event | category | flops | bytes accessed | tf_op | source)
XLA Modules:
  0.0 165.9 jit_solution(7549429021385775178)
XLA Ops:
  0.6 5.6 %coil_forward_0.1 = bf16[32,2,128,128]{3,2,1,0:T(8,128)(2,1)} custom-call(bf16[512,512]{1,0:T(8,128)(2,1)} %constant.20.refs_0_, bf16[4,2,8,256,128]{4,3,2,1,0:T(8,128)(2,1)} %sens_hbm.3, f32[2,8,256,128]{3,2,1,0:T(8,128)} %refs_2_.3), custom_call_target="tpu_custom_call" | custom-call | tf_op jit(solution)/shard_map/coil_forward_0/pallas_call | solution.py:153
  6.2 7.5 %all-to-all-start.2 = ((bf16[32,2,128,128]{3,2,1,0:T(8,128)(2,1)}), bf16[32,2,128,128]{3,2,1,0:T(8,128)(2,1)}, u32[]{:S(2)}, u32[]{:S(2)}) async-start(bf16[32,2,128,128]{3,2,1,0:T(8,128)(2,1)} %coil_forward_0.1), calls=%async_computation.2 | async-start | bytes 4194304 | tf_op jit(solution)/shard_map/all_to_all | solution.py:616
  13.8 0.0 copy-start.7
  13.8 5.4 %coil_forward_1.1 = bf16[32,2,128,128]{3,2,1,0:T(8,128)(2,1)} custom-call(bf16[512,512]{1,0:T(8,128)(2,1)} %constant.20.refs_0_, bf16[4,2,8,256,128]{4,3,2,1,0:T(8,128)(2,1)} %sens_hbm.3, f32[2,8,256,128]{3,2,1,0:T(8,128)} %refs_2_.3), custom_call_target="tpu_custom_call" | custom-call | tf_op jit(solution)/shard_map/coil_forward_1/pallas_call | solution.py:153
  19.9 0.0 copy-done.7
  19.9 2.9 %copy.14 = bf16[1,24,128,512]{2,3,1,0:T(8,128)(2,1)} copy(bf16[1,24,128,512]{3,2,1,0:T(8,128)(2,1)S(1)} %copy-done.7) | data formatting | bytes 6291456 | tf_op args[2]
  22.8 2.3 %samples_by_coil.1.refs_7_ = bf16[4,24,128,256]{3,2,1,0:T(8,128)(2,1)} custom-call(s32[1]{0:T(128)S(6)} %copy.21.counts_ref.refs_1_, bf16[24,128,8,128]{3,2,1,0:T(8,128)(2,1)} %bitcast.21), custom_call_target="tpu_custom_call" | custom-call | tf_op jit(solution)/shard_map/samples_by_coil/pallas_call | solution.py:207
  25.0 0.0 copy-start.1
  25.0 0.0 copy-start.2
  25.0 0.0 copy-start.6
  25.1 17.6 %all-to-all-done.2 = bf16[32,2,128,128]{3,2,1,0:T(8,128)(2,1)} async-done(((bf16[32,2,128,128]{3,2,1,0:T(8,128)(2,1)}), bf16[32,2,128,128]{3,2,1,0:T(8,128)(2,1)}, u32[]{:S(2)}, u32[]{:S(2)}) %all-to-all-start.2) | async-done | bytes 2097184 | tf_op jit(solution)/shard_map/all_to_all | solution.py:616
  42.7 4.0 %all-to-all-start = ((bf16[32,2,128,128]{3,2,1,0:T(8,128)(2,1)}), bf16[32,2,128,128]{3,2,1,0:T(8,128)(2,1)S(1)}, u32[]{:S(2)}, u32[]{:S(2)}) async-start(bf16[32,2,128,128]{3,2,1,0:T(8,128)(2,1)} %coil_forward_1.1), calls=%async_computation | async-start | bytes 4194304 | tf_op jit(solution)/shard_map/all_to_all | solution.py:616
  46.7 0.0 copy-done.1
  46.7 0.0 copy-done.2
  46.7 0.0 copy-done.6
  46.7 10.8 %grid_tile_0.1 = bf16[32,2,8,16,128]{4,3,2,1,0:T(8,128)(2,1)} custom-call(s32[1,24]{1,0:T(1,128)S(1)} %copy-done.6, s32[1]{0:T(128)S(6)} %copy.21.counts_ref.refs_1_, bf16[32,2,8,16,128]{4,3,2,1,0:T(8,128)(2,1)} %bitcast.9.refs_2_, bf16[512,512]{1,0:T(8,128)(2,1)S(1)} %copy-done.2, bf16[512,512]{1,0:T(8,128)(2,1)S(1)} %bitcast.15, ...), custom_call_target="tpu_custom_call" | custom-call | tf_op jit(solution)/shard_map/grid_tile_0/pallas_call | solution.py:360
  57.5 18.1 %all-to-all-done = bf16[32,2,128,128]{3,2,1,0:T(8,128)(2,1)S(1)} async-done(((bf16[32,2,128,128]{3,2,1,0:T(8,128)(2,1)}), bf16[32,2,128,128]{3,2,1,0:T(8,128)(2,1)S(1)}, u32[]{:S(2)}, u32[]{:S(2)}) %all-to-all-start) | async-done | bytes 2097184 | tf_op jit(solution)/shard_map/all_to_all | solution.py:616
  75.6 4.8 %all-to-all-start.3 = ((bf16[32,2,8,16,128]{4,3,2,1,0:T(8,128)(2,1)}), bf16[32,2,8,16,128]{4,3,2,1,0:T(8,128)(2,1)}, u32[]{:S(2)}, u32[]{:S(2)}) async-start(bf16[32,2,8,16,128]{4,3,2,1,0:T(8,128)(2,1)} %grid_tile_0.1), calls=%async_computation.3 | async-start | bytes 4194304 | tf_op jit(solution)/shard_map/all_to_all | solution.py:633
  80.3 9.3 %grid_tile_1.1 = bf16[32,2,8,16,128]{4,3,2,1,0:T(8,128)(2,1)} custom-call(s32[1,24]{1,0:T(1,128)S(1)} %copy-done.6, s32[1]{0:T(128)S(6)} %copy.21.counts_ref.refs_1_, bf16[32,2,8,16,128]{4,3,2,1,0:T(8,128)(2,1)S(1)} %bitcast.12, bf16[512,512]{1,0:T(8,128)(2,1)S(1)} %copy-done.2, bf16[512,512]{1,0:T(8,128)(2,1)S(1)} %bitcast.16, ...), custom_call_target="tpu_custom_call" | custom-call | tf_op jit(solution)/shard_map/grid_tile_1/pallas_call | solution.py:360
  89.6 0.0 copy-start
  89.6 19.6 %all-to-all-done.3 = bf16[32,2,8,16,128]{4,3,2,1,0:T(8,128)(2,1)} async-done(((bf16[32,2,8,16,128]{4,3,2,1,0:T(8,128)(2,1)}), bf16[32,2,8,16,128]{4,3,2,1,0:T(8,128)(2,1)}, u32[]{:S(2)}, u32[]{:S(2)}) %all-to-all-start.3) | async-done | bytes 2097184 | tf_op jit(solution)/shard_map/all_to_all | solution.py:633
  109.2 5.0 %all-to-all-start.1 = ((bf16[32,2,8,16,128]{4,3,2,1,0:T(8,128)(2,1)}), bf16[32,2,8,16,128]{4,3,2,1,0:T(8,128)(2,1)}, u32[]{:S(2)}, u32[]{:S(2)}) async-start(bf16[32,2,8,16,128]{4,3,2,1,0:T(8,128)(2,1)} %grid_tile_1.1), calls=%async_computation.1 | async-start | bytes 4194304 | tf_op jit(solution)/shard_map/all_to_all | solution.py:633
  114.2 0.0 copy-done
  114.2 5.7 %gradient_first.1.before_ref = f32[2,8,256,128]{3,2,1,0:T(8,128)S(1)} custom-call(bf16[512,512]{1,0:T(8,128)(2,1)S(1)} %bitcast.13, bf16[32,2,128,128]{3,2,1,0:T(8,128)(2,1)} %bitcast.10.piece_hbm, bf16[4,2,8,256,128]{4,3,2,1,0:T(8,128)(2,1)} %sens_hbm.3), custom_call_target="tpu_custom_call" | custom-call | tf_op jit(solution)/shard_map/gradient_first/pallas_call | solution.py:425
  119.9 23.0 %all-to-all-done.1 = bf16[32,2,8,16,128]{4,3,2,1,0:T(8,128)(2,1)} async-done(((bf16[32,2,8,16,128]{4,3,2,1,0:T(8,128)(2,1)}), bf16[32,2,8,16,128]{4,3,2,1,0:T(8,128)(2,1)}, u32[]{:S(2)}, u32[]{:S(2)}) %all-to-all-start.1) | async-done | bytes 2097184 | tf_op jit(solution)/shard_map/all_to_all | solution.py:633
  142.9 0.0 copy-start.3
  142.9 0.0 copy-start.4
  142.9 4.9 %gradient_last.1 = (bf16[2,8,64,128]{3,2,1,0:T(8,128)(2,1)}, bf16[2,8,64,128]{3,2,1,0:T(8,128)(2,1)}, bf16[2,8,64,128]{3,2,1,0:T(8,128)(2,1)}, bf16[2,8,64,128]{3,2,1,0:T(8,128)(2,1)}) custom-call(s32[1]{0:T(128)} %bitcast.position_ref, bf16[512,512]{1,0:T(8,128)(2,1)S(1)} %bitcast.14, bf16[32,2,128,128]{3,2,1,0:T(8,128)(2,1)} %bitcast.8.piece_hbm, ...), custom_call_target="tpu_custom_call" | custom-call | tf_op jit(solution)/shard_map/gradient_last/pallas_call | solution.py:488
  147.7 0.0 copy-start.5
  147.7 4.0 %collective-permute-start = (bf16[2,8,64,128]{3,2,1,0:T(8,128)(2,1)}, bf16[2,8,64,128]{3,2,1,0:T(8,128)(2,1)S(1)}, u32[]{:S(2)}, u32[]{:S(2)}) collective-permute-start(bf16[2,8,64,128]{3,2,1,0:T(8,128)(2,1)} %get-tuple-element.22), channel_id=1, source_target_pairs={{0,64},{32,96},{64,0},{96,32},{1,65},{33,97},{65,1},{97,33},{2,66}... | collective-permute-start | bytes 786440 | tf_op jit(solution)/shard_map/ppermute | solution.py:640
  151.7 1.0 collective-permute-start.1
  152.7 2.2 %collective-permute-start.2 = (bf16[2,8,64,128]{3,2,1,0:T(8,128)(2,1)}, bf16[2,8,64,128]{3,2,1,0:T(8,128)(2,1)S(1)}, u32[]{:S(2)}, u32[]{:S(2)}) collective-permute-start(bf16[2,8,64,128]{3,2,1,0:T(8,128)(2,1)} %get-tuple-element.24), channel_id=1, source_target_pairs={{0,96},{32,0},{64,32},{96,64},{1,97},{33,1},{65,33},{97,65},{2,98}... | collective-permute-start | bytes 786440 | tf_op jit(solution)/shard_map/ppermute | solution.py:640
  154.9 0.0 copy-done.3
  154.9 0.0 copy-done.4
  154.9 1.3 target.1.base_ref
  156.2 2.9 %collective-permute-done.s1 = bf16[2,8,64,128]{3,2,1,0:T(8,128)(2,1)S(1)} collective-permute-done((bf16[2,8,64,128]{3,2,1,0:T(8,128)(2,1)}, bf16[2,8,64,128]{3,2,1,0:T(8,128)(2,1)S(1)}, u32[]{:S(2)}, u32[]{:S(2)}) %collective-permute-start) | collective-permute-done | bytes 262176 | tf_op jit(solution)/shard_map/ppermute | solution.py:640
  159.1 4.5 %collective-permute-done.1.s2 = bf16[2,8,64,128]{3,2,1,0:T(8,128)(2,1)S(1)} collective-permute-done((bf16[2,8,64,128]{3,2,1,0:T(8,128)(2,1)}, bf16[2,8,64,128]{3,2,1,0:T(8,128)(2,1)S(1)}, u32[]{:S(2)}, u32[]{:S(2)}) %collective-permute-start.1) | collective-permute-done | bytes 262176 | tf_op jit(solution)/shard_map/ppermute | solution.py:640
  163.6 0.8 collective-permute-done.2.s3
  164.4 0.0 copy-done.5
  164.4 1.3 update.1
Async XLA Ops:
  6.2 36.5 %all-to-all-start.2 = ((bf16[32,2,128,128]{3,2,1,0:T(8,128)(2,1)}), bf16[32,2,128,128]{3,2,1,0:T(8,128)(2,1)}, u32[]{:S(2)}, u32[]{:S(2)}) async-start(bf16[32,2,128,128]{3,2,1,0:T(8,128)(2,1)} %coil_forward_0.1), calls=%async_computation.2 | async-start | bytes 4194304 | tf_op jit(solution)/shard_map/all_to_all | solution.py:616
  13.8 6.1 %copy-start.7 = (bf16[1,24,128,512]{3,2,1,0:T(8,128)(2,1)S(1)}, bf16[1,24,128,512]{3,2,1,0:T(8,128)(2,1)}, u32[]{:S(2)}) copy-start(bf16[1,24,128,512]{3,2,1,0:T(8,128)(2,1)} %param.12) | copy-start | bytes 9437188
  25.0 21.7 %copy-start.1 = (bf16[512,512]{0,1:T(8,128)(2,1)S(1)}, bf16[512,512]{0,1:T(8,128)(2,1)}, u32[]{:S(2)}) copy-start(bf16[512,512]{0,1:T(8,128)(2,1)} %constant.11.clone) | copy-start | bytes 1572868
  25.0 21.7 %copy-start.2 = (bf16[512,512]{1,0:T(8,128)(2,1)S(1)}, bf16[512,512]{1,0:T(8,128)(2,1)}, u32[]{:S(2)}) copy-start(bf16[512,512]{1,0:T(8,128)(2,1)} %constant.21.refs_3_) | copy-start | bytes 1572868
  25.0 21.7 %copy-start.6 = (s32[1,24]{1,0:T(1,128)S(1)}, s32[1,24]{1,0:T(1,128)}, u32[]{:S(2)}) copy-start(s32[1,24]{1,0:T(1,128)} %refs_0_.5) | copy-start | bytes 292
  42.7 32.9 %all-to-all-start = ((bf16[32,2,128,128]{3,2,1,0:T(8,128)(2,1)}), bf16[32,2,128,128]{3,2,1,0:T(8,128)(2,1)S(1)}, u32[]{:S(2)}, u32[]{:S(2)}) async-start(bf16[32,2,128,128]{3,2,1,0:T(8,128)(2,1)} %coil_forward_1.1), calls=%async_computation | async-start | bytes 4194304 | tf_op jit(solution)/shard_map/all_to_all | solution.py:616
  75.6 33.6 %all-to-all-start.3 = ((bf16[32,2,8,16,128]{4,3,2,1,0:T(8,128)(2,1)}), bf16[32,2,8,16,128]{4,3,2,1,0:T(8,128)(2,1)}, u32[]{:S(2)}, u32[]{:S(2)}) async-start(bf16[32,2,8,16,128]{4,3,2,1,0:T(8,128)(2,1)} %grid_tile_0.1), calls=%async_computation.3 | async-start | bytes 4194304 | tf_op jit(solution)/shard_map/all_to_all | solution.py:633
  89.6 24.6 %copy-start = (bf16[512,512]{0,1:T(8,128)(2,1)S(1)}, bf16[512,512]{0,1:T(8,128)(2,1)}, u32[]{:S(2)}) copy-start(bf16[512,512]{0,1:T(8,128)(2,1)} %constant.10.clone) | copy-start | bytes 1572868
  109.2 33.7 %all-to-all-start.1 = ((bf16[32,2,8,16,128]{4,3,2,1,0:T(8,128)(2,1)}), bf16[32,2,8,16,128]{4,3,2,1,0:T(8,128)(2,1)}, u32[]{:S(2)}, u32[]{:S(2)}) async-start(bf16[32,2,8,16,128]{4,3,2,1,0:T(8,128)(2,1)} %grid_tile_1.1), calls=%async_computation.1 | async-start | bytes 4194304 | tf_op jit(solution)/shard_map/all_to_all | solution.py:633
  142.9 12.1 %copy-start.3 = (f32[2,8,64,128]{3,2,1,0:T(8,128)S(1)}, f32[2,8,64,128]{3,2,1,0:T(8,128)}, u32[]{:S(2)}) copy-start(f32[2,8,64,128]{3,2,1,0:T(8,128)} %dual_ref.3) | copy-start | bytes 1572868
  142.9 12.1 %copy-start.4 = (f32[2,8,64,128]{3,2,1,0:T(8,128)S(1)}, f32[2,8,64,128]{3,2,1,0:T(8,128)}, u32[]{:S(2)}) copy-start(f32[2,8,64,128]{3,2,1,0:T(8,128)} %aux_ref.1) | copy-start | bytes 1572868
  147.7 16.7 %copy-start.5 = (bf16[2,8,64,128]{3,2,1,0:T(8,128)(2,1)S(1)}, bf16[2,8,64,128]{3,2,1,0:T(8,128)(2,1)}, u32[]{:S(2)}) copy-start(bf16[2,8,64,128]{3,2,1,0:T(8,128)(2,1)} %get-tuple-element.21.s0) | copy-start | bytes 786436
  147.7 11.4 %collective-permute-start = (bf16[2,8,64,128]{3,2,1,0:T(8,128)(2,1)}, bf16[2,8,64,128]{3,2,1,0:T(8,128)(2,1)S(1)}, u32[]{:S(2)}, u32[]{:S(2)}) collective-permute-start(bf16[2,8,64,128]{3,2,1,0:T(8,128)(2,1)} %get-tuple-element.22), channel_id=1, source_target_pairs={{0,64},{32,96},{64,0},{96,32},{1,65},{33,97},{65,1},{97,33},{2,66}... | collective-permute-start | bytes 786440 | tf_op jit(solution)/shard_map/ppermute | solution.py:640
  151.7 11.9 %collective-permute-start.1 = (bf16[2,8,64,128]{3,2,1,0:T(8,128)(2,1)}, bf16[2,8,64,128]{3,2,1,0:T(8,128)(2,1)S(1)}, u32[]{:S(2)}, u32[]{:S(2)}) collective-permute-start(bf16[2,8,64,128]{3,2,1,0:T(8,128)(2,1)} %get-tuple-element.23), channel_id=1, source_target_pairs={{0,32},{32,64},{64,96},{96,0},{1,33},{33,65},{65,97},{97,1},{2,34}... | collective-permute-start | bytes 786440 | tf_op jit(solution)/shard_map/ppermute | solution.py:640
  152.7 11.7 %collective-permute-start.2 = (bf16[2,8,64,128]{3,2,1,0:T(8,128)(2,1)}, bf16[2,8,64,128]{3,2,1,0:T(8,128)(2,1)S(1)}, u32[]{:S(2)}, u32[]{:S(2)}) collective-permute-start(bf16[2,8,64,128]{3,2,1,0:T(8,128)(2,1)} %get-tuple-element.24), channel_id=1, source_target_pairs={{0,96},{32,0},{64,32},{96,64},{1,97},{33,1},{65,33},{97,65},{2,98}... | collective-permute-start | bytes 786440 | tf_op jit(solution)/shard_map/ppermute | solution.py:640

commit v4 on v3

--- a/solution.py
+++ b/solution.py
@@ -43,11 +43,7 @@
     along_y = np.stack(
         [np.concatenate([re, -im], 1), np.concatenate([im, re], 1)], 1
     ).reshape(2 * N, 2 * N)
-    re_c = re.reshape(N, TILES, KYD)
-    im_c = im.reshape(N, TILES, KYD)
-    along_x = np.stack(
-        [np.stack([re_c, -im_c], 2), np.stack([im_c, re_c], 2)], 0
-    ).reshape(2 * N, 2 * N)
+    along_x = np.concatenate([np.concatenate([re, -im], 1), np.concatenate([im, re], 1)], 0)
     return along_y, along_x
 
 
@@ -65,12 +61,9 @@
 DMA = pltpu.SemaphoreType.DMA
 
 
-def coil_kernel(
-    chunk, table_hbm, sens_hbm, image_hbm, out_hbm, table, sens, image, spread, out, sems, leave
-):
+def coil_kernel(chunk, table_hbm, sens_hbm, image_hbm, out_hbm, table, sens, image, out, sems, leave):
     stages = 2
     span = KYD // stages
-    group = TILES // stages
 
     def sens_copy(c, stage):
         rows = pl.ds(stage * span, span)
@@ -83,8 +76,8 @@
         return pltpu.make_async_copy(image_hbm.at[:, rows], image.at[:, rows], sems.at[PER, stage])
 
     def leave_copy(c, stage):
-        tiles = pl.ds(stage * group, group)
-        return pltpu.make_async_copy(out.at[tiles, c], out_hbm.at[tiles, c], leave.at[c, stage])
+        rows = pl.ds(stage * span, span)
+        return pltpu.make_async_copy(out.at[:, c, rows], out_hbm.at[:, c, rows], leave.at[c, stage])
 
     whole = pltpu.make_async_copy(table_hbm, table, leave.at[PER, 0])
     whole.start()
@@ -111,16 +104,9 @@
                     c_im = (s_re * m_im + s_im * m_re).astype(BF)
                     parts.append(jnp.concatenate([c_re, c_im], 0))
                 data = jnp.concatenate(parts, 1)
-                result = jnp.dot(table[...], data, preferred_element_type=F32)
+                result = jnp.dot(table[...], data, preferred_element_type=F32).astype(BF)
                 for i in range(2):
-                    spread[c, pl.ds(first + i, 2 * N, stride=KYD), :] = result[
-                        :, i * Z : (i + 1) * Z
-                    ]
-        for stage in range(stages):
-            rows = slice(stage * group * 128, (stage + 1) * group * 128)
-            out[stage * group : (stage + 1) * group, c] = (
-                spread[c, rows].astype(BF).reshape(group, 128, Z)
-            )
+                    out[:, c, first + i] = result[:, i * Z : (i + 1) * Z].reshape(TILES, 16, Z)
             leave_copy(c, stage).start()
 
     def arrive_staged(c, stage):
@@ -152,19 +138,18 @@
 
     return pl.pallas_call(
         kernel,
-        out_shape=hbm((TILES, PER, 128, Z), BF),
+        out_shape=hbm((TILES, PER, KYD, 16, Z), BF),
         in_specs=[HBM, HBM, HBM],
         out_specs=HBM,
         scratch_shapes=[
             pltpu.VMEM((2 * N, 2 * N), BF),
             pltpu.VMEM((PER, 2, KYD, N, Z), BF),
             pltpu.VMEM((2, KYD, N, Z), F32),
-            pltpu.VMEM((PER, TILES * 128, Z), F32),
-            pltpu.VMEM((TILES, PER, 128, Z), BF),
+            pltpu.VMEM((TILES, PER, KYD, 16, Z), BF),
             DMA((PER + 1, 2)),
             DMA((PER + 1, 2)),
         ],
-        compiler_params=pltpu.CompilerParams(vmem_limit_bytes=18 << 20),
+        compiler_params=pltpu.CompilerParams(vmem_limit_bytes=14 << 20),
         name=f"coil_forward_{chunk}",
     )(table, sensitivity, image)
 
@@ -238,6 +223,7 @@
     samples,
     window,
     total,
+    spread,
     out,
     sems,
     leave,
@@ -272,9 +258,22 @@
     if chunk == 0:
         arrival.wait()
 
+    for c in range(PER):
+        spread[c] = piece[:, c].astype(F32).reshape(ROWS * 2, Z)
+
     def forward_row(ky, carry):
         data = jnp.concatenate(
-            [piece[:, c, ky].reshape(2 * N, Z) for c in range(PER)], 1
+            [
+                jnp.concatenate(
+                    [
+                        spread[c, pl.ds(2 * ky + part, N, stride=2 * KYD), :].astype(BF)
+                        for part in range(2)
+                    ],
+                    0,
+                )
+                for c in range(PER)
+            ],
+            1,
         )
         result = jnp.dot(forward_ref[...], data, preferred_element_type=F32)
         for c in range(PER):
@@ -340,12 +339,16 @@
                 ],
                 1,
             )
-            result = jnp.dot(inverse_ref[...], data, preferred_element_type=F32).astype(BF)
+            result = jnp.dot(inverse_ref[...], data, preferred_element_type=F32)
             for i in range(2):
-                out[:, c, 2 * pair + i] = result[:, i * Z : (i + 1) * Z].reshape(TILES, 16, Z)
+                for part in range(2):
+                    spread[c, pl.ds(2 * (2 * pair + i) + part, N, stride=2 * KYD), :] = result[
+                        part * N : (part + 1) * N, i * Z : (i + 1) * Z
+                    ]
             return carry
 
         lax.fori_loop(0, KYD // 2, inverse_rows, 0)
+        out[:, c] = spread[c].astype(BF).reshape(TILES, KYD, 16, Z)
         copy = pltpu.make_async_copy(out.at[:, c], out_hbm.at[:, c], leave.at[c])
         copy.start()
         leaving.append(copy)
@@ -369,11 +372,12 @@
             pltpu.VMEM((CH, P_SIZE, 2 * Z * PER), BF),
             pltpu.VMEM((2, ROWS, 2 * Z * PER), BF),
             pltpu.VMEM((2 * PER, ROWS + KYD, Z), F32),
+            pltpu.VMEM((PER, 2 * ROWS, Z), F32),
             pltpu.VMEM((TILES, PER, KYD, 16, Z), BF),
             DMA((2 + PER, CH)),
             DMA((PER + 1,)),
         ],
-        compiler_params=pltpu.CompilerParams(vmem_limit_bytes=30 << 20),
+        compiler_params=pltpu.CompilerParams(vmem_limit_bytes=34 << 20),
         name=f"grid_tile_{chunk}",
     )(offsets, counts, piece, forward, inverse, blocks, turned, samples)
 
@@ -393,27 +397,23 @@
     return g_re, g_im
 
 
-def adjoint_row(table_ref, spread, x):
-    data = jnp.concatenate(
-        [spread[c, pl.ds(x, 2 * N, stride=KYD), :].astype(BF) for c in range(PER)], 1
-    )
+def adjoint_row(table_ref, piece, x):
+    data = jnp.concatenate([piece[:, c, x].reshape(2 * N, Z) for c in range(PER)], 1)
     return jnp.dot(table_ref[...], data, preferred_element_type=F32).astype(BF).astype(F32)
 
 
-def gradient_first_kernel(table_ref, piece_hbm, sens_hbm, out_ref, piece, sens, spread, sems):
+def gradient_first_kernel(table_ref, piece_hbm, sens_hbm, out_ref, piece, sens, sems):
     copies = [
         pltpu.make_async_copy(piece_hbm, piece, sems.at[0]),
         pltpu.make_async_copy(sens_hbm.at[pl.ds(0, PER)], sens, sems.at[1]),
     ]
     for copy in copies:
         copy.start()
-    copies[0].wait()
-    for c in range(PER):
-        spread[c] = piece[:, c].astype(F32).reshape(TILES * 128, Z)
-    copies[1].wait()
+    for copy in copies:
+        copy.wait()
 
     def row(x, carry):
-        g_re, g_im = combine(adjoint_row(table_ref, spread, x), sens, x, (None, None))
+        g_re, g_im = combine(adjoint_row(table_ref, piece, x), sens, x, (None, None))
         out_ref[0, x] = g_re
         out_ref[1, x] = g_im
         return carry
@@ -428,79 +428,105 @@
         in_specs=[VMEM, HBM, HBM],
         out_specs=VMEM,
         scratch_shapes=[
-            pltpu.VMEM((TILES, PER, 128, Z), BF),
+            pltpu.VMEM((TILES, PER, KYD, 16, Z), BF),
             pltpu.VMEM((PER, 2, KYD, N, Z), BF),
-            pltpu.VMEM((PER, TILES * 128, Z), F32),
             DMA((2,)),
         ],
-        compiler_params=pltpu.CompilerParams(vmem_limit_bytes=18 << 20),
+        compiler_params=pltpu.CompilerParams(vmem_limit_bytes=12 << 20),
         name="gradient_first",
     )(table, piece, sensitivity)
 
 
 def gradient_last_kernel(position_ref, table_ref, piece_hbm, sens_hbm, before_ref, *rest):
-    shares = rest[:NCOIL]
-    piece, sens, spread, out, arrive, sems = rest[NCOIL:]
-    position = position_ref[0]
+    near_send, far_send, mine, near_keep, far_keep = rest[:5]
+    piece, sens, out, arrive, sems = rest[5:]
+    me = position_ref[0]
+    near = me + 1 - 2 * lax.rem(me, 2)
+    far = NCOIL - 1 - me
+    across = NCOIL - 1 - near
     span = KYD // 2
 
-    def sens_copy(stage):
+    def arrivals(stage):
         rows = pl.ds(stage * span, span)
-        return pltpu.make_async_copy(
-            sens_hbm.at[pl.ds(PER, PER), :, rows], sens.at[:, :, rows], arrive.at[stage]
+        return (
+            pltpu.make_async_copy(
+                piece_hbm.at[:, :, rows], piece.at[:, :, rows], arrive.at[0, stage]
+            ),
+            pltpu.make_async_copy(
+                sens_hbm.at[pl.ds(PER, PER), :, rows], sens.at[:, :, rows], arrive.at[1, stage]
+            ),
         )
 
-    def leave(k, stage):
+    def departures(stage):
         rows = pl.ds(stage * span, span)
-        target = lax.rem(position + k, NCOIL)
-        return pltpu.make_async_copy(
-            out.at[target, :, rows], shares[k].at[:, rows], sems.at[k, stage]
+        first, keep = ((near, far), (far, near))[stage]
+        send, kept = ((near_send, near_keep), (far_send, far_keep))[stage]
+        pairs = (
+            (first, send.at[0]),
+            (across, send.at[1]),
+            (keep, kept),
+            (me, mine.at[:, rows]),
         )
-
-    arrivals = [
-        pltpu.make_async_copy(piece_hbm.at[:, c], piece.at[:, c], arrive.at[2 + c])
-        for c in range(PER)
-    ]
-    for copy in arrivals:
-        copy.start()
+        return [
+            pltpu.make_async_copy(out.at[target, :, rows], place, sems.at[stage, k])
+            for k, (target, place) in enumerate(pairs)
+        ]
+
     for stage in range(2):
-        sens_copy(stage).start()
-    for c in range(PER):
-        arrivals[c].wait()
-        spread[c] = piece[:, c].astype(F32).reshape(TILES * 128, Z)
+        for copy in arrivals(stage):
+            copy.start()
+    leaving = []
     for stage in range(2):
-        sens_copy(stage).wait()
+        for copy in arrivals(stage):
+            copy.wait()
         for x in range(stage * span, (stage + 1) * span):
             g_re, g_im = combine(
-                adjoint_row(table_ref, spread, x), sens, x, (before_ref[0, x], before_ref[1, x])
+                adjoint_row(table_ref, piece, x), sens, x, (before_ref[0, x], before_ref[1, x])
             )
             out[:, 0, x] = g_re.astype(BF).reshape(NCOIL, N // NCOIL, Z)
             out[:, 1, x] = g_im.astype(BF).reshape(NCOIL, N // NCOIL, Z)
-        for k in range(NCOIL):
-            leave(k, stage).start()
-    for stage in range(2):
-        for k in range(NCOIL):
-            leave(k, stage).wait()
+        for copy in departures(stage):
+            copy.start()
+            leaving.append(copy)
+    for copy in leaving:
+        copy.wait()
 
 
 def gradient_last(position, table, piece, sens, before):
     share = (2, KYD, N // NCOIL, Z)
+    half = (2, KYD // 2, N // NCOIL, Z)
+    shapes = ((2,) + half, (2,) + half, share, half, half)
     return pl.pallas_call(
         gradient_last_kernel,
-        out_shape=(hbm(share, BF),) * NCOIL,
+        out_shape=tuple(hbm(shape, BF) for shape in shapes),
         in_specs=[SMEM, VMEM, HBM, HBM, VMEM],
-        out_specs=(HBM,) * NCOIL,
+        out_specs=(HBM,) * 5,
         scratch_shapes=[
-            pltpu.VMEM((TILES, PER, 128, Z), BF),
+            pltpu.VMEM((TILES, PER, KYD, 16, Z), BF),
             pltpu.VMEM((PER, 2, KYD, N, Z), BF),
-            pltpu.VMEM((PER, TILES * 128, Z), F32),
             pltpu.VMEM((NCOIL,) + share, BF),
-            DMA((2 + PER,)),
-            DMA((NCOIL, 2)),
+            DMA((2, 2)),
+            DMA((2, 4)),
         ],
-        compiler_params=pltpu.CompilerParams(vmem_limit_bytes=16 << 20),
+        compiler_params=pltpu.CompilerParams(vmem_limit_bytes=12 << 20),
         name="gradient_last",
     )(position, table, piece, sens, before)
+
+
+def sum_over_planes(near_send, far_send, mine, near_keep, far_keep):
+    near = [(i, i ^ 1) for i in range(NCOIL)]
+    far = [(i, NCOIL - 1 - i) for i in range(NCOIL)]
+    near_got = lax.ppermute(near_send, "coil", near)
+    far_got = lax.ppermute(far_send, "coil", far)
+    near_pass = (near_keep.astype(F32) + near_got[1].astype(F32)).astype(BF)
+    far_pass = (far_keep.astype(F32) + far_got[1].astype(F32)).astype(BF)
+    return (
+        mine,
+        near_got,
+        far_got,
+        lax.ppermute(near_pass, "coil", far),
+        lax.ppermute(far_pass, "coil", near),
+    )
 
 
 def haar_rows(top, low):
@@ -546,17 +572,34 @@
 
 
 def update_kernel(
-    base_ref, s0, s1, s2, s3, dual_ref, image_hbm, aux_hbm, dual_hbm, image, aux, dual, sems
+    base_ref,
+    mine,
+    near,
+    far,
+    near_last,
+    far_last,
+    dual_ref,
+    image_hbm,
+    aux_hbm,
+    dual_hbm,
+    image,
+    aux,
+    dual,
+    sems,
 ):
+    span = KYD // 2
     leaving = []
     for m in range(KYD // 2):
         coeffs = []
         for part in range(2):
             rows = []
             for x in (2 * m, 2 * m + 1):
-                gradient = s0[part, x].astype(F32)
-                for share in (s1, s2, s3):
-                    gradient = gradient + share[part, x].astype(F32)
+                first, second = ((near, near_last), (far, far_last))[x // span]
+                gradient = (
+                    mine[part, x].astype(F32)
+                    + first[0, part, x % span].astype(F32)
+                    + second[part, x % span].astype(F32)
+                )
                 value = base_ref[part, x] - step_size * gradient
                 image[part, x] = value
                 rows.append(value)
@@ -572,8 +615,8 @@
                 aux[part, 2 * m + i] = kept
                 dual[part, 2 * m + i] = value - kept
         pair = pl.ds(2 * m, 2)
-        for k, (near, far) in enumerate(((image, image_hbm), (aux, aux_hbm), (dual, dual_hbm))):
-            copy = pltpu.make_async_copy(near.at[:, pair], far.at[:, pair], sems.at[k, m])
+        for k, (held, place) in enumerate(((image, image_hbm), (aux, aux_hbm), (dual, dual_hbm))):
+            copy = pltpu.make_async_copy(held.at[:, pair], place.at[:, pair], sems.at[k, m])
             copy.start()
             leaving.append(copy)
     for copy in leaving:
@@ -585,7 +628,7 @@
     return pl.pallas_call(
         update_kernel,
         out_shape=(shape, shape, shape),
-        in_specs=[VMEM] * (NCOIL + 2),
+        in_specs=[VMEM] * 7,
         out_specs=(HBM, HBM, HBM),
         scratch_shapes=[pltpu.VMEM(scaled_dual.shape, F32)] * 3 + [DMA((3, KYD // 2))],
         compiler_params=pltpu.CompilerParams(vmem_limit_bytes=8 << 20),
@@ -614,7 +657,7 @@
                 (half, turned, by_coil, y_inverse, x_inverse)
             )
         piece = lax.all_to_all(half, "slab", 0, 0, tiled=True)
-        pieces.append(piece.reshape(TILES, PER, KYD, 16, Z))
+        pieces.append(piece)
     position = lax.axis_index("coil").reshape(1)
     base = target_step(position, image, auxiliary, scaled_dual)
     backs = []
@@ -631,14 +674,10 @@
             in_hbm(by_coil),
         )
         backs.append(lax.all_to_all(back, "slab", 0, 0, tiled=True))
-    first, last = (back.reshape(TILES, PER, 128, Z) for back in backs)
+    first, last = backs
     before = gradient_first(y_inverse, in_hbm(first), sensitivity)
-    own, *others = gradient_last(position, y_inverse, in_hbm(last), sensitivity, before)
-    shares = [own]
-    for k in (2, 1, 3):
-        ring = [(i, (i + k) % NCOIL) for i in range(NCOIL)]
-        shares.append(lax.ppermute(others[k - 1], "coil", ring))
-    return update_step(base, shares, scaled_dual)
+    shares = gradient_last(position, y_inverse, in_hbm(last), sensitivity, before)
+    return update_step(base, sum_over_planes(*shares), scaled_dual)
 
 
 def solution(mesh):

time: 167 us -> 168 us (level)
  other arithmetic: 0 us -> 1.89 us
  waiting for transfers between devices: 86.4 us -> 84.6 us
  Pallas kernels: 46.4 us -> 48.2 us
    pallas_call x2, Pallas kernels: 20 us -> 24 us  [grid_tile(): pl.pallas_call(kernel, out_shape=hbm((TILES, PER, KYD, 16, Z), BF), in_sp...]
    convert_element_type x0 -> x2, other arithmetic: none -> 1.89 us  [the longest x1 0.94 us: sum_over_planes(): near_pass = (near_keep.astype(F32) + near_got[1].astype(F32)).astype(BF)]
    ppermute x3 -> x4, waiting for transfers between devices: 8.19 us -> 9.06 us  [the longest x1 6.32 us: sum_over_planes(): far_got = lax.ppermute(far_send, 'coil', far)]
    ppermute x3 -> x4, starting transfers between devices: 7.19 us -> 6.84 us  [the longest x1 4.11 us: sum_over_planes(): far_got = lax.ppermute(far_send, 'coil', far)]
  transfers between devices with their start and end apart: 7 -> 8, of which waited for: 7 -> 7; matrix products, arithmetic and copies ran while one was open for 2% -> 3% of each run, Pallas kernels for 21% -> 22%
where the time goes in v4:
time: 168 us; the launch traced here: 167 us
  waiting for transfers between devices  84.6 us (50%)
  Pallas kernels  48.2 us (29%)
  starting transfers between devices  28.1 us (17%)
  local copies, waits for them, and re-layouts  2.94 us (2%)
  other arithmetic  1.89 us (1%)
    all_to_all x2, waiting for transfers between devices, body(): backs.append(lax.all_to_all(back, 'slab', 0, 0, tiled=True))  41.4 us
    all_to_all x2, waiting for transfers between devices, body(): piece = lax.all_to_all(half, 'slab', 0, 0, tiled=True)  34.1 us
    pallas_call x2, Pallas kernels, grid_tile(): pl.pallas_call(kernel, out_shape=hbm((TILES, PER, KYD, 16, Z), BF), in_sp...  24 us
    all_to_all x2, starting transfers between devices, body(): piece = lax.all_to_all(half, 'slab', 0, 0, tiled=True)  11.6 us
    pallas_call x2, Pallas kernels, coil_forward(): pl.pallas_call(kernel, out_shape=hbm((TILES, PER, KYD, 16, Z), BF), in_sp...  10.2 us
    all_to_all x2, starting transfers between devices, body(): backs.append(lax.all_to_all(back, 'slab', 0, 0, tiled=True))  9.71 us
    ppermute x1, waiting for transfers between devices, sum_over_planes(): far_got = lax.ppermute(far_send, 'coil', far)  6.32 us
    pallas_call x1, Pallas kernels, gradient_first(): pl.pallas_call(gradient_first_kernel, out_shape=jax.ShapeDtypeStruct((2,...  4.87 us
  transfers between devices with their start and end apart: 8, of which 7 were waited for; matrix products, arithmetic and copies ran while one was open for 3% of the time, Pallas kernels for 22%

profile of v4, /device:TPU:0, one launch (start us, length us, event | category | flops | bytes accessed | tf_op | source)
XLA Modules:
  0.0 167.4 jit_solution(4152095763595129921)
XLA Ops:
  0.6 5.2 %coil_forward_0.1 = bf16[32,2,8,16,128]{4,3,2,1,0:T(8,128)(2,1)} custom-call(bf16[512,512]{1,0:T(8,128)(2,1)} %constant.20.refs_0_, bf16[4,2,8,256,128]{4,3,2,1,0:T(8,128)(2,1)} %sens_hbm.3, f32[2,8,256,128]{3,2,1,0:T(8,128)} %refs_2_.3), custom_call_target="tpu_custom_call" | custom-call | tf_op jit(solution)/shard_map/coil_forward_0/pallas_call | solution.py:139
  5.8 7.5 %all-to-all-start.2 = ((bf16[32,2,8,16,128]{4,3,2,1,0:T(8,128)(2,1)}), bf16[32,2,8,16,128]{4,3,2,1,0:T(8,128)(2,1)}, u32[]{:S(2)}, u32[]{:S(2)}) async-start(bf16[32,2,8,16,128]{4,3,2,1,0:T(8,128)(2,1)} %coil_forward_0.1), calls=%async_computation.2 | async-start | bytes 4194304 | tf_op jit(solution)/shard_map/all_to_all | solution.py:659
  13.4 0.0 copy-start.7
  13.4 5.0 %coil_forward_1.1 = bf16[32,2,8,16,128]{4,3,2,1,0:T(8,128)(2,1)} custom-call(bf16[512,512]{1,0:T(8,128)(2,1)} %constant.20.refs_0_, bf16[4,2,8,256,128]{4,3,2,1,0:T(8,128)(2,1)} %sens_hbm.3, f32[2,8,256,128]{3,2,1,0:T(8,128)} %refs_2_.3), custom_call_target="tpu_custom_call" | custom-call | tf_op jit(solution)/shard_map/coil_forward_1/pallas_call | solution.py:139
  19.1 0.0 copy-done.7
  19.1 2.9 %copy.14 = bf16[1,24,128,512]{2,3,1,0:T(8,128)(2,1)} copy(bf16[1,24,128,512]{3,2,1,0:T(8,128)(2,1)S(1)} %copy-done.7) | data formatting | bytes 6291456 | tf_op args[2]
  22.0 2.2 %samples_by_coil.1.refs_7_ = bf16[4,24,128,256]{3,2,1,0:T(8,128)(2,1)} custom-call(s32[1]{0:T(128)S(6)} %copy.21.counts_ref.refs_1_, bf16[24,128,8,128]{3,2,1,0:T(8,128)(2,1)} %bitcast.26), custom_call_target="tpu_custom_call" | custom-call | tf_op jit(solution)/shard_map/samples_by_coil/pallas_call | solution.py:192
  24.2 0.0 copy-start.1
  24.2 0.0 copy-start.2
  24.3 0.0 copy-start.6
  24.3 18.0 %all-to-all-done.2.refs_2_ = bf16[32,2,8,16,128]{4,3,2,1,0:T(8,128)(2,1)} async-done(((bf16[32,2,8,16,128]{4,3,2,1,0:T(8,128)(2,1)}), bf16[32,2,8,16,128]{4,3,2,1,0:T(8,128)(2,1)}, u32[]{:S(2)}, u32[]{:S(2)}) %all-to-all-start.2) | async-done | bytes 2097184 | tf_op jit(solution)/shard_map/all_to_all | solution.py:659
  42.3 4.0 %all-to-all-start = ((bf16[32,2,8,16,128]{4,3,2,1,0:T(8,128)(2,1)}), bf16[32,2,8,16,128]{4,3,2,1,0:T(8,128)(2,1)S(1)}, u32[]{:S(2)}, u32[]{:S(2)}) async-start(bf16[32,2,8,16,128]{4,3,2,1,0:T(8,128)(2,1)} %coil_forward_1.1), calls=%async_computation | async-start | bytes 4194304 | tf_op jit(solution)/shard_map/all_to_all | solution.py:659
  46.3 0.0 copy-done.1
  46.3 0.0 copy-done.2
  46.3 0.0 copy-done.6
  46.4 12.8 %grid_tile_0.1 = bf16[32,2,8,16,128]{4,3,2,1,0:T(8,128)(2,1)} custom-call(s32[1,24]{1,0:T(1,128)S(1)} %copy-done.6, s32[1]{0:T(128)S(6)} %copy.21.counts_ref.refs_1_, bf16[32,2,8,16,128]{4,3,2,1,0:T(8,128)(2,1)} %all-to-all-done.2.refs_2_, bf16[512,512]{1,0:T(8,128)(2,1)S(1)} %copy-done.2, bf16[512,512]{1,0:T(8,128)(2,1)S(1)} %bitcast.20, ...), custom_call_target="tpu_custom_call" | custom-call | tf_op jit(solution)/shard_map/grid_tile_0/pallas_call | solution.py:363
  59.1 16.1 %all-to-all-done.refs_2_ = bf16[32,2,8,16,128]{4,3,2,1,0:T(8,128)(2,1)S(1)} async-done(((bf16[32,2,8,16,128]{4,3,2,1,0:T(8,128)(2,1)}), bf16[32,2,8,16,128]{4,3,2,1,0:T(8,128)(2,1)S(1)}, u32[]{:S(2)}, u32[]{:S(2)}) %all-to-all-start) | async-done | bytes 2097184 | tf_op jit(solution)/shard_map/all_to_all | solution.py:659
  75.2 4.8 %all-to-all-start.3 = ((bf16[32,2,8,16,128]{4,3,2,1,0:T(8,128)(2,1)}), bf16[32,2,8,16,128]{4,3,2,1,0:T(8,128)(2,1)}, u32[]{:S(2)}, u32[]{:S(2)}) async-start(bf16[32,2,8,16,128]{4,3,2,1,0:T(8,128)(2,1)} %grid_tile_0.1), calls=%async_computation.3 | async-start | bytes 4194304 | tf_op jit(solution)/shard_map/all_to_all | solution.py:676
  80.0 11.3 %grid_tile_1.1 = bf16[32,2,8,16,128]{4,3,2,1,0:T(8,128)(2,1)} custom-call(s32[1,24]{1,0:T(1,128)S(1)} %copy-done.6, s32[1]{0:T(128)S(6)} %copy.21.counts_ref.refs_1_, bf16[32,2,8,16,128]{4,3,2,1,0:T(8,128)(2,1)S(1)} %all-to-all-done.refs_2_, bf16[512,512]{1,0:T(8,128)(2,1)S(1)} %copy-done.2, bf16[512,512]{1,0:T(8,128)(2,1)S(1)} %bitcast.21, ...), custom_call_target="tpu_custom_call" | custom-call | tf_op jit(solution)/shard_map/grid_tile_1/pallas_call | solution.py:363
  91.3 0.0 copy-start
  91.3 17.6 %all-to-all-done.3.piece_hbm = bf16[32,2,8,16,128]{4,3,2,1,0:T(8,128)(2,1)} async-done(((bf16[32,2,8,16,128]{4,3,2,1,0:T(8,128)(2,1)}), bf16[32,2,8,16,128]{4,3,2,1,0:T(8,128)(2,1)}, u32[]{:S(2)}, u32[]{:S(2)}) %all-to-all-start.3) | async-done | bytes 2097184 | tf_op jit(solution)/shard_map/all_to_all | solution.py:676
  108.9 4.9 %all-to-all-start.1 = ((bf16[32,2,8,16,128]{4,3,2,1,0:T(8,128)(2,1)}), bf16[32,2,8,16,128]{4,3,2,1,0:T(8,128)(2,1)}, u32[]{:S(2)}, u32[]{:S(2)}) async-start(bf16[32,2,8,16,128]{4,3,2,1,0:T(8,128)(2,1)} %grid_tile_1.1), calls=%async_computation.1 | async-start | bytes 4194304 | tf_op jit(solution)/shard_map/all_to_all | solution.py:676
  113.8 0.0 copy-done
  113.8 4.9 %gradient_first.1.before_ref = f32[2,8,256,128]{3,2,1,0:T(8,128)S(1)} custom-call(bf16[512,512]{1,0:T(8,128)(2,1)S(1)} %bitcast.18, bf16[32,2,8,16,128]{4,3,2,1,0:T(8,128)(2,1)} %all-to-all-done.3.piece_hbm, bf16[4,2,8,256,128]{4,3,2,1,0:T(8,128)(2,1)} %sens_hbm.3), custom_call_target="tpu_custom_call" | custom-call | tf_op jit(solution)/shard_map/gradient_first/pallas_call | solution.py:425
  118.7 23.8 %all-to-all-done.1.piece_hbm = bf16[32,2,8,16,128]{4,3,2,1,0:T(8,128)(2,1)} async-done(((bf16[32,2,8,16,128]{4,3,2,1,0:T(8,128)(2,1)}), bf16[32,2,8,16,128]{4,3,2,1,0:T(8,128)(2,1)}, u32[]{:S(2)}, u32[]{:S(2)}) %all-to-all-start.1) | async-done | bytes 2097184 | tf_op jit(solution)/shard_map/all_to_all | solution.py:676
  142.5 0.0 copy-start.3
  142.5 0.0 copy-start.4
  142.5 4.2 %gradient_last.1 = (bf16[2,2,4,64,128]{4,3,2,1,0:T(8,128)(2,1)}, bf16[2,2,4,64,128]{4,3,2,1,0:T(8,128)(2,1)}, bf16[2,8,64,128]{3,2,1,0:T(8,128)(2,1)}, bf16[2,4,...) custom-call(s32[1]{0:T(128)} %bitcast.position_ref, bf16[512,512]{1,0:T(8,128)(2,1)S(1)} %bitcast.19, ...), custom_call_target="tpu_custom_call" | custom-call | tf_op jit(solution)/shard_map/gradient_last/pallas_call | solution.py:499
  146.8 4.1 %collective-permute-start.1 = (bf16[2,2,4,64,128]{4,3,2,1,0:T(8,128)(2,1)}, bf16[2,2,4,64,128]{4,3,2,1,0:T(8,128)(2,1)S(1)}, u32[]{:S(2)}, u32[]{:S(2)}) collective-permute-start(bf16[2,2,4,64,128]{4,3,2,1,0:T(8,128)(2,1)} %get-tuple-element.24), channel_id=1, source_target_pairs={{0,96},{32,64},{64,32},{96,0},{1,97},{33,65},{65,33},{97,1},{2,98}... | collective-permute-start | bytes 786440 | tf_op jit(solution)/shard_map/ppermute | solution.py:520
  150.9 0.0 collective-permute-start
  150.9 6.3 %collective-permute-done.1.far = bf16[2,2,4,64,128]{4,3,2,1,0:T(8,128)(2,1)S(1)} collective-permute-done((bf16[2,2,4,64,128]{4,3,2,1,0:T(8,128)(2,1)}, bf16[2,2,4,64,128]{4,3,2,1,0:T(8,128)(2,1)S(1)}, u32[]{:S(2)}, u32[]{:S(2)}) %collective-permute-start.1) | collective-permute-done | bytes 262176 | tf_op jit(solution)/shard_map/ppermute | solution.py:520
  157.2 0.9 fusion
  158.1 0.0 copy-start.5
  158.2 0.1 collective-permute-start.3
  158.3 0.4 collective-permute-done.near
  158.7 0.9 fusion.1
  159.6 2.6 %collective-permute-start.2 = (bf16[2,4,64,128]{3,2,1,0:T(8,128)(2,1)S(1)}, bf16[2,4,64,128]{3,2,1,0:T(8,128)(2,1)S(1)}, u32[]{:S(2)}, u32[]{:S(2)}) collective-permute-start(bf16[2,4,64,128]{3,2,1,0:T(8,128)(2,1)S(1)} %fusion.1), channel_id=1, source_target_pairs={{0,96},{32,64},{64,32},{96,0},{1,97},{33,65},{65,33},{97,1},{2,98}... | collective-permute-start | bytes 393224 | tf_op jit(solution)/shard_map/ppermute | solution.py:527
  162.2 0.0 copy-done.3
  162.2 0.0 copy-done.4
  162.2 1.3 target.1.base_ref
  163.5 0.0 collective-permute-done.3.far_last
  163.5 2.3 %collective-permute-done.2.near_last = bf16[2,4,64,128]{3,2,1,0:T(8,128)(2,1)S(1)} collective-permute-done((bf16[2,4,64,128]{3,2,1,0:T(8,128)(2,1)S(1)}, bf16[2,4,64,128]{3,2,1,0:T(8,128)(2,1)S(1)}, u32[]{:S(2)}, u32[]{:S(2)}) %collective-permute-start.2) | collective-permute-done | bytes 131104 | tf_op jit(solution)/shard_map/ppermute | solution.py:527
  165.9 0.0 copy-done.5
  165.9 1.3 update.1
Async XLA Ops:
  5.8 36.5 %all-to-all-start.2 = ((bf16[32,2,8,16,128]{4,3,2,1,0:T(8,128)(2,1)}), bf16[32,2,8,16,128]{4,3,2,1,0:T(8,128)(2,1)}, u32[]{:S(2)}, u32[]{:S(2)}) async-start(bf16[32,2,8,16,128]{4,3,2,1,0:T(8,128)(2,1)} %coil_forward_0.1), calls=%async_computation.2 | async-start | bytes 4194304 | tf_op jit(solution)/shard_map/all_to_all | solution.py:659
  13.4 5.7 %copy-start.7 = (bf16[1,24,128,512]{3,2,1,0:T(8,128)(2,1)S(1)}, bf16[1,24,128,512]{3,2,1,0:T(8,128)(2,1)}, u32[]{:S(2)}) copy-start(bf16[1,24,128,512]{3,2,1,0:T(8,128)(2,1)} %param.12) | copy-start | bytes 9437188
  24.2 22.1 %copy-start.1 = (bf16[512,512]{0,1:T(8,128)(2,1)S(1)}, bf16[512,512]{0,1:T(8,128)(2,1)}, u32[]{:S(2)}) copy-start(bf16[512,512]{0,1:T(8,128)(2,1)} %constant.11.clone) | copy-start | bytes 1572868
  24.2 22.1 %copy-start.2 = (bf16[512,512]{1,0:T(8,128)(2,1)S(1)}, bf16[512,512]{1,0:T(8,128)(2,1)}, u32[]{:S(2)}) copy-start(bf16[512,512]{1,0:T(8,128)(2,1)} %constant.21.refs_3_) | copy-start | bytes 1572868
  24.3 22.1 %copy-start.6 = (s32[1,24]{1,0:T(1,128)S(1)}, s32[1,24]{1,0:T(1,128)}, u32[]{:S(2)}) copy-start(s32[1,24]{1,0:T(1,128)} %refs_0_.5) | copy-start | bytes 292
  42.3 32.9 %all-to-all-start = ((bf16[32,2,8,16,128]{4,3,2,1,0:T(8,128)(2,1)}), bf16[32,2,8,16,128]{4,3,2,1,0:T(8,128)(2,1)S(1)}, u32[]{:S(2)}, u32[]{:S(2)}) async-start(bf16[32,2,8,16,128]{4,3,2,1,0:T(8,128)(2,1)} %coil_forward_1.1), calls=%async_computation | async-start | bytes 4194304 | tf_op jit(solution)/shard_map/all_to_all | solution.py:659
  75.2 33.6 %all-to-all-start.3 = ((bf16[32,2,8,16,128]{4,3,2,1,0:T(8,128)(2,1)}), bf16[32,2,8,16,128]{4,3,2,1,0:T(8,128)(2,1)}, u32[]{:S(2)}, u32[]{:S(2)}) async-start(bf16[32,2,8,16,128]{4,3,2,1,0:T(8,128)(2,1)} %grid_tile_0.1), calls=%async_computation.3 | async-start | bytes 4194304 | tf_op jit(solution)/shard_map/all_to_all | solution.py:676
  91.3 22.6 %copy-start = (bf16[512,512]{0,1:T(8,128)(2,1)S(1)}, bf16[512,512]{0,1:T(8,128)(2,1)}, u32[]{:S(2)}) copy-start(bf16[512,512]{0,1:T(8,128)(2,1)} %constant.10.clone) | copy-start | bytes 1572868
  108.9 33.6 %all-to-all-start.1 = ((bf16[32,2,8,16,128]{4,3,2,1,0:T(8,128)(2,1)}), bf16[32,2,8,16,128]{4,3,2,1,0:T(8,128)(2,1)}, u32[]{:S(2)}, u32[]{:S(2)}) async-start(bf16[32,2,8,16,128]{4,3,2,1,0:T(8,128)(2,1)} %grid_tile_1.1), calls=%async_computation.1 | async-start | bytes 4194304 | tf_op jit(solution)/shard_map/all_to_all | solution.py:676
  142.5 19.7 %copy-start.3 = (f32[2,8,64,128]{3,2,1,0:T(8,128)S(1)}, f32[2,8,64,128]{3,2,1,0:T(8,128)}, u32[]{:S(2)}) copy-start(f32[2,8,64,128]{3,2,1,0:T(8,128)} %dual_ref.3) | copy-start | bytes 1572868
  142.5 19.7 %copy-start.4 = (f32[2,8,64,128]{3,2,1,0:T(8,128)S(1)}, f32[2,8,64,128]{3,2,1,0:T(8,128)}, u32[]{:S(2)}) copy-start(f32[2,8,64,128]{3,2,1,0:T(8,128)} %aux_ref.1) | copy-start | bytes 1572868
  146.8 10.4 %collective-permute-start.1 = (bf16[2,2,4,64,128]{4,3,2,1,0:T(8,128)(2,1)}, bf16[2,2,4,64,128]{4,3,2,1,0:T(8,128)(2,1)S(1)}, u32[]{:S(2)}, u32[]{:S(2)}) collective-permute-start(bf16[2,2,4,64,128]{4,3,2,1,0:T(8,128)(2,1)} %get-tuple-element.24), channel_id=1, source_target_pairs={{0,96},{32,64},{64,32},{96,0},{1,97},{33,65},{65,33},{97,1},{2,98}... | collective-permute-start | bytes 786440 | tf_op jit(solution)/shard_map/ppermute | solution.py:520
  150.9 7.8 %collective-permute-start = (bf16[2,2,4,64,128]{4,3,2,1,0:T(8,128)(2,1)}, bf16[2,2,4,64,128]{4,3,2,1,0:T(8,128)(2,1)S(1)}, u32[]{:S(2)}, u32[]{:S(2)}) collective-permute-start(bf16[2,2,4,64,128]{4,3,2,1,0:T(8,128)(2,1)} %get-tuple-element.23), channel_id=1, source_target_pairs={{0,32},{32,0},{64,96},{96,64},{1,33},{33,1},{65,97},{97,65},{2,34}... | collective-permute-start | bytes 786440 | tf_op jit(solution)/shard_map/ppermute | solution.py:519
  158.1 7.7 %copy-start.5 = (bf16[2,8,64,128]{3,2,1,0:T(8,128)(2,1)S(1)}, bf16[2,8,64,128]{3,2,1,0:T(8,128)(2,1)}, u32[]{:S(2)}) copy-start(bf16[2,8,64,128]{3,2,1,0:T(8,128)(2,1)} %get-tuple-element.22.mine) | copy-start | bytes 786436
  158.2 5.4 %collective-permute-start.3 = (bf16[2,4,64,128]{3,2,1,0:T(8,128)(2,1)S(1)}, bf16[2,4,64,128]{3,2,1,0:T(8,128)(2,1)S(1)}, u32[]{:S(2)}, u32[]{:S(2)}) collective-permute-start(bf16[2,4,64,128]{3,2,1,0:T(8,128)(2,1)S(1)} %fusion), channel_id=1, source_target_pairs={{0,32},{32,0},{64,96},{96,64},{1,33},{33,1},{65,97},{97,65},{2,34}... | collective-permute-start | bytes 393224 | tf_op jit(solution)/shard_map/ppermute | solution.py:528
  159.6 6.3 %collective-permute-start.2 = (bf16[2,4,64,128]{3,2,1,0:T(8,128)(2,1)S(1)}, bf16[2,4,64,128]{3,2,1,0:T(8,128)(2,1)S(1)}, u32[]{:S(2)}, u32[]{:S(2)}) collective-permute-start(bf16[2,4,64,128]{3,2,1,0:T(8,128)(2,1)S(1)} %fusion.1), channel_id=1, source_target_pairs={{0,96},{32,64},{64,32},{96,0},{1,97},{33,65},{65,33},{97,1},{2,98}... | collective-permute-start | bytes 393224 | tf_op jit(solution)/shard_map/ppermute | solution.py:527

commit v5 on v4

--- a/solution.py
+++ b/solution.py
@@ -438,12 +438,9 @@
 
 
 def gradient_last_kernel(position_ref, table_ref, piece_hbm, sens_hbm, before_ref, *rest):
-    near_send, far_send, mine, near_keep, far_keep = rest[:5]
-    piece, sens, out, arrive, sems = rest[5:]
-    me = position_ref[0]
-    near = me + 1 - 2 * lax.rem(me, 2)
-    far = NCOIL - 1 - me
-    across = NCOIL - 1 - near
+    shares = rest[:NCOIL]
+    piece, sens, out, arrive, sems = rest[NCOIL:]
+    position = position_ref[0]
     span = KYD // 2
 
     def arrivals(stage):
@@ -457,25 +454,16 @@
             ),
         )
 
-    def departures(stage):
+    def leave(k, stage):
         rows = pl.ds(stage * span, span)
-        first, keep = ((near, far), (far, near))[stage]
-        send, kept = ((near_send, near_keep), (far_send, far_keep))[stage]
-        pairs = (
-            (first, send.at[0]),
-            (across, send.at[1]),
-            (keep, kept),
-            (me, mine.at[:, rows]),
+        target = lax.rem(position + k, NCOIL)
+        return pltpu.make_async_copy(
+            out.at[target, :, rows], shares[k].at[:, rows], sems.at[k, stage]
         )
-        return [
-            pltpu.make_async_copy(out.at[target, :, rows], place, sems.at[stage, k])
-            for k, (target, place) in enumerate(pairs)
-        ]
 
     for stage in range(2):
         for copy in arrivals(stage):
             copy.start()
-    leaving = []
     for stage in range(2):
         for copy in arrivals(stage):
             copy.wait()
@@ -485,48 +473,30 @@
             )
             out[:, 0, x] = g_re.astype(BF).reshape(NCOIL, N // NCOIL, Z)
             out[:, 1, x] = g_im.astype(BF).reshape(NCOIL, N // NCOIL, Z)
-        for copy in departures(stage):
-            copy.start()
-            leaving.append(copy)
-    for copy in leaving:
-        copy.wait()
+        for k in range(NCOIL):
+            leave(k, stage).start()
+    for stage in range(2):
+        for k in range(NCOIL):
+            leave(k, stage).wait()
 
 
 def gradient_last(position, table, piece, sens, before):
     share = (2, KYD, N // NCOIL, Z)
-    half = (2, KYD // 2, N // NCOIL, Z)
-    shapes = ((2,) + half, (2,) + half, share, half, half)
     return pl.pallas_call(
         gradient_last_kernel,
-        out_shape=tuple(hbm(shape, BF) for shape in shapes),
+        out_shape=(hbm(share, BF),) * NCOIL,
         in_specs=[SMEM, VMEM, HBM, HBM, VMEM],
-        out_specs=(HBM,) * 5,
+        out_specs=(HBM,) * NCOIL,
         scratch_shapes=[
             pltpu.VMEM((TILES, PER, KYD, 16, Z), BF),
             pltpu.VMEM((PER, 2, KYD, N, Z), BF),
             pltpu.VMEM((NCOIL,) + share, BF),
             DMA((2, 2)),
-            DMA((2, 4)),
+            DMA((NCOIL, 2)),
         ],
         compiler_params=pltpu.CompilerParams(vmem_limit_bytes=12 << 20),
         name="gradient_last",
     )(position, table, piece, sens, before)
-
-
-def sum_over_planes(near_send, far_send, mine, near_keep, far_keep):
-    near = [(i, i ^ 1) for i in range(NCOIL)]
-    far = [(i, NCOIL - 1 - i) for i in range(NCOIL)]
-    near_got = lax.ppermute(near_send, "coil", near)
-    far_got = lax.ppermute(far_send, "coil", far)
-    near_pass = (near_keep.astype(F32) + near_got[1].astype(F32)).astype(BF)
-    far_pass = (far_keep.astype(F32) + far_got[1].astype(F32)).astype(BF)
-    return (
-        mine,
-        near_got,
-        far_got,
-        lax.ppermute(near_pass, "coil", far),
-        lax.ppermute(far_pass, "coil", near),
-    )
 
 
 def haar_rows(top, low):
@@ -572,34 +542,17 @@
 
 
 def update_kernel(
-    base_ref,
-    mine,
-    near,
-    far,
-    near_last,
-    far_last,
-    dual_ref,
-    image_hbm,
-    aux_hbm,
-    dual_hbm,
-    image,
-    aux,
-    dual,
-    sems,
+    base_ref, s0, s1, s2, s3, dual_ref, image_hbm, aux_hbm, dual_hbm, image, aux, dual, sems
 ):
-    span = KYD // 2
     leaving = []
     for m in range(KYD // 2):
         coeffs = []
         for part in range(2):
             rows = []
             for x in (2 * m, 2 * m + 1):
-                first, second = ((near, near_last), (far, far_last))[x // span]
-                gradient = (
-                    mine[part, x].astype(F32)
-                    + first[0, part, x % span].astype(F32)
-                    + second[part, x % span].astype(F32)
-                )
+                gradient = s0[part, x].astype(F32)
+                for share in (s1, s2, s3):
+                    gradient = gradient + share[part, x].astype(F32)
                 value = base_ref[part, x] - step_size * gradient
                 image[part, x] = value
                 rows.append(value)
@@ -615,8 +568,8 @@
                 aux[part, 2 * m + i] = kept
                 dual[part, 2 * m + i] = value - kept
         pair = pl.ds(2 * m, 2)
-        for k, (held, place) in enumerate(((image, image_hbm), (aux, aux_hbm), (dual, dual_hbm))):
-            copy = pltpu.make_async_copy(held.at[:, pair], place.at[:, pair], sems.at[k, m])
+        for k, (near, far) in enumerate(((image, image_hbm), (aux, aux_hbm), (dual, dual_hbm))):
+            copy = pltpu.make_async_copy(near.at[:, pair], far.at[:, pair], sems.at[k, m])
             copy.start()
             leaving.append(copy)
     for copy in leaving:
@@ -628,7 +581,7 @@
     return pl.pallas_call(
         update_kernel,
         out_shape=(shape, shape, shape),
-        in_specs=[VMEM] * 7,
+        in_specs=[VMEM] * (NCOIL + 2),
         out_specs=(HBM, HBM, HBM),
         scratch_shapes=[pltpu.VMEM(scaled_dual.shape, F32)] * 3 + [DMA((3, KYD // 2))],
         compiler_params=pltpu.CompilerParams(vmem_limit_bytes=8 << 20),
@@ -676,8 +629,12 @@
         backs.append(lax.all_to_all(back, "slab", 0, 0, tiled=True))
     first, last = backs
     before = gradient_first(y_inverse, in_hbm(first), sensitivity)
-    shares = gradient_last(position, y_inverse, in_hbm(last), sensitivity, before)
-    return update_step(base, sum_over_planes(*shares), scaled_dual)
+    own, *others = gradient_last(position, y_inverse, in_hbm(last), sensitivity, before)
+    shares = [own]
+    for k in (2, 1, 3):
+        ring = [(i, (i + k) % NCOIL) for i in range(NCOIL)]
+        shares.append(lax.ppermute(others[k - 1], "coil", ring))
+    return update_step(base, shares, scaled_dual)
 
 
 def solution(mesh):

time: 168 us -> 166 us (0.988)
  other arithmetic: 1.89 us -> 0 us
    convert_element_type x2 -> x0, other arithmetic: 1.89 us -> none  [the longest x1 0.94 us: sum_over_planes(): near_pass = (near_keep.astype(F32) + near_got[1].astype(F32)).astype(BF)]
    ppermute x4 -> x3, waiting for transfers between devices: 9.06 us -> 8.19 us  [body(): shares.append(lax.ppermute(others[k - 1], 'coil', ring))]
    ppermute x4 -> x3, starting transfers between devices: 6.84 us -> 7.19 us  [body(): shares.append(lax.ppermute(others[k - 1], 'coil', ring))]
  transfers between devices with their start and end apart: 8 -> 7, of which waited for: 7 -> 7; matrix products, arithmetic and copies ran while one was open for 3% -> 2% of each run, Pallas kernels for 22% -> 23%
where the time goes in v5:
time: 166 us; the launch traced here: 165 us
  waiting for transfers between devices  83.8 us (50%)
  Pallas kernels  48.1 us (29%)
  starting transfers between devices  28.5 us (17%)
  local copies, waits for them, and re-layouts  2.94 us (2%)
    all_to_all x2, waiting for transfers between devices, body(): backs.append(lax.all_to_all(back, 'slab', 0, 0, tiled=True))  41.5 us
    all_to_all x2, waiting for transfers between devices, body(): piece = lax.all_to_all(half, 'slab', 0, 0, tiled=True)  34.2 us
    pallas_call x2, Pallas kernels, grid_tile(): pl.pallas_call(kernel, out_shape=hbm((TILES, PER, KYD, 16, Z), BF), in_sp...  23.9 us
    all_to_all x2, starting transfers between devices, body(): piece = lax.all_to_all(half, 'slab', 0, 0, tiled=True)  11.6 us
    pallas_call x2, Pallas kernels, coil_forward(): pl.pallas_call(kernel, out_shape=hbm((TILES, PER, KYD, 16, Z), BF), in_sp...  10.3 us
    all_to_all x2, starting transfers between devices, body(): backs.append(lax.all_to_all(back, 'slab', 0, 0, tiled=True))  9.71 us
    ppermute x3, waiting for transfers between devices, body(): shares.append(lax.ppermute(others[k - 1], 'coil', ring))  8.19 us
    ppermute x3, starting transfers between devices, body(): shares.append(lax.ppermute(others[k - 1], 'coil', ring))  7.19 us
  transfers between devices with their start and end apart: 7, of which 7 were waited for; matrix products, arithmetic and copies ran while one was open for 2% of the time, Pallas kernels for 23%

profile of v5, /device:TPU:0, one launch (start us, length us, event | category | flops | bytes accessed | tf_op | source)
XLA Modules:
  0.0 164.9 jit_solution(17031859585973697185)
XLA Ops:
  0.6 5.2 %coil_forward_0.1 = bf16[32,2,8,16,128]{4,3,2,1,0:T(8,128)(2,1)} custom-call(bf16[512,512]{1,0:T(8,128)(2,1)} %constant.20.refs_0_, bf16[4,2,8,256,128]{4,3,2,1,0:T(8,128)(2,1)} %sens_hbm.3, f32[2,8,256,128]{3,2,1,0:T(8,128)} %refs_2_.3), custom_call_target="tpu_custom_call" | custom-call | tf_op jit(solution)/shard_map/coil_forward_0/pallas_call | solution.py:139
  5.9 7.5 %all-to-all-start.2 = ((bf16[32,2,8,16,128]{4,3,2,1,0:T(8,128)(2,1)}), bf16[32,2,8,16,128]{4,3,2,1,0:T(8,128)(2,1)}, u32[]{:S(2)}, u32[]{:S(2)}) async-start(bf16[32,2,8,16,128]{4,3,2,1,0:T(8,128)(2,1)} %coil_forward_0.1), calls=%async_computation.2 | async-start | bytes 4194304 | tf_op jit(solution)/shard_map/all_to_all | solution.py:612
  13.4 0.0 copy-start.7
  13.4 5.0 %coil_forward_1.1 = bf16[32,2,8,16,128]{4,3,2,1,0:T(8,128)(2,1)} custom-call(bf16[512,512]{1,0:T(8,128)(2,1)} %constant.20.refs_0_, bf16[4,2,8,256,128]{4,3,2,1,0:T(8,128)(2,1)} %sens_hbm.3, f32[2,8,256,128]{3,2,1,0:T(8,128)} %refs_2_.3), custom_call_target="tpu_custom_call" | custom-call | tf_op jit(solution)/shard_map/coil_forward_1/pallas_call | solution.py:139
  19.1 0.0 copy-done.7
  19.1 2.9 %copy.14 = bf16[1,24,128,512]{2,3,1,0:T(8,128)(2,1)} copy(bf16[1,24,128,512]{3,2,1,0:T(8,128)(2,1)S(1)} %copy-done.7) | data formatting | bytes 6291456 | tf_op args[2]
  22.0 2.3 %samples_by_coil.1.refs_7_ = bf16[4,24,128,256]{3,2,1,0:T(8,128)(2,1)} custom-call(s32[1]{0:T(128)S(6)} %copy.21.counts_ref.refs_1_, bf16[24,128,8,128]{3,2,1,0:T(8,128)(2,1)} %bitcast.16), custom_call_target="tpu_custom_call" | custom-call | tf_op jit(solution)/shard_map/samples_by_coil/pallas_call | solution.py:192
  24.3 0.0 copy-start.1
  24.3 0.0 copy-start.2
  24.3 0.0 copy-start.6
  24.3 18.0 %all-to-all-done.2.refs_2_ = bf16[32,2,8,16,128]{4,3,2,1,0:T(8,128)(2,1)} async-done(((bf16[32,2,8,16,128]{4,3,2,1,0:T(8,128)(2,1)}), bf16[32,2,8,16,128]{4,3,2,1,0:T(8,128)(2,1)}, u32[]{:S(2)}, u32[]{:S(2)}) %all-to-all-start.2) | async-done | bytes 2097184 | tf_op jit(solution)/shard_map/all_to_all | solution.py:612
  42.3 4.0 %all-to-all-start = ((bf16[32,2,8,16,128]{4,3,2,1,0:T(8,128)(2,1)}), bf16[32,2,8,16,128]{4,3,2,1,0:T(8,128)(2,1)S(1)}, u32[]{:S(2)}, u32[]{:S(2)}) async-start(bf16[32,2,8,16,128]{4,3,2,1,0:T(8,128)(2,1)} %coil_forward_1.1), calls=%async_computation | async-start | bytes 4194304 | tf_op jit(solution)/shard_map/all_to_all | solution.py:612
  46.3 0.0 copy-done.1
  46.3 0.0 copy-done.2
  46.4 0.0 copy-done.6
  46.4 12.7 %grid_tile_0.1 = bf16[32,2,8,16,128]{4,3,2,1,0:T(8,128)(2,1)} custom-call(s32[1,24]{1,0:T(1,128)S(1)} %copy-done.6, s32[1]{0:T(128)S(6)} %copy.21.counts_ref.refs_1_, bf16[32,2,8,16,128]{4,3,2,1,0:T(8,128)(2,1)} %all-to-all-done.2.refs_2_, bf16[512,512]{1,0:T(8,128)(2,1)S(1)} %copy-done.2, bf16[512,512]{1,0:T(8,128)(2,1)S(1)} %bitcast.10, ...), custom_call_target="tpu_custom_call" | custom-call | tf_op jit(solution)/shard_map/grid_tile_0/pallas_call | solution.py:363
  59.1 16.2 %all-to-all-done.refs_2_ = bf16[32,2,8,16,128]{4,3,2,1,0:T(8,128)(2,1)S(1)} async-done(((bf16[32,2,8,16,128]{4,3,2,1,0:T(8,128)(2,1)}), bf16[32,2,8,16,128]{4,3,2,1,0:T(8,128)(2,1)S(1)}, u32[]{:S(2)}, u32[]{:S(2)}) %all-to-all-start) | async-done | bytes 2097184 | tf_op jit(solution)/shard_map/all_to_all | solution.py:612
  75.2 4.8 %all-to-all-start.3 = ((bf16[32,2,8,16,128]{4,3,2,1,0:T(8,128)(2,1)}), bf16[32,2,8,16,128]{4,3,2,1,0:T(8,128)(2,1)}, u32[]{:S(2)}, u32[]{:S(2)}) async-start(bf16[32,2,8,16,128]{4,3,2,1,0:T(8,128)(2,1)} %grid_tile_0.1), calls=%async_computation.3 | async-start | bytes 4194304 | tf_op jit(solution)/shard_map/all_to_all | solution.py:629
  80.0 11.2 %grid_tile_1.1 = bf16[32,2,8,16,128]{4,3,2,1,0:T(8,128)(2,1)} custom-call(s32[1,24]{1,0:T(1,128)S(1)} %copy-done.6, s32[1]{0:T(128)S(6)} %copy.21.counts_ref.refs_1_, bf16[32,2,8,16,128]{4,3,2,1,0:T(8,128)(2,1)S(1)} %all-to-all-done.refs_2_, bf16[512,512]{1,0:T(8,128)(2,1)S(1)} %copy-done.2, bf16[512,512]{1,0:T(8,128)(2,1)S(1)} %bitcast.11, ...), custom_call_target="tpu_custom_call" | custom-call | tf_op jit(solution)/shard_map/grid_tile_1/pallas_call | solution.py:363
  91.2 0.0 copy-start
  91.2 17.7 %all-to-all-done.3.piece_hbm = bf16[32,2,8,16,128]{4,3,2,1,0:T(8,128)(2,1)} async-done(((bf16[32,2,8,16,128]{4,3,2,1,0:T(8,128)(2,1)}), bf16[32,2,8,16,128]{4,3,2,1,0:T(8,128)(2,1)}, u32[]{:S(2)}, u32[]{:S(2)}) %all-to-all-start.3) | async-done | bytes 2097184 | tf_op jit(solution)/shard_map/all_to_all | solution.py:629
  108.9 5.0 %all-to-all-start.1 = ((bf16[32,2,8,16,128]{4,3,2,1,0:T(8,128)(2,1)}), bf16[32,2,8,16,128]{4,3,2,1,0:T(8,128)(2,1)}, u32[]{:S(2)}, u32[]{:S(2)}) async-start(bf16[32,2,8,16,128]{4,3,2,1,0:T(8,128)(2,1)} %grid_tile_1.1), calls=%async_computation.1 | async-start | bytes 4194304 | tf_op jit(solution)/shard_map/all_to_all | solution.py:629
  113.8 0.0 copy-done
  113.8 4.9 %gradient_first.1.before_ref = f32[2,8,256,128]{3,2,1,0:T(8,128)S(1)} custom-call(bf16[512,512]{1,0:T(8,128)(2,1)S(1)} %bitcast.8, bf16[32,2,8,16,128]{4,3,2,1,0:T(8,128)(2,1)} %all-to-all-done.3.piece_hbm, bf16[4,2,8,256,128]{4,3,2,1,0:T(8,128)(2,1)} %sens_hbm.3), custom_call_target="tpu_custom_call" | custom-call | tf_op jit(solution)/shard_map/gradient_first/pallas_call | solution.py:425
  118.7 23.8 %all-to-all-done.1.piece_hbm = bf16[32,2,8,16,128]{4,3,2,1,0:T(8,128)(2,1)} async-done(((bf16[32,2,8,16,128]{4,3,2,1,0:T(8,128)(2,1)}), bf16[32,2,8,16,128]{4,3,2,1,0:T(8,128)(2,1)}, u32[]{:S(2)}, u32[]{:S(2)}) %all-to-all-start.1) | async-done | bytes 2097184 | tf_op jit(solution)/shard_map/all_to_all | solution.py:629
  142.5 0.0 copy-start.3
  142.5 0.0 copy-start.4
  142.5 4.2 %gradient_last.1 = (bf16[2,8,64,128]{3,2,1,0:T(8,128)(2,1)}, bf16[2,8,64,128]{3,2,1,0:T(8,128)(2,1)}, bf16[2,8,64,128]{3,2,1,0:T(8,128)(2,1)}, bf16[2,8,64,128]{3,2,1,0:T(8,128)(2,1)}) custom-call(s32[1]{0:T(128)} %bitcast.position_ref, bf16[512,512]{1,0:T(8,128)(2,1)S(1)} %bitcast.9, bf16[32,2,8,16,128]{4,3,2,1,0:T(8,128)(2,1)} %all-to-all-done.1.piece_hbm, ...), custom_call_target="tpu_custom_call" | custom-call | tf_op jit(solution)/shard_map/gradient_last/pallas_call | solution.py:485
  146.7 0.0 copy-start.5
  146.8 4.0 %collective-permute-start = (bf16[2,8,64,128]{3,2,1,0:T(8,128)(2,1)}, bf16[2,8,64,128]{3,2,1,0:T(8,128)(2,1)S(1)}, u32[]{:S(2)}, u32[]{:S(2)}) collective-permute-start(bf16[2,8,64,128]{3,2,1,0:T(8,128)(2,1)} %get-tuple-element.22), channel_id=1, source_target_pairs={{0,64},{32,96},{64,0},{96,32},{1,65},{33,97},{65,1},{97,33},{2,66}... | collective-permute-start | bytes 786440 | tf_op jit(solution)/shard_map/ppermute | solution.py:636
  150.7 1.0 collective-permute-start.1
  151.7 2.2 %collective-permute-start.2 = (bf16[2,8,64,128]{3,2,1,0:T(8,128)(2,1)}, bf16[2,8,64,128]{3,2,1,0:T(8,128)(2,1)S(1)}, u32[]{:S(2)}, u32[]{:S(2)}) collective-permute-start(bf16[2,8,64,128]{3,2,1,0:T(8,128)(2,1)} %get-tuple-element.24), channel_id=1, source_target_pairs={{0,96},{32,0},{64,32},{96,64},{1,97},{33,1},{65,33},{97,65},{2,98}... | collective-permute-start | bytes 786440 | tf_op jit(solution)/shard_map/ppermute | solution.py:636
  154.0 0.0 copy-done.3
  154.0 0.0 copy-done.4
  154.0 1.3 target.1.base_ref
  155.2 2.9 %collective-permute-done.s1 = bf16[2,8,64,128]{3,2,1,0:T(8,128)(2,1)S(1)} collective-permute-done((bf16[2,8,64,128]{3,2,1,0:T(8,128)(2,1)}, bf16[2,8,64,128]{3,2,1,0:T(8,128)(2,1)S(1)}, u32[]{:S(2)}, u32[]{:S(2)}) %collective-permute-start) | collective-permute-done | bytes 262176 | tf_op jit(solution)/shard_map/ppermute | solution.py:636
  158.1 4.5 %collective-permute-done.1.s2 = bf16[2,8,64,128]{3,2,1,0:T(8,128)(2,1)S(1)} collective-permute-done((bf16[2,8,64,128]{3,2,1,0:T(8,128)(2,1)}, bf16[2,8,64,128]{3,2,1,0:T(8,128)(2,1)S(1)}, u32[]{:S(2)}, u32[]{:S(2)}) %collective-permute-start.1) | collective-permute-done | bytes 262176 | tf_op jit(solution)/shard_map/ppermute | solution.py:636
  162.7 0.8 collective-permute-done.2.s3
  163.4 0.0 copy-done.5
  163.4 1.3 update.1
Async XLA Ops:
  5.9 36.5 %all-to-all-start.2 = ((bf16[32,2,8,16,128]{4,3,2,1,0:T(8,128)(2,1)}), bf16[32,2,8,16,128]{4,3,2,1,0:T(8,128)(2,1)}, u32[]{:S(2)}, u32[]{:S(2)}) async-start(bf16[32,2,8,16,128]{4,3,2,1,0:T(8,128)(2,1)} %coil_forward_0.1), calls=%async_computation.2 | async-start | bytes 4194304 | tf_op jit(solution)/shard_map/all_to_all | solution.py:612
  13.4 5.7 %copy-start.7 = (bf16[1,24,128,512]{3,2,1,0:T(8,128)(2,1)S(1)}, bf16[1,24,128,512]{3,2,1,0:T(8,128)(2,1)}, u32[]{:S(2)}) copy-start(bf16[1,24,128,512]{3,2,1,0:T(8,128)(2,1)} %param.12) | copy-start | bytes 9437188
  24.3 22.1 %copy-start.1 = (bf16[512,512]{0,1:T(8,128)(2,1)S(1)}, bf16[512,512]{0,1:T(8,128)(2,1)}, u32[]{:S(2)}) copy-start(bf16[512,512]{0,1:T(8,128)(2,1)} %constant.11.clone) | copy-start | bytes 1572868
  24.3 22.1 %copy-start.2 = (bf16[512,512]{1,0:T(8,128)(2,1)S(1)}, bf16[512,512]{1,0:T(8,128)(2,1)}, u32[]{:S(2)}) copy-start(bf16[512,512]{1,0:T(8,128)(2,1)} %constant.21.refs_3_) | copy-start | bytes 1572868
  24.3 22.1 %copy-start.6 = (s32[1,24]{1,0:T(1,128)S(1)}, s32[1,24]{1,0:T(1,128)}, u32[]{:S(2)}) copy-start(s32[1,24]{1,0:T(1,128)} %refs_0_.5) | copy-start | bytes 292
  42.3 32.9 %all-to-all-start = ((bf16[32,2,8,16,128]{4,3,2,1,0:T(8,128)(2,1)}), bf16[32,2,8,16,128]{4,3,2,1,0:T(8,128)(2,1)S(1)}, u32[]{:S(2)}, u32[]{:S(2)}) async-start(bf16[32,2,8,16,128]{4,3,2,1,0:T(8,128)(2,1)} %coil_forward_1.1), calls=%async_computation | async-start | bytes 4194304 | tf_op jit(solution)/shard_map/all_to_all | solution.py:612
  75.2 33.6 %all-to-all-start.3 = ((bf16[32,2,8,16,128]{4,3,2,1,0:T(8,128)(2,1)}), bf16[32,2,8,16,128]{4,3,2,1,0:T(8,128)(2,1)}, u32[]{:S(2)}, u32[]{:S(2)}) async-start(bf16[32,2,8,16,128]{4,3,2,1,0:T(8,128)(2,1)} %grid_tile_0.1), calls=%async_computation.3 | async-start | bytes 4194304 | tf_op jit(solution)/shard_map/all_to_all | solution.py:629
  91.2 22.6 %copy-start = (bf16[512,512]{0,1:T(8,128)(2,1)S(1)}, bf16[512,512]{0,1:T(8,128)(2,1)}, u32[]{:S(2)}) copy-start(bf16[512,512]{0,1:T(8,128)(2,1)} %constant.10.clone) | copy-start | bytes 1572868
  108.9 33.7 %all-to-all-start.1 = ((bf16[32,2,8,16,128]{4,3,2,1,0:T(8,128)(2,1)}), bf16[32,2,8,16,128]{4,3,2,1,0:T(8,128)(2,1)}, u32[]{:S(2)}, u32[]{:S(2)}) async-start(bf16[32,2,8,16,128]{4,3,2,1,0:T(8,128)(2,1)} %grid_tile_1.1), calls=%async_computation.1 | async-start | bytes 4194304 | tf_op jit(solution)/shard_map/all_to_all | solution.py:629
  142.5 11.4 %copy-start.3 = (f32[2,8,64,128]{3,2,1,0:T(8,128)S(1)}, f32[2,8,64,128]{3,2,1,0:T(8,128)}, u32[]{:S(2)}) copy-start(f32[2,8,64,128]{3,2,1,0:T(8,128)} %dual_ref.3) | copy-start | bytes 1572868
  142.5 11.4 %copy-start.4 = (f32[2,8,64,128]{3,2,1,0:T(8,128)S(1)}, f32[2,8,64,128]{3,2,1,0:T(8,128)}, u32[]{:S(2)}) copy-start(f32[2,8,64,128]{3,2,1,0:T(8,128)} %aux_ref.1) | copy-start | bytes 1572868
  146.7 16.7 %copy-start.5 = (bf16[2,8,64,128]{3,2,1,0:T(8,128)(2,1)S(1)}, bf16[2,8,64,128]{3,2,1,0:T(8,128)(2,1)}, u32[]{:S(2)}) copy-start(bf16[2,8,64,128]{3,2,1,0:T(8,128)(2,1)} %get-tuple-element.21.s0) | copy-start | bytes 786436
  146.8 11.4 %collective-permute-start = (bf16[2,8,64,128]{3,2,1,0:T(8,128)(2,1)}, bf16[2,8,64,128]{3,2,1,0:T(8,128)(2,1)S(1)}, u32[]{:S(2)}, u32[]{:S(2)}) collective-permute-start(bf16[2,8,64,128]{3,2,1,0:T(8,128)(2,1)} %get-tuple-element.22), channel_id=1, source_target_pairs={{0,64},{32,96},{64,0},{96,32},{1,65},{33,97},{65,1},{97,33},{2,66}... | collective-permute-start | bytes 786440 | tf_op jit(solution)/shard_map/ppermute | solution.py:636
  150.7 11.9 %collective-permute-start.1 = (bf16[2,8,64,128]{3,2,1,0:T(8,128)(2,1)}, bf16[2,8,64,128]{3,2,1,0:T(8,128)(2,1)S(1)}, u32[]{:S(2)}, u32[]{:S(2)}) collective-permute-start(bf16[2,8,64,128]{3,2,1,0:T(8,128)(2,1)} %get-tuple-element.23), channel_id=1, source_target_pairs={{0,32},{32,64},{64,96},{96,0},{1,33},{33,65},{65,97},{97,1},{2,34}... | collective-permute-start | bytes 786440 | tf_op jit(solution)/shard_map/ppermute | solution.py:636
  151.7 11.7 %collective-permute-start.2 = (bf16[2,8,64,128]{3,2,1,0:T(8,128)(2,1)}, bf16[2,8,64,128]{3,2,1,0:T(8,128)(2,1)S(1)}, u32[]{:S(2)}, u32[]{:S(2)}) collective-permute-start(bf16[2,8,64,128]{3,2,1,0:T(8,128)(2,1)} %get-tuple-element.24), channel_id=1, source_target_pairs={{0,96},{32,0},{64,32},{96,64},{1,97},{33,1},{65,33},{97,65},{2,98}... | collective-permute-start | bytes 786440 | tf_op jit(solution)/shard_map/ppermute | solution.py:636

commit v6 on v5

--- a/solution.py
+++ b/solution.py
@@ -61,80 +61,73 @@
 DMA = pltpu.SemaphoreType.DMA
 
 
-def coil_kernel(chunk, table_hbm, sens_hbm, image_hbm, out_hbm, table, sens, image, out, sems, leave):
+def pack(even, odd, half):
+    low = lax.broadcasted_iota(jnp.int32, even.shape, 1) < Z // 2
+    if half == 0:
+        return jnp.where(low, even, pltpu.roll(odd, Z // 2, 1))
+    return jnp.where(low, pltpu.roll(even, Z // 2, 1), odd)
+
+
+def coil_kernel(half, table_hbm, sens_hbm, image_hbm, out_hbm, table, sens, image, out, sems, leave):
     stages = 2
     span = KYD // stages
 
-    def sens_copy(c, stage):
+    def copies(stage):
         rows = pl.ds(stage * span, span)
-        return pltpu.make_async_copy(
-            sens_hbm.at[chunk * PER + c, :, rows], sens.at[c, :, rows], sems.at[c, stage]
+        return (
+            pltpu.make_async_copy(image_hbm.at[:, rows], image.at[:, rows], sems.at[0, stage]),
+            pltpu.make_async_copy(sens_hbm.at[:, :, rows], sens.at[:, :, rows], sems.at[1, stage]),
         )
 
-    def image_copy(stage):
+    def leave_copy(stage):
         rows = pl.ds(stage * span, span)
-        return pltpu.make_async_copy(image_hbm.at[:, rows], image.at[:, rows], sems.at[PER, stage])
-
-    def leave_copy(c, stage):
-        rows = pl.ds(stage * span, span)
-        return pltpu.make_async_copy(out.at[:, c, rows], out_hbm.at[:, c, rows], leave.at[c, stage])
-
-    whole = pltpu.make_async_copy(table_hbm, table, leave.at[PER, 0])
+        return pltpu.make_async_copy(out.at[:, :, rows], out_hbm.at[:, :, rows], leave.at[stage])
+
+    whole = pltpu.make_async_copy(table_hbm, table, sems.at[2, 0])
     whole.start()
     for stage in range(stages):
-        image_copy(stage).start()
-        sens_copy(0, stage).start()
-    for c in range(1, PER):
-        for stage in range(stages):
-            sens_copy(c, stage).start()
+        for copy in copies(stage):
+            copy.start()
     whole.wait()
 
-    def one_coil(c, arrive):
-        for stage in range(stages):
-            arrive(c, stage)
-            for pair in range(span // 2):
-                first = stage * span + 2 * pair
-                parts = []
-                for x in (first, first + 1):
-                    s_re = sens[c, 0, x].astype(F32)
-                    s_im = sens[c, 1, x].astype(F32)
-                    m_re = image[0, x]
-                    m_im = image[1, x]
-                    c_re = (s_re * m_re - s_im * m_im).astype(BF)
-                    c_im = (s_re * m_im + s_im * m_re).astype(BF)
-                    parts.append(jnp.concatenate([c_re, c_im], 0))
-                data = jnp.concatenate(parts, 1)
-                result = jnp.dot(table[...], data, preferred_element_type=F32).astype(BF)
-                for i in range(2):
-                    out[:, c, first + i] = result[:, i * Z : (i + 1) * Z].reshape(TILES, 16, Z)
-            leave_copy(c, stage).start()
-
-    def arrive_staged(c, stage):
-        if c == 0:
-            image_copy(stage).wait()
-        sens_copy(c, stage).wait()
-
-    if chunk == 0:
-        for c in range(PER):
-            one_coil(c, arrive_staged)
-    else:
-        for stage in range(stages):
-            for c in range(PER):
-                arrive_staged(c, stage)
-
-        def rolled(c, carry):
-            one_coil(c, lambda c, stage: None)
-            return carry
-
-        lax.fori_loop(0, PER, rolled, 0)
-    for c in range(PER):
-        for stage in range(stages):
-            leave_copy(c, stage).wait()
-
-
-def coil_forward(chunk, table, sensitivity, image):
+    def row(x):
+        m_re = pack(image[0, x], image[0, x], half)
+        m_im = pack(image[1, x], image[1, x], half)
+        parts = []
+        for pair in range(PER):
+            s_re, s_im = (
+                pack(*(sens[2 * pair + k, part, x].astype(F32) for k in range(2)), half)
+                for part in range(2)
+            )
+            c_re = (s_re * m_re - s_im * m_im).astype(BF)
+            c_im = (s_re * m_im + s_im * m_re).astype(BF)
+            parts.append(jnp.concatenate([c_re, c_im], 0))
+        data = jnp.concatenate(parts, 1)
+        result = jnp.dot(table[...], data, preferred_element_type=F32).astype(BF)
+        for pair in range(PER):
+            out[:, pair, x] = result[:, pair * Z : (pair + 1) * Z].reshape(TILES, 16, Z)
+
+    for stage in range(stages):
+        for copy in copies(stage):
+            copy.wait()
+        if half == 0:
+            for x in range(stage * span, (stage + 1) * span):
+                row(x)
+        else:
+
+            def rolled(x, carry):
+                row(x)
+                return carry
+
+            lax.fori_loop(stage * span, (stage + 1) * span, rolled, 0)
+        leave_copy(stage).start()
+    for stage in range(stages):
+        leave_copy(stage).wait()
+
+
+def coil_forward(half, table, sensitivity, image):
     def kernel(*refs):
-        coil_kernel(chunk, *refs)
+        coil_kernel(half, *refs)
 
     return pl.pallas_call(
         kernel,
@@ -143,14 +136,14 @@
         out_specs=HBM,
         scratch_shapes=[
             pltpu.VMEM((2 * N, 2 * N), BF),
-            pltpu.VMEM((PER, 2, KYD, N, Z), BF),
+            pltpu.VMEM((NCOIL, 2, KYD, N, Z), BF),
             pltpu.VMEM((2, KYD, N, Z), F32),
             pltpu.VMEM((TILES, PER, KYD, 16, Z), BF),
-            DMA((PER + 1, 2)),
-            DMA((PER + 1, 2)),
+            DMA((3, 2)),
+            DMA((2,)),
         ],
-        compiler_params=pltpu.CompilerParams(vmem_limit_bytes=14 << 20),
-        name=f"coil_forward_{chunk}",
+        compiler_params=pltpu.CompilerParams(vmem_limit_bytes=16 << 20),
+        name=f"coil_forward_{half}",
     )(table, sensitivity, image)
 
 
@@ -171,11 +164,16 @@
         into(j).wait()
         slot = j % 2
         spread[slot] = samples[j].astype(F32).reshape(P_SIZE * 8, Z)
-        for coil in range(NCOIL):
+        for pair in range(PER):
             for part in range(2):
-                out[coil, j, :, part * Z : (part + 1) * Z] = spread[
-                    slot, pl.ds(2 * coil + part, P_SIZE, stride=8), :
-                ].astype(BF)
+                even, odd = (
+                    spread[slot, pl.ds(2 * (2 * pair + k) + part, P_SIZE, stride=8), :]
+                    for k in range(2)
+                )
+                for half in range(2):
+                    out[half * PER + pair, j, :, part * Z : (part + 1) * Z] = pack(
+                        even, odd, half
+                    ).astype(BF)
         back(j).start()
         return carry
 
@@ -206,13 +204,16 @@
     )(counts, samples)
 
 
+def conjugate(values, part):
+    return values if part == 0 else -values
+
+
 def grid_kernel(
     chunk,
     offsets_ref,
     counts_ref,
     piece_hbm,
-    forward_ref,
-    inverse_ref,
+    table_ref,
     blocks_hbm,
     turned_hbm,
     samples_hbm,
@@ -275,7 +276,7 @@
             ],
             1,
         )
-        result = jnp.dot(forward_ref[...], data, preferred_element_type=F32)
+        result = jnp.dot(table_ref[...], data, preferred_element_type=F32)
         for c in range(PER):
             for part in range(2):
                 total[2 * c + part, pl.ds(ky, N, stride=KYD), :] = result[
@@ -330,7 +331,9 @@
                 [
                     jnp.concatenate(
                         [
-                            total[2 * c + part, pl.ds(2 * pair + i, N, stride=KYD), :].astype(BF)
+                            conjugate(
+                                total[2 * c + part, pl.ds(2 * pair + i, N, stride=KYD), :], part
+                            ).astype(BF)
                             for part in range(2)
                         ],
                         0,
@@ -339,12 +342,12 @@
                 ],
                 1,
             )
-            result = jnp.dot(inverse_ref[...], data, preferred_element_type=F32)
+            result = jnp.dot(table_ref[...], data, preferred_element_type=F32)
             for i in range(2):
                 for part in range(2):
-                    spread[c, pl.ds(2 * (2 * pair + i) + part, N, stride=2 * KYD), :] = result[
-                        part * N : (part + 1) * N, i * Z : (i + 1) * Z
-                    ]
+                    spread[c, pl.ds(2 * (2 * pair + i) + part, N, stride=2 * KYD), :] = conjugate(
+                        result[part * N : (part + 1) * N, i * Z : (i + 1) * Z], part
+                    )
             return carry
 
         lax.fori_loop(0, KYD // 2, inverse_rows, 0)
@@ -356,14 +359,14 @@
         copy.wait()
 
 
-def grid_tile(chunk, offsets, counts, piece, forward, inverse, blocks, turned, samples):
+def grid_tile(chunk, offsets, counts, piece, table, blocks, turned, samples):
     def kernel(*refs):
         grid_kernel(chunk, *refs)
 
     return pl.pallas_call(
         kernel,
         out_shape=hbm((TILES, PER, KYD, 16, Z), BF),
-        in_specs=[SMEM, SMEM, HBM if chunk == 0 else VMEM, VMEM, VMEM, HBM, HBM, HBM],
+        in_specs=[SMEM, SMEM, HBM if chunk == 0 else VMEM, VMEM, HBM, HBM, HBM],
         out_specs=HBM,
         scratch_shapes=[
             pltpu.VMEM((TILES, PER, KYD, 16, Z) if chunk == 0 else (16, Z), BF),
@@ -379,33 +382,44 @@
         ],
         compiler_params=pltpu.CompilerParams(vmem_limit_bytes=34 << 20),
         name=f"grid_tile_{chunk}",
-    )(offsets, counts, piece, forward, inverse, blocks, turned, samples)
-
-
-def combine(adjoint, sens, x, before):
-    g_re, g_im = before
-    for c in range(PER):
-        lanes = slice(c * Z, (c + 1) * Z)
+    )(offsets, counts, piece, table, blocks, turned, samples)
+
+
+def combine(adjoint, packed):
+    g_re = g_im = None
+    for pair in range(PER):
+        lanes = slice(pair * Z, (pair + 1) * Z)
         a_re = adjoint[:N, lanes]
         a_im = adjoint[N:, lanes]
-        s_re = sens[c, 0, x].astype(F32)
-        s_im = sens[c, 1, x].astype(F32)
+        s_re, s_im = packed[pair]
         t_re = s_re * a_re + s_im * a_im
         t_im = s_re * a_im - s_im * a_re
         g_re = t_re if g_re is None else g_re + t_re
         g_im = t_im if g_im is None else g_im + t_im
-    return g_re, g_im
+    low = lax.broadcasted_iota(jnp.int32, g_re.shape, 1) < Z // 2
+    return jnp.where(low, g_re + pltpu.roll(g_re, Z // 2, 1), g_im + pltpu.roll(g_im, Z // 2, 1))
 
 
 def adjoint_row(table_ref, piece, x):
-    data = jnp.concatenate([piece[:, c, x].reshape(2 * N, Z) for c in range(PER)], 1)
+    data = jnp.concatenate([piece[:, pair, x].reshape(2 * N, Z) for pair in range(PER)], 1)
     return jnp.dot(table_ref[...], data, preferred_element_type=F32).astype(BF).astype(F32)
 
 
-def gradient_first_kernel(table_ref, piece_hbm, sens_hbm, out_ref, piece, sens, sems):
+def share_copies(position, out, shares, rows, sems):
+    return [
+        pltpu.make_async_copy(
+            out.at[lax.rem(position + k, NCOIL), rows], shares[k].at[rows], sems.at[k]
+        )
+        for k in range(NCOIL)
+    ]
+
+
+def gradient_first_kernel(position_ref, table_ref, piece_hbm, sens_hbm, *rest):
+    shares = rest[:NCOIL]
+    later_hbm, piece, sens, later, out, arrive, sems, last = rest[NCOIL:]
     copies = [
-        pltpu.make_async_copy(piece_hbm, piece, sems.at[0]),
-        pltpu.make_async_copy(sens_hbm.at[pl.ds(0, PER)], sens, sems.at[1]),
+        pltpu.make_async_copy(piece_hbm, piece, arrive.at[0]),
+        pltpu.make_async_copy(sens_hbm, sens, arrive.at[1]),
     ]
     for copy in copies:
         copy.start()
@@ -413,90 +427,95 @@
         copy.wait()
 
     def row(x, carry):
-        g_re, g_im = combine(adjoint_row(table_ref, piece, x), sens, x, (None, None))
-        out_ref[0, x] = g_re
-        out_ref[1, x] = g_im
+        packed = []
+        for pair in range(PER):
+            both = []
+            for part in range(2):
+                even, odd = (sens[2 * pair + k, part, x].astype(F32) for k in range(2))
+                both.append(pack(even, odd, 0))
+                later[pair, part, x] = pack(even, odd, 1).astype(BF)
+            packed.append(both)
+        gradient = combine(adjoint_row(table_ref, piece, x), packed)
+        out[:, x] = gradient.astype(BF).reshape(NCOIL, N // NCOIL, Z)
         return carry
 
     lax.fori_loop(0, KYD, row, 0)
-
-
-def gradient_first(table, piece, sensitivity):
+    leaving = share_copies(position_ref[0], out, shares, pl.ds(0, KYD), sems)
+    leaving.append(pltpu.make_async_copy(later, later_hbm, last.at[0]))
+    for copy in leaving:
+        copy.start()
+    for copy in leaving:
+        copy.wait()
+
+
+def gradient_first(position, table, piece, sensitivity):
+    share = (KYD, N // NCOIL, Z)
+    packed = (PER, 2, KYD, N, Z)
     return pl.pallas_call(
         gradient_first_kernel,
-        out_shape=jax.ShapeDtypeStruct((2, KYD, N, Z), F32),
-        in_specs=[VMEM, HBM, HBM],
-        out_specs=VMEM,
+        out_shape=(hbm(share, BF),) * NCOIL + (hbm(packed, BF),),
+        in_specs=[SMEM, VMEM, HBM, HBM],
+        out_specs=(HBM,) * (NCOIL + 1),
         scratch_shapes=[
             pltpu.VMEM((TILES, PER, KYD, 16, Z), BF),
-            pltpu.VMEM((PER, 2, KYD, N, Z), BF),
+            pltpu.VMEM((NCOIL, 2, KYD, N, Z), BF),
+            pltpu.VMEM(packed, BF),
+            pltpu.VMEM((NCOIL,) + share, BF),
             DMA((2,)),
+            DMA((NCOIL,)),
+            DMA((1,)),
         ],
-        compiler_params=pltpu.CompilerParams(vmem_limit_bytes=12 << 20),
+        compiler_params=pltpu.CompilerParams(vmem_limit_bytes=14 << 20),
         name="gradient_first",
-    )(table, piece, sensitivity)
-
-
-def gradient_last_kernel(position_ref, table_ref, piece_hbm, sens_hbm, before_ref, *rest):
+    )(position, table, piece, sensitivity)
+
+
+def gradient_last_kernel(position_ref, table_ref, piece, sens_hbm, *rest):
     shares = rest[:NCOIL]
-    piece, sens, out, arrive, sems = rest[NCOIL:]
-    position = position_ref[0]
+    sens, out, arrive, sems = rest[NCOIL:]
     span = KYD // 2
 
     def arrivals(stage):
         rows = pl.ds(stage * span, span)
-        return (
-            pltpu.make_async_copy(
-                piece_hbm.at[:, :, rows], piece.at[:, :, rows], arrive.at[0, stage]
-            ),
-            pltpu.make_async_copy(
-                sens_hbm.at[pl.ds(PER, PER), :, rows], sens.at[:, :, rows], arrive.at[1, stage]
-            ),
+        return pltpu.make_async_copy(
+            sens_hbm.at[:, :, rows], sens.at[:, :, rows], arrive.at[stage]
         )
 
-    def leave(k, stage):
+    for stage in range(2):
+        arrivals(stage).start()
+    leaving = []
+    for stage in range(2):
+        arrivals(stage).wait()
+        for x in range(stage * span, (stage + 1) * span):
+            packed = [
+                [sens[pair, part, x].astype(F32) for part in range(2)] for pair in range(PER)
+            ]
+            gradient = combine(adjoint_row(table_ref, piece, x), packed)
+            out[:, x] = gradient.astype(BF).reshape(NCOIL, N // NCOIL, Z)
         rows = pl.ds(stage * span, span)
-        target = lax.rem(position + k, NCOIL)
-        return pltpu.make_async_copy(
-            out.at[target, :, rows], shares[k].at[:, rows], sems.at[k, stage]
-        )
-
-    for stage in range(2):
-        for copy in arrivals(stage):
+        for copy in share_copies(position_ref[0], out, shares, rows, sems.at[stage]):
             copy.start()
-    for stage in range(2):
-        for copy in arrivals(stage):
-            copy.wait()
-        for x in range(stage * span, (stage + 1) * span):
-            g_re, g_im = combine(
-                adjoint_row(table_ref, piece, x), sens, x, (before_ref[0, x], before_ref[1, x])
-            )
-            out[:, 0, x] = g_re.astype(BF).reshape(NCOIL, N // NCOIL, Z)
-            out[:, 1, x] = g_im.astype(BF).reshape(NCOIL, N // NCOIL, Z)
-        for k in range(NCOIL):
-            leave(k, stage).start()
-    for stage in range(2):
-        for k in range(NCOIL):
-            leave(k, stage).wait()
-
-
-def gradient_last(position, table, piece, sens, before):
-    share = (2, KYD, N // NCOIL, Z)
+            leaving.append(copy)
+    for copy in leaving:
+        copy.wait()
+
+
+def gradient_last(position, table, piece, packed):
+    share = (KYD, N // NCOIL, Z)
     return pl.pallas_call(
         gradient_last_kernel,
         out_shape=(hbm(share, BF),) * NCOIL,
-        in_specs=[SMEM, VMEM, HBM, HBM, VMEM],
+        in_specs=[SMEM, VMEM, VMEM, HBM],
         out_specs=(HBM,) * NCOIL,
         scratch_shapes=[
-            pltpu.VMEM((TILES, PER, KYD, 16, Z), BF),
             pltpu.VMEM((PER, 2, KYD, N, Z), BF),
             pltpu.VMEM((NCOIL,) + share, BF),
-            DMA((2, 2)),
-            DMA((NCOIL, 2)),
+            DMA((2,)),
+            DMA((2, NCOIL)),
         ],
-        compiler_params=pltpu.CompilerParams(vmem_limit_bytes=12 << 20),
+        compiler_params=pltpu.CompilerParams(vmem_limit_bytes=8 << 20),
         name="gradient_last",
-    )(position, table, piece, sens, before)
+    )(position, table, piece, packed)
 
 
 def haar_rows(top, low):
@@ -541,23 +560,32 @@
     )(position, image, auxiliary, scaled_dual)
 
 
-def update_kernel(
-    base_ref, s0, s1, s2, s3, dual_ref, image_hbm, aux_hbm, dual_hbm, image, aux, dual, sems
-):
+def update_kernel(base_ref, *rest):
+    halves = (rest[:NCOIL], rest[NCOIL : 2 * NCOIL])
+    dual_ref, image_hbm, aux_hbm, dual_hbm, image, aux, dual, sems = rest[2 * NCOIL :]
+    low = lax.broadcasted_iota(jnp.int32, (N // NCOIL, Z), 1) < Z // 2
     leaving = []
     for m in range(KYD // 2):
+        rows = ([], [])
+        for x in (2 * m, 2 * m + 1):
+            sums = []
+            for shares in halves:
+                total = shares[0][x].astype(F32)
+                for share in shares[1:]:
+                    total = total + share[x].astype(F32)
+                sums.append(total)
+            gradient = (
+                jnp.where(low, sums[0], pltpu.roll(sums[1], Z // 2, 1)),
+                jnp.where(low, pltpu.roll(sums[0], Z // 2, 1), sums[1]),
+            )
+            for part in range(2):
+                value = base_ref[part, x] - step_size * gradient[part]
+                image[part, x] = value
+                rows[part].append(value)
         coeffs = []
         for part in range(2):
-            rows = []
-            for x in (2 * m, 2 * m + 1):
-                gradient = s0[part, x].astype(F32)
-                for share in (s1, s2, s3):
-                    gradient = gradient + share[part, x].astype(F32)
-                value = base_ref[part, x] - step_size * gradient
-                image[part, x] = value
-                rows.append(value)
-            top, low = haar_rows(*rows)
-            coeffs.append((top + dual_ref[part, 2 * m], low + dual_ref[part, 2 * m + 1]))
+            top, bottom = haar_rows(*rows[part])
+            coeffs.append((top + dual_ref[part, 2 * m], bottom + dual_ref[part, 2 * m + 1]))
         for i in range(2):
             c_re = coeffs[0][i]
             c_im = coeffs[1][i]
@@ -568,8 +596,8 @@
                 aux[part, 2 * m + i] = kept
                 dual[part, 2 * m + i] = value - kept
         pair = pl.ds(2 * m, 2)
-        for k, (near, far) in enumerate(((image, image_hbm), (aux, aux_hbm), (dual, dual_hbm))):
-            copy = pltpu.make_async_copy(near.at[:, pair], far.at[:, pair], sems.at[k, m])
+        for k, (held, place) in enumerate(((image, image_hbm), (aux, aux_hbm), (dual, dual_hbm))):
+            copy = pltpu.make_async_copy(held.at[:, pair], place.at[:, pair], sems.at[k, m])
             copy.start()
             leaving.append(copy)
     for copy in leaving:
@@ -581,7 +609,7 @@
     return pl.pallas_call(
         update_kernel,
         out_shape=(shape, shape, shape),
-        in_specs=[VMEM] * (NCOIL + 2),
+        in_specs=[VMEM] * (2 * NCOIL + 2),
         out_specs=(HBM, HBM, HBM),
         scratch_shapes=[pltpu.VMEM(scaled_dual.shape, F32)] * 3 + [DMA((3, KYD // 2))],
         compiler_params=pltpu.CompilerParams(vmem_limit_bytes=8 << 20),
@@ -589,12 +617,19 @@
     )(base, *shares, scaled_dual)
 
 
+def over_planes(shares):
+    own, *others = shares
+    got = [own]
+    for k in (2, 1, 3):
+        ring = [(i, (i + k) % NCOIL) for i in range(NCOIL)]
+        got.append(lax.ppermute(others[k - 1], "coil", ring))
+    return got
+
+
 def body(image, sensitivity, blocks, samples, offsets, counts, auxiliary, scaled_dual):
     along_y, along_x = real_tables()
     y_forward, x_forward = jnp.asarray(along_y), jnp.asarray(along_x)
-    y_kept, x_kept = lax.optimization_barrier((y_forward, x_forward))
-    y_inverse = y_kept.T
-    x_inverse = x_kept.T
+    y_inverse = lax.optimization_barrier(y_forward).T
 
     image, sensitivity = in_hbm(image), in_hbm(sensitivity)
     y_forward = in_hbm(y_forward)
@@ -606,8 +641,8 @@
     for chunk in chunks:
         half = coil_forward(chunk, y_forward, sensitivity, image)
         if chunk == 1:
-            half, turned, by_coil, y_inverse, x_inverse = lax.optimization_barrier(
-                (half, turned, by_coil, y_inverse, x_inverse)
+            half, turned, by_coil, y_inverse = lax.optimization_barrier(
+                (half, turned, by_coil, y_inverse)
             )
         piece = lax.all_to_all(half, "slab", 0, 0, tiled=True)
         pieces.append(piece)
@@ -621,20 +656,15 @@
             counts,
             in_hbm(pieces[chunk]) if chunk == 0 else pieces[chunk],
             x_forward,
-            x_inverse,
             in_hbm(blocks[0]),
             in_hbm(turned),
             in_hbm(by_coil),
         )
         backs.append(lax.all_to_all(back, "slab", 0, 0, tiled=True))
-    first, last = backs
-    before = gradient_first(y_inverse, in_hbm(first), sensitivity)
-    own, *others = gradient_last(position, y_inverse, in_hbm(last), sensitivity, before)
-    shares = [own]
-    for k in (2, 1, 3):
-        ring = [(i, (i + k) % NCOIL) for i in range(NCOIL)]
-        shares.append(lax.ppermute(others[k - 1], "coil", ring))
-    return update_step(base, shares, scaled_dual)
+    *shares, packed = gradient_first(position, y_inverse, in_hbm(backs[0]), sensitivity)
+    early = over_planes(shares)
+    late = over_planes(gradient_last(position, y_inverse, backs[1], in_hbm(packed)))
+    return update_step(base, early + late, scaled_dual)
 
 
 def solution(mesh):

time: 166 us -> 159 us (0.958)
  waiting for transfers between devices: 83.8 us -> 66.1 us
  starting transfers between devices: 28.5 us -> 34.9 us
  Pallas kernels: 48.1 us -> 53.3 us
    all_to_all x2, waiting for transfers between devices: 41.5 us -> 31.5 us  [body(): backs.append(lax.all_to_all(back, 'slab', 0, 0, tiled=True))]
    ppermute x3 -> x6, starting transfers between devices: 7.19 us -> 14.4 us  [over_planes(): got.append(lax.ppermute(others[k - 1], 'coil', ring))]
    ppermute x3 -> x6, waiting for transfers between devices: 8.19 us -> 2.51 us  [over_planes(): got.append(lax.ppermute(others[k - 1], 'coil', ring))]
    pallas_call x1, Pallas kernels: 4.87 us -> 7.55 us  [gradient_first(): pl.pallas_call(gradient_first_kernel, out_shape=(hbm(share, BF),) * NCOIL...]
    pallas_call x2, Pallas kernels: 10.3 us -> 12.6 us  [coil_forward(): pl.pallas_call(kernel, out_shape=hbm((TILES, PER, KYD, 16, Z), BF), in_sp...]
    all_to_all x2, waiting for transfers between devices: 34.2 us -> 32 us  [body(): piece = lax.all_to_all(half, 'slab', 0, 0, tiled=True)]
  transfers between devices with their start and end apart: 7 -> 10, of which waited for: 7 -> 6; matrix products, arithmetic and copies ran while one was open for 2% -> 2% of each run, Pallas kernels for 23% -> 29%
where the time goes in v6:
time: 159 us
  waiting for transfers between devices  66.1 us (42%)
  Pallas kernels  53.3 us (34%)
  starting transfers between devices  34.9 us (22%)
  local copies, waits for them, and re-layouts  2.9 us (2%)
  between operations  1.64 us (1%)
    all_to_all x2, waiting for transfers between devices, body(): piece = lax.all_to_all(half, 'slab', 0, 0, tiled=True)  32 us
    all_to_all x2, waiting for transfers between devices, body(): backs.append(lax.all_to_all(back, 'slab', 0, 0, tiled=True))  31.5 us
    pallas_call x2, Pallas kernels, grid_tile(): pl.pallas_call(kernel, out_shape=hbm((TILES, PER, KYD, 16, Z), BF), in_sp...  24 us
    ppermute x6, starting transfers between devices, over_planes(): got.append(lax.ppermute(others[k - 1], 'coil', ring))  14.4 us
    pallas_call x2, Pallas kernels, coil_forward(): pl.pallas_call(kernel, out_shape=hbm((TILES, PER, KYD, 16, Z), BF), in_sp...  12.6 us
    all_to_all x2, starting transfers between devices, body(): piece = lax.all_to_all(half, 'slab', 0, 0, tiled=True)  11.6 us
    all_to_all x2, starting transfers between devices, body(): backs.append(lax.all_to_all(back, 'slab', 0, 0, tiled=True))  8.95 us
    pallas_call x1, Pallas kernels, gradient_first(): pl.pallas_call(gradient_first_kernel, out_shape=(hbm(share, BF),) * NCOIL...  7.55 us
  transfers between devices with their start and end apart: 10, of which 6 were waited for; matrix products, arithmetic and copies ran while one was open for 2% of the time, Pallas kernels for 29%

profile of v6, /device:TPU:0, one launch (start us, length us, event | category | flops | bytes accessed | tf_op | source)
XLA Modules:
  0.0 158.8 jit_solution(7495354169131106202)
XLA Ops:
  0.6 5.5 %coil_forward_0.1 = bf16[32,2,8,16,128]{4,3,2,1,0:T(8,128)(2,1)} custom-call(bf16[512,512]{1,0:T(8,128)(2,1)} %constant.20.refs_0_, bf16[4,2,8,256,128]{4,3,2,1,0:T(8,128)(2,1)} %sens_hbm.1, f32[2,8,256,128]{3,2,1,0:T(8,128)} %refs_2_.3), custom_call_target="tpu_custom_call" | custom-call | tf_op jit(solution)/shard_map/coil_forward_0/pallas_call | solution.py:132
  6.1 7.5 %all-to-all-start = ((bf16[32,2,8,16,128]{4,3,2,1,0:T(8,128)(2,1)}), bf16[32,2,8,16,128]{4,3,2,1,0:T(8,128)(2,1)}, u32[]{:S(2)}, u32[]{:S(2)}) async-start(bf16[32,2,8,16,128]{4,3,2,1,0:T(8,128)(2,1)} %coil_forward_0.1), calls=%async_computation | async-start | bytes 4194304 | tf_op jit(solution)/shard_map/all_to_all | solution.py:647
  13.7 0.0 copy-start.7
  13.7 7.1 %coil_forward_1.1 = bf16[32,2,8,16,128]{4,3,2,1,0:T(8,128)(2,1)} custom-call(bf16[512,512]{1,0:T(8,128)(2,1)} %constant.20.refs_0_, bf16[4,2,8,256,128]{4,3,2,1,0:T(8,128)(2,1)} %sens_hbm.1, f32[2,8,256,128]{3,2,1,0:T(8,128)} %refs_2_.3), custom_call_target="tpu_custom_call" | custom-call | tf_op jit(solution)/shard_map/coil_forward_1/pallas_call | solution.py:132
  21.5 0.0 copy-done.7
  21.5 2.9 %copy.14 = bf16[1,24,128,512]{2,3,1,0:T(8,128)(2,1)} copy(bf16[1,24,128,512]{3,2,1,0:T(8,128)(2,1)S(1)} %copy-done.7) | data formatting | bytes 6291456 | tf_op args[2]
  24.3 2.3 %samples_by_coil.1.refs_6_ = bf16[4,24,128,256]{3,2,1,0:T(8,128)(2,1)} custom-call(s32[1]{0:T(128)S(6)} %copy.19.counts_ref.refs_1_, bf16[24,128,8,128]{3,2,1,0:T(8,128)(2,1)} %bitcast.13), custom_call_target="tpu_custom_call" | custom-call | tf_op jit(solution)/shard_map/samples_by_coil/pallas_call | solution.py:190
  26.6 0.0 copy-start
  26.6 0.0 copy-start.6
  26.6 16.0 %all-to-all-done.refs_2_ = bf16[32,2,8,16,128]{4,3,2,1,0:T(8,128)(2,1)} async-done(((bf16[32,2,8,16,128]{4,3,2,1,0:T(8,128)(2,1)}), bf16[32,2,8,16,128]{4,3,2,1,0:T(8,128)(2,1)}, u32[]{:S(2)}, u32[]{:S(2)}) %all-to-all-start) | async-done | bytes 2097184 | tf_op jit(solution)/shard_map/all_to_all | solution.py:647
  42.6 4.0 %all-to-all-start.2 = ((bf16[32,2,8,16,128]{4,3,2,1,0:T(8,128)(2,1)}), bf16[32,2,8,16,128]{4,3,2,1,0:T(8,128)(2,1)S(1)}, u32[]{:S(2)}, u32[]{:S(2)}) async-start(bf16[32,2,8,16,128]{4,3,2,1,0:T(8,128)(2,1)} %coil_forward_1.1), calls=%async_computation.2 | async-start | bytes 4194304 | tf_op jit(solution)/shard_map/all_to_all | solution.py:647
  46.6 0.0 copy-done
  46.6 0.0 copy-done.6
  46.6 12.8 %grid_tile_0.1 = bf16[32,2,8,16,128]{4,3,2,1,0:T(8,128)(2,1)} custom-call(s32[1,24]{1,0:T(1,128)S(1)} %copy-done.6, s32[1]{0:T(128)S(6)} %copy.19.counts_ref.refs_1_, bf16[32,2,8,16,128]{4,3,2,1,0:T(8,128)(2,1)} %all-to-all-done.refs_2_, bf16[512,512]{1,0:T(8,128)(2,1)S(1)} %copy-done, bf16[24,128,512]{2,1,0:T(8,128)(2,1)} %bitcast.9, ...), custom_call_target="tpu_custom_call" | custom-call | tf_op jit(solution)/shard_map/grid_tile_0/pallas_call | solution.py:366
  59.4 16.1 %all-to-all-done.2.refs_2_ = bf16[32,2,8,16,128]{4,3,2,1,0:T(8,128)(2,1)S(1)} async-done(((bf16[32,2,8,16,128]{4,3,2,1,0:T(8,128)(2,1)}), bf16[32,2,8,16,128]{4,3,2,1,0:T(8,128)(2,1)S(1)}, u32[]{:S(2)}, u32[]{:S(2)}) %all-to-all-start.2) | async-done | bytes 2097184 | tf_op jit(solution)/shard_map/all_to_all | solution.py:647
  75.5 4.8 %all-to-all-start.1 = ((bf16[32,2,8,16,128]{4,3,2,1,0:T(8,128)(2,1)}), bf16[32,2,8,16,128]{4,3,2,1,0:T(8,128)(2,1)}, u32[]{:S(2)}, u32[]{:S(2)}) async-start(bf16[32,2,8,16,128]{4,3,2,1,0:T(8,128)(2,1)} %grid_tile_0.1), calls=%async_computation.1 | async-start | bytes 4194304 | tf_op jit(solution)/shard_map/all_to_all | solution.py:663
  80.3 11.3 %grid_tile_1.1 = bf16[32,2,8,16,128]{4,3,2,1,0:T(8,128)(2,1)} custom-call(s32[1,24]{1,0:T(1,128)S(1)} %copy-done.6, s32[1]{0:T(128)S(6)} %copy.19.counts_ref.refs_1_, bf16[32,2,8,16,128]{4,3,2,1,0:T(8,128)(2,1)S(1)} %all-to-all-done.2.refs_2_, bf16[512,512]{1,0:T(8,128)(2,1)S(1)} %copy-done, bf16[24,128,512]{2,1,0:T(8,128)(2,1)} %bitcast.10, ...), custom_call_target="tpu_custom_call" | custom-call | tf_op jit(solution)/shard_map/grid_tile_1/pallas_call | solution.py:366
  91.5 0.0 copy-start.2
  91.6 17.6 %all-to-all-done.1.piece_hbm = bf16[32,2,8,16,128]{4,3,2,1,0:T(8,128)(2,1)} async-done(((bf16[32,2,8,16,128]{4,3,2,1,0:T(8,128)(2,1)}), bf16[32,2,8,16,128]{4,3,2,1,0:T(8,128)(2,1)}, u32[]{:S(2)}, u32[]{:S(2)}) %all-to-all-start.1) | async-done | bytes 2097184 | tf_op jit(solution)/shard_map/all_to_all | solution.py:663
  109.2 4.2 %all-to-all-start.3 = ((bf16[32,2,8,16,128]{4,3,2,1,0:T(8,128)(2,1)}), bf16[32,2,8,16,128]{4,3,2,1,0:T(8,128)(2,1)S(1)}, u32[]{:S(2)}, u32[]{:S(2)}) async-start(bf16[32,2,8,16,128]{4,3,2,1,0:T(8,128)(2,1)} %grid_tile_1.1), calls=%async_computation.3 | async-start | bytes 4194304 | tf_op jit(solution)/shard_map/all_to_all | solution.py:663
  113.4 0.0 copy-done.2
  113.4 7.6 %gradient_first.1 = (bf16[8,64,128]{2,1,0:T(8,128)(2,1)}, bf16[8,64,128]{2,1,0:T(8,128)(2,1)}, bf16[8,64,128]{2,1,0:T(8,128)(2,1)}, bf16[8,64,128]{2,1,0:T(8,128)(2,1)}, bf16[2,2,8,256,128]{4,3,2,1,0:T(8,128)(2,1)}) custom-call(s32[1]{0:T(128)} %bitcast.position_ref, bf16[512,512]{1,0:T(8,128)(2,1)S(1)} %bitcast.7, ...), custom_call_target="tpu_custom_call" | custom-call | tf_op jit(solution)/shard_map/gradient_first/pallas_call | solution.py:454
  120.9 4.0 %collective-permute-start = (bf16[8,64,128]{2,1,0:T(8,128)(2,1)}, bf16[8,64,128]{2,1,0:T(8,128)(2,1)S(1)}, u32[]{:S(2)}, u32[]{:S(2)}) collective-permute-start(bf16[8,64,128]{2,1,0:T(8,128)(2,1)} %get-tuple-element.20), channel_id=1, source_target_pairs={{0,64},{32,96},{64,0},{96,32},{1,65},{33,97},{65,1},{97,33},{2,66}... | collective-permute-start | bytes 393224 | tf_op jit(solution)/shard_map/ppermute | solution.py:625
  124.9 1.0 collective-permute-start.1
  125.9 2.2 %collective-permute-start.2 = (bf16[8,64,128]{2,1,0:T(8,128)(2,1)}, bf16[8,64,128]{2,1,0:T(8,128)(2,1)S(1)}, u32[]{:S(2)}, u32[]{:S(2)}) collective-permute-start(bf16[8,64,128]{2,1,0:T(8,128)(2,1)} %get-tuple-element.22), channel_id=1, source_target_pairs={{0,96},{32,0},{64,32},{96,64},{1,97},{33,1},{65,33},{97,65},{2,98}... | collective-permute-start | bytes 393224 | tf_op jit(solution)/shard_map/ppermute | solution.py:625
  128.1 13.9 %all-to-all-done.3.piece = bf16[32,2,8,16,128]{4,3,2,1,0:T(8,128)(2,1)S(1)} async-done(((bf16[32,2,8,16,128]{4,3,2,1,0:T(8,128)(2,1)}), bf16[32,2,8,16,128]{4,3,2,1,0:T(8,128)(2,1)S(1)}, u32[]{:S(2)}, u32[]{:S(2)}) %all-to-all-start.3) | async-done | bytes 2097184 | tf_op jit(solution)/shard_map/all_to_all | solution.py:663
  142.1 0.0 copy-start.1
  142.1 0.0 copy-start.3
  142.1 4.1 %gradient_last.1 = (bf16[8,64,128]{2,1,0:T(8,128)(2,1)}, bf16[8,64,128]{2,1,0:T(8,128)(2,1)}, bf16[8,64,128]{2,1,0:T(8,128)(2,1)}, bf16[8,64,128]{2,1,0:T(8,128)(2,1)}) custom-call(s32[1]{0:T(128)} %bitcast.position_ref, bf16[512,512]{1,0:T(8,128)(2,1)S(1)} %bitcast.8, bf16[32,2,8,16,128]{4,3,2,1,0:T(8,128)(2,1)S(1)} %all-to-all-done.3.piece, ...), custom_call_target="tpu_custom_call" | custom-call | tf_op jit(solution)/shard_map/gradient_last/pallas_call | solution.py:505
  146.2 0.0 copy-start.4
  146.2 0.0 copy-start.5
  146.2 4.0 %collective-permute-start.3 = (bf16[8,64,128]{2,1,0:T(8,128)(2,1)}, bf16[8,64,128]{2,1,0:T(8,128)(2,1)S(1)}, u32[]{:S(2)}, u32[]{:S(2)}) collective-permute-start(bf16[8,64,128]{2,1,0:T(8,128)(2,1)} %get-tuple-element.26), channel_id=1, source_target_pairs={{0,64},{32,96},{64,0},{96,32},{1,65},{33,97},{65,1},{97,33},{2,66}... | collective-permute-start | bytes 393224 | tf_op jit(solution)/shard_map/ppermute | solution.py:625
  150.2 1.0 collective-permute-start.4
  151.2 0.0 collective-permute-done.rest_1_
  151.2 2.2 %collective-permute-start.5 = (bf16[8,64,128]{2,1,0:T(8,128)(2,1)}, bf16[8,64,128]{2,1,0:T(8,128)(2,1)S(1)}, u32[]{:S(2)}, u32[]{:S(2)}) collective-permute-start(bf16[8,64,128]{2,1,0:T(8,128)(2,1)} %get-tuple-element.28), channel_id=1, source_target_pairs={{0,96},{32,0},{64,32},{96,64},{1,97},{33,1},{65,33},{97,65},{2,98}... | collective-permute-start | bytes 393224 | tf_op jit(solution)/shard_map/ppermute | solution.py:625
  153.4 0.0 copy-done.1
  153.4 0.0 copy-done.3
  153.4 1.3 target.1.base_ref
  154.7 0.0 collective-permute-done.1.rest_2_
  154.7 0.0 collective-permute-done.2.rest_3_
  154.8 0.0 collective-permute-done.3.rest_5_
  154.8 2.2 %collective-permute-done.4.rest_6_ = bf16[8,64,128]{2,1,0:T(8,128)(2,1)S(1)} collective-permute-done((bf16[8,64,128]{2,1,0:T(8,128)(2,1)}, bf16[8,64,128]{2,1,0:T(8,128)(2,1)S(1)}, u32[]{:S(2)}, u32[]{:S(2)}) %collective-permute-start.4) | collective-permute-done | bytes 131104 | tf_op jit(solution)/shard_map/ppermute | solution.py:625
  157.0 0.3 collective-permute-done.5.rest_7_
  157.3 0.0 copy-done.4
  157.3 0.0 copy-done.5
  157.3 1.4 update.1
Async XLA Ops:
  6.1 36.5 %all-to-all-start = ((bf16[32,2,8,16,128]{4,3,2,1,0:T(8,128)(2,1)}), bf16[32,2,8,16,128]{4,3,2,1,0:T(8,128)(2,1)}, u32[]{:S(2)}, u32[]{:S(2)}) async-start(bf16[32,2,8,16,128]{4,3,2,1,0:T(8,128)(2,1)} %coil_forward_0.1), calls=%async_computation | async-start | bytes 4194304 | tf_op jit(solution)/shard_map/all_to_all | solution.py:647
  13.7 7.8 %copy-start.7 = (bf16[1,24,128,512]{3,2,1,0:T(8,128)(2,1)S(1)}, bf16[1,24,128,512]{3,2,1,0:T(8,128)(2,1)}, u32[]{:S(2)}) copy-start(bf16[1,24,128,512]{3,2,1,0:T(8,128)(2,1)} %param.12) | copy-start | bytes 9437188
  26.6 20.0 %copy-start = (bf16[512,512]{1,0:T(8,128)(2,1)S(1)}, bf16[512,512]{1,0:T(8,128)(2,1)}, u32[]{:S(2)}) copy-start(bf16[512,512]{1,0:T(8,128)(2,1)} %constant.11.clone.refs_3_) | copy-start | bytes 1572868
  26.6 20.0 %copy-start.6 = (s32[1,24]{1,0:T(1,128)S(1)}, s32[1,24]{1,0:T(1,128)}, u32[]{:S(2)}) copy-start(s32[1,24]{1,0:T(1,128)} %refs_0_.5) | copy-start | bytes 292
  42.6 32.9 %all-to-all-start.2 = ((bf16[32,2,8,16,128]{4,3,2,1,0:T(8,128)(2,1)}), bf16[32,2,8,16,128]{4,3,2,1,0:T(8,128)(2,1)S(1)}, u32[]{:S(2)}, u32[]{:S(2)}) async-start(bf16[32,2,8,16,128]{4,3,2,1,0:T(8,128)(2,1)} %coil_forward_1.1), calls=%async_computation.2 | async-start | bytes 4194304 | tf_op jit(solution)/shard_map/all_to_all | solution.py:647
  75.5 33.6 %all-to-all-start.1 = ((bf16[32,2,8,16,128]{4,3,2,1,0:T(8,128)(2,1)}), bf16[32,2,8,16,128]{4,3,2,1,0:T(8,128)(2,1)}, u32[]{:S(2)}, u32[]{:S(2)}) async-start(bf16[32,2,8,16,128]{4,3,2,1,0:T(8,128)(2,1)} %grid_tile_0.1), calls=%async_computation.1 | async-start | bytes 4194304 | tf_op jit(solution)/shard_map/all_to_all | solution.py:663
  91.5 21.8 %copy-start.2 = (bf16[512,512]{0,1:T(8,128)(2,1)S(1)}, bf16[512,512]{0,1:T(8,128)(2,1)}, u32[]{:S(2)}) copy-start(bf16[512,512]{0,1:T(8,128)(2,1)} %constant.10.clone) | copy-start | bytes 1572868
  109.2 32.9 %all-to-all-start.3 = ((bf16[32,2,8,16,128]{4,3,2,1,0:T(8,128)(2,1)}), bf16[32,2,8,16,128]{4,3,2,1,0:T(8,128)(2,1)S(1)}, u32[]{:S(2)}, u32[]{:S(2)}) async-start(bf16[32,2,8,16,128]{4,3,2,1,0:T(8,128)(2,1)} %grid_tile_1.1), calls=%async_computation.3 | async-start | bytes 4194304 | tf_op jit(solution)/shard_map/all_to_all | solution.py:663
  120.9 30.3 %collective-permute-start = (bf16[8,64,128]{2,1,0:T(8,128)(2,1)}, bf16[8,64,128]{2,1,0:T(8,128)(2,1)S(1)}, u32[]{:S(2)}, u32[]{:S(2)}) collective-permute-start(bf16[8,64,128]{2,1,0:T(8,128)(2,1)} %get-tuple-element.20), channel_id=1, source_target_pairs={{0,64},{32,96},{64,0},{96,32},{1,65},{33,97},{65,1},{97,33},{2,66}... | collective-permute-start | bytes 393224 | tf_op jit(solution)/shard_map/ppermute | solution.py:625
  124.9 29.9 %collective-permute-start.1 = (bf16[8,64,128]{2,1,0:T(8,128)(2,1)}, bf16[8,64,128]{2,1,0:T(8,128)(2,1)S(1)}, u32[]{:S(2)}, u32[]{:S(2)}) collective-permute-start(bf16[8,64,128]{2,1,0:T(8,128)(2,1)} %get-tuple-element.21), channel_id=1, source_target_pairs={{0,32},{32,64},{64,96},{96,0},{1,33},{33,65},{65,97},{97,1},{2,34}... | collective-permute-start | bytes 393224 | tf_op jit(solution)/shard_map/ppermute | solution.py:625
  125.9 28.8 %collective-permute-start.2 = (bf16[8,64,128]{2,1,0:T(8,128)(2,1)}, bf16[8,64,128]{2,1,0:T(8,128)(2,1)S(1)}, u32[]{:S(2)}, u32[]{:S(2)}) collective-permute-start(bf16[8,64,128]{2,1,0:T(8,128)(2,1)} %get-tuple-element.22), channel_id=1, source_target_pairs={{0,96},{32,0},{64,32},{96,64},{1,97},{33,1},{65,33},{97,65},{2,98}... | collective-permute-start | bytes 393224 | tf_op jit(solution)/shard_map/ppermute | solution.py:625
  142.1 11.4 %copy-start.1 = (f32[2,8,64,128]{3,2,1,0:T(8,128)S(1)}, f32[2,8,64,128]{3,2,1,0:T(8,128)}, u32[]{:S(2)}) copy-start(f32[2,8,64,128]{3,2,1,0:T(8,128)} %rest_8_.1) | copy-start | bytes 1572868
  142.1 11.4 %copy-start.3 = (f32[2,8,64,128]{3,2,1,0:T(8,128)S(1)}, f32[2,8,64,128]{3,2,1,0:T(8,128)}, u32[]{:S(2)}) copy-start(f32[2,8,64,128]{3,2,1,0:T(8,128)} %aux_ref.1) | copy-start | bytes 1572868
  146.2 11.0 %copy-start.4 = (bf16[8,64,128]{2,1,0:T(8,128)(2,1)S(1)}, bf16[8,64,128]{2,1,0:T(8,128)(2,1)}, u32[]{:S(2)}) copy-start(bf16[8,64,128]{2,1,0:T(8,128)(2,1)} %get-tuple-element.19.rest_0_) | copy-start | bytes 393220
  146.2 11.0 %copy-start.5 = (bf16[8,64,128]{2,1,0:T(8,128)(2,1)S(1)}, bf16[8,64,128]{2,1,0:T(8,128)(2,1)}, u32[]{:S(2)}) copy-start(bf16[8,64,128]{2,1,0:T(8,128)(2,1)} %get-tuple-element.25.rest_4_) | copy-start | bytes 393220
  146.2 8.5 %collective-permute-start.3 = (bf16[8,64,128]{2,1,0:T(8,128)(2,1)}, bf16[8,64,128]{2,1,0:T(8,128)(2,1)S(1)}, u32[]{:S(2)}, u32[]{:S(2)}) collective-permute-start(bf16[8,64,128]{2,1,0:T(8,128)(2,1)} %get-tuple-element.26), channel_id=1, source_target_pairs={{0,64},{32,96},{64,0},{96,32},{1,65},{33,97},{65,1},{97,33},{2,66}... | collective-permute-start | bytes 393224 | tf_op jit(solution)/shard_map/ppermute | solution.py:625
  150.2 6.8 %collective-permute-start.4 = (bf16[8,64,128]{2,1,0:T(8,128)(2,1)}, bf16[8,64,128]{2,1,0:T(8,128)(2,1)S(1)}, u32[]{:S(2)}, u32[]{:S(2)}) collective-permute-start(bf16[8,64,128]{2,1,0:T(8,128)(2,1)} %get-tuple-element.27), channel_id=1, source_target_pairs={{0,32},{32,64},{64,96},{96,0},{1,33},{33,65},{65,97},{97,1},{2,34}... | collective-permute-start | bytes 393224 | tf_op jit(solution)/shard_map/ppermute | solution.py:625
  151.2 6.0 %collective-permute-start.5 = (bf16[8,64,128]{2,1,0:T(8,128)(2,1)}, bf16[8,64,128]{2,1,0:T(8,128)(2,1)S(1)}, u32[]{:S(2)}, u32[]{:S(2)}) collective-permute-start(bf16[8,64,128]{2,1,0:T(8,128)(2,1)} %get-tuple-element.28), channel_id=1, source_target_pairs={{0,96},{32,0},{64,32},{96,64},{1,97},{33,1},{65,33},{97,65},{2,98}... | collective-permute-start | bytes 393224 | tf_op jit(solution)/shard_map/ppermute | solution.py:625

commit v7 on v6

--- a/solution.py
+++ b/solution.py
@@ -96,7 +96,7 @@
         parts = []
         for pair in range(PER):
             s_re, s_im = (
-                pack(*(sens[2 * pair + k, part, x].astype(F32) for k in range(2)), half)
+                pack(*(sens[2 * pair + k, part, x] for k in range(2)), half).astype(F32)
                 for part in range(2)
             )
             c_re = (s_re * m_re - s_im * m_im).astype(BF)
@@ -402,7 +402,7 @@
 
 def adjoint_row(table_ref, piece, x):
     data = jnp.concatenate([piece[:, pair, x].reshape(2 * N, Z) for pair in range(PER)], 1)
-    return jnp.dot(table_ref[...], data, preferred_element_type=F32).astype(BF).astype(F32)
+    return jnp.dot(table_ref[...], data, preferred_element_type=F32).astype(BF)
 
 
 def share_copies(position, out, shares, rows, sems):
@@ -431,11 +431,11 @@
         for pair in range(PER):
             both = []
             for part in range(2):
-                even, odd = (sens[2 * pair + k, part, x].astype(F32) for k in range(2))
-                both.append(pack(even, odd, 0))
-                later[pair, part, x] = pack(even, odd, 1).astype(BF)
+                even, odd = (sens[2 * pair + k, part, x] for k in range(2))
+                both.append(pack(even, odd, 0).astype(F32))
+                later[pair, part, x] = pack(even, odd, 1)
             packed.append(both)
-        gradient = combine(adjoint_row(table_ref, piece, x), packed)
+        gradient = combine(adjoint_row(table_ref, piece, x).astype(F32), packed)
         out[:, x] = gradient.astype(BF).reshape(NCOIL, N // NCOIL, Z)
         return carry
 
@@ -472,7 +472,7 @@
 
 def gradient_last_kernel(position_ref, table_ref, piece, sens_hbm, *rest):
     shares = rest[:NCOIL]
-    sens, out, arrive, sems = rest[NCOIL:]
+    sens, adjoint, out, arrive, sems = rest[NCOIL:]
     span = KYD // 2
 
     def arrivals(stage):
@@ -485,12 +485,14 @@
         arrivals(stage).start()
     leaving = []
     for stage in range(2):
+        for x in range(stage * span, (stage + 1) * span):
+            adjoint[x] = adjoint_row(table_ref, piece, x)
         arrivals(stage).wait()
         for x in range(stage * span, (stage + 1) * span):
             packed = [
                 [sens[pair, part, x].astype(F32) for part in range(2)] for pair in range(PER)
             ]
-            gradient = combine(adjoint_row(table_ref, piece, x), packed)
+            gradient = combine(adjoint[x].astype(F32), packed)
             out[:, x] = gradient.astype(BF).reshape(NCOIL, N // NCOIL, Z)
         rows = pl.ds(stage * span, span)
         for copy in share_copies(position_ref[0], out, shares, rows, sems.at[stage]):
@@ -509,11 +511,12 @@
         out_specs=(HBM,) * NCOIL,
         scratch_shapes=[
             pltpu.VMEM((PER, 2, KYD, N, Z), BF),
+            pltpu.VMEM((KYD, 2 * N, 2 * Z), BF),
             pltpu.VMEM((NCOIL,) + share, BF),
             DMA((2,)),
             DMA((2, NCOIL)),
         ],
-        compiler_params=pltpu.CompilerParams(vmem_limit_bytes=8 << 20),
+        compiler_params=pltpu.CompilerParams(vmem_limit_bytes=10 << 20),
         name="gradient_last",
     )(position, table, piece, packed)
 
@@ -641,8 +644,8 @@
     for chunk in chunks:
         half = coil_forward(chunk, y_forward, sensitivity, image)
         if chunk == 1:
-            half, turned, by_coil, y_inverse = lax.optimization_barrier(
-                (half, turned, by_coil, y_inverse)
+            half, turned, by_coil, y_inverse, pieces[0] = lax.optimization_barrier(
+                (half, turned, by_coil, y_inverse, pieces[0])
             )
         piece = lax.all_to_all(half, "slab", 0, 0, tiled=True)
         pieces.append(piece)

time: 159 us -> 159 us (level)
  no operation moved by 1% of the time
where the time goes in v7:
time: 159 us; the launch traced here: 158 us
  waiting for transfers between devices  65.8 us (41%)
  Pallas kernels  52.8 us (33%)
  starting transfers between devices  35 us (22%)
  local copies, waits for them, and re-layouts  2.89 us (2%)
  between operations  1.63 us (1%)
    all_to_all x2, waiting for transfers between devices, body(): piece = lax.all_to_all(half, 'slab', 0, 0, tiled=True)  32.1 us
    all_to_all x2, waiting for transfers between devices, body(): backs.append(lax.all_to_all(back, 'slab', 0, 0, tiled=True))  31.3 us
    pallas_call x2, Pallas kernels, grid_tile(): pl.pallas_call(kernel, out_shape=hbm((TILES, PER, KYD, 16, Z), BF), in_sp...  24.1 us
    ppermute x6, starting transfers between devices, over_planes(): got.append(lax.ppermute(others[k - 1], 'coil', ring))  14.4 us
    pallas_call x2, Pallas kernels, coil_forward(): pl.pallas_call(kernel, out_shape=hbm((TILES, PER, KYD, 16, Z), BF), in_sp...  12.4 us
    all_to_all x2, starting transfers between devices, body(): piece = lax.all_to_all(half, 'slab', 0, 0, tiled=True)  11.7 us
    all_to_all x2, starting transfers between devices, body(): backs.append(lax.all_to_all(back, 'slab', 0, 0, tiled=True))  8.95 us
    pallas_call x1, Pallas kernels, gradient_first(): pl.pallas_call(gradient_first_kernel, out_shape=(hbm(share, BF),) * NCOIL...  7.82 us
  transfers between devices with their start and end apart: 10, of which 6 were waited for; matrix products, arithmetic and copies ran while one was open for 2% of the time, Pallas kernels for 29%

profile of v7, /device:TPU:0, one launch (start us, length us, event | category | flops | bytes accessed | tf_op | source)
XLA Modules:
  0.0 158.2 jit_solution(13029240201743571457)
XLA Ops:
  0.6 5.3 %coil_forward_0.1 = bf16[32,2,8,16,128]{4,3,2,1,0:T(8,128)(2,1)} custom-call(bf16[512,512]{1,0:T(8,128)(2,1)} %constant.20.refs_0_, bf16[4,2,8,256,128]{4,3,2,1,0:T(8,128)(2,1)} %sens_hbm.1, f32[2,8,256,128]{3,2,1,0:T(8,128)} %refs_2_.3), custom_call_target="tpu_custom_call" | custom-call | tf_op jit(solution)/shard_map/coil_forward_0/pallas_call | solution.py:132
  5.9 7.5 %all-to-all-start = ((bf16[32,2,8,16,128]{4,3,2,1,0:T(8,128)(2,1)}), bf16[32,2,8,16,128]{4,3,2,1,0:T(8,128)(2,1)}, u32[]{:S(2)}, u32[]{:S(2)}) async-start(bf16[32,2,8,16,128]{4,3,2,1,0:T(8,128)(2,1)} %coil_forward_0.1), calls=%async_computation | async-start | bytes 4194304 | tf_op jit(solution)/shard_map/all_to_all | solution.py:650
  13.5 0.0 copy-start.7
  13.5 7.0 %coil_forward_1.1 = bf16[32,2,8,16,128]{4,3,2,1,0:T(8,128)(2,1)} custom-call(bf16[512,512]{1,0:T(8,128)(2,1)} %constant.20.refs_0_, bf16[4,2,8,256,128]{4,3,2,1,0:T(8,128)(2,1)} %sens_hbm.1, f32[2,8,256,128]{3,2,1,0:T(8,128)} %refs_2_.3), custom_call_target="tpu_custom_call" | custom-call | tf_op jit(solution)/shard_map/coil_forward_1/pallas_call | solution.py:132
  21.2 0.0 copy-done.7
  21.2 2.9 %copy.14 = bf16[1,24,128,512]{2,3,1,0:T(8,128)(2,1)} copy(bf16[1,24,128,512]{3,2,1,0:T(8,128)(2,1)S(1)} %copy-done.7) | data formatting | bytes 6291456 | tf_op args[2]
  24.1 2.3 %samples_by_coil.1.refs_6_ = bf16[4,24,128,256]{3,2,1,0:T(8,128)(2,1)} custom-call(s32[1]{0:T(128)S(6)} %copy.19.counts_ref.refs_1_, bf16[24,128,8,128]{3,2,1,0:T(8,128)(2,1)} %bitcast.13), custom_call_target="tpu_custom_call" | custom-call | tf_op jit(solution)/shard_map/samples_by_coil/pallas_call | solution.py:190
  26.4 16.0 %all-to-all-done.refs_2_ = bf16[32,2,8,16,128]{4,3,2,1,0:T(8,128)(2,1)} async-done(((bf16[32,2,8,16,128]{4,3,2,1,0:T(8,128)(2,1)}), bf16[32,2,8,16,128]{4,3,2,1,0:T(8,128)(2,1)}, u32[]{:S(2)}, u32[]{:S(2)}) %all-to-all-start) | async-done | bytes 2097184 | tf_op jit(solution)/shard_map/all_to_all | solution.py:650
  42.4 0.0 copy-start
  42.4 0.0 copy-start.6
  42.4 4.1 %all-to-all-start.2 = ((bf16[32,2,8,16,128]{4,3,2,1,0:T(8,128)(2,1)}), bf16[32,2,8,16,128]{4,3,2,1,0:T(8,128)(2,1)S(1)}, u32[]{:S(2)}, u32[]{:S(2)}) async-start(bf16[32,2,8,16,128]{4,3,2,1,0:T(8,128)(2,1)} %coil_forward_1.1), calls=%async_computation.2 | async-start | bytes 4194304 | tf_op jit(solution)/shard_map/all_to_all | solution.py:650
  46.6 0.0 copy-done
  46.6 0.0 copy-done.6
  46.6 12.8 %grid_tile_0.1 = bf16[32,2,8,16,128]{4,3,2,1,0:T(8,128)(2,1)} custom-call(s32[1,24]{1,0:T(1,128)S(1)} %copy-done.6, s32[1]{0:T(128)S(6)} %copy.19.counts_ref.refs_1_, bf16[32,2,8,16,128]{4,3,2,1,0:T(8,128)(2,1)} %all-to-all-done.refs_2_, bf16[512,512]{1,0:T(8,128)(2,1)S(1)} %copy-done, bf16[24,128,512]{2,1,0:T(8,128)(2,1)} %bitcast.9, ...), custom_call_target="tpu_custom_call" | custom-call | tf_op jit(solution)/shard_map/grid_tile_0/pallas_call | solution.py:366
  59.4 16.1 %all-to-all-done.2.refs_2_ = bf16[32,2,8,16,128]{4,3,2,1,0:T(8,128)(2,1)S(1)} async-done(((bf16[32,2,8,16,128]{4,3,2,1,0:T(8,128)(2,1)}), bf16[32,2,8,16,128]{4,3,2,1,0:T(8,128)(2,1)S(1)}, u32[]{:S(2)}, u32[]{:S(2)}) %all-to-all-start.2) | async-done | bytes 2097184 | tf_op jit(solution)/shard_map/all_to_all | solution.py:650
  75.4 4.8 %all-to-all-start.1 = ((bf16[32,2,8,16,128]{4,3,2,1,0:T(8,128)(2,1)}), bf16[32,2,8,16,128]{4,3,2,1,0:T(8,128)(2,1)}, u32[]{:S(2)}, u32[]{:S(2)}) async-start(bf16[32,2,8,16,128]{4,3,2,1,0:T(8,128)(2,1)} %grid_tile_0.1), calls=%async_computation.1 | async-start | bytes 4194304 | tf_op jit(solution)/shard_map/all_to_all | solution.py:666
  80.2 11.3 %grid_tile_1.1 = bf16[32,2,8,16,128]{4,3,2,1,0:T(8,128)(2,1)} custom-call(s32[1,24]{1,0:T(1,128)S(1)} %copy-done.6, s32[1]{0:T(128)S(6)} %copy.19.counts_ref.refs_1_, bf16[32,2,8,16,128]{4,3,2,1,0:T(8,128)(2,1)S(1)} %all-to-all-done.2.refs_2_, bf16[512,512]{1,0:T(8,128)(2,1)S(1)} %copy-done, bf16[24,128,512]{2,1,0:T(8,128)(2,1)} %bitcast.10, ...), custom_call_target="tpu_custom_call" | custom-call | tf_op jit(solution)/shard_map/grid_tile_1/pallas_call | solution.py:366
  91.5 0.0 copy-start.2
  91.5 17.6 %all-to-all-done.1.piece_hbm = bf16[32,2,8,16,128]{4,3,2,1,0:T(8,128)(2,1)} async-done(((bf16[32,2,8,16,128]{4,3,2,1,0:T(8,128)(2,1)}), bf16[32,2,8,16,128]{4,3,2,1,0:T(8,128)(2,1)}, u32[]{:S(2)}, u32[]{:S(2)}) %all-to-all-start.1) | async-done | bytes 2097184 | tf_op jit(solution)/shard_map/all_to_all | solution.py:666
  109.1 4.2 %all-to-all-start.3 = ((bf16[32,2,8,16,128]{4,3,2,1,0:T(8,128)(2,1)}), bf16[32,2,8,16,128]{4,3,2,1,0:T(8,128)(2,1)S(1)}, u32[]{:S(2)}, u32[]{:S(2)}) async-start(bf16[32,2,8,16,128]{4,3,2,1,0:T(8,128)(2,1)} %grid_tile_1.1), calls=%async_computation.3 | async-start | bytes 4194304 | tf_op jit(solution)/shard_map/all_to_all | solution.py:666
  113.3 0.0 copy-done.2
  113.3 7.8 %gradient_first.1 = (bf16[8,64,128]{2,1,0:T(8,128)(2,1)}, bf16[8,64,128]{2,1,0:T(8,128)(2,1)}, bf16[8,64,128]{2,1,0:T(8,128)(2,1)}, bf16[8,64,128]{2,1,0:T(8,128)(2,1)}, bf16[2,2,8,256,128]{4,3,2,1,0:T(8,128)(2,1)}) custom-call(s32[1]{0:T(128)} %bitcast.position_ref, bf16[512,512]{1,0:T(8,128)(2,1)S(1)} %bitcast.7, ...), custom_call_target="tpu_custom_call" | custom-call | tf_op jit(solution)/shard_map/gradient_first/pallas_call | solution.py:454
  121.1 4.0 %collective-permute-start = (bf16[8,64,128]{2,1,0:T(8,128)(2,1)}, bf16[8,64,128]{2,1,0:T(8,128)(2,1)S(1)}, u32[]{:S(2)}, u32[]{:S(2)}) collective-permute-start(bf16[8,64,128]{2,1,0:T(8,128)(2,1)} %get-tuple-element.22), channel_id=1, source_target_pairs={{0,64},{32,96},{64,0},{96,32},{1,65},{33,97},{65,1},{97,33},{2,66}... | collective-permute-start | bytes 393224 | tf_op jit(solution)/shard_map/ppermute | solution.py:628
  125.1 1.0 collective-permute-start.1
  126.1 2.2 %collective-permute-start.2 = (bf16[8,64,128]{2,1,0:T(8,128)(2,1)}, bf16[8,64,128]{2,1,0:T(8,128)(2,1)S(1)}, u32[]{:S(2)}, u32[]{:S(2)}) collective-permute-start(bf16[8,64,128]{2,1,0:T(8,128)(2,1)} %get-tuple-element.24), channel_id=1, source_target_pairs={{0,96},{32,0},{64,32},{96,64},{1,97},{33,1},{65,33},{97,65},{2,98}... | collective-permute-start | bytes 393224 | tf_op jit(solution)/shard_map/ppermute | solution.py:628
  128.3 13.7 %all-to-all-done.3.piece = bf16[32,2,8,16,128]{4,3,2,1,0:T(8,128)(2,1)S(1)} async-done(((bf16[32,2,8,16,128]{4,3,2,1,0:T(8,128)(2,1)}), bf16[32,2,8,16,128]{4,3,2,1,0:T(8,128)(2,1)S(1)}, u32[]{:S(2)}, u32[]{:S(2)}) %all-to-all-start.3) | async-done | bytes 2097184 | tf_op jit(solution)/shard_map/all_to_all | solution.py:666
  142.0 0.0 copy-start.1
  142.0 0.0 copy-start.3
  142.0 3.6 %gradient_last.1 = (bf16[8,64,128]{2,1,0:T(8,128)(2,1)}, bf16[8,64,128]{2,1,0:T(8,128)(2,1)}, bf16[8,64,128]{2,1,0:T(8,128)(2,1)}, bf16[8,64,128]{2,1,0:T(8,128)(2,1)}) custom-call(s32[1]{0:T(128)} %bitcast.position_ref, bf16[512,512]{1,0:T(8,128)(2,1)S(1)} %bitcast.8, bf16[32,2,8,16,128]{4,3,2,1,0:T(8,128)(2,1)S(1)} %all-to-all-done.3.piece, ...), custom_call_target="tpu_custom_call" | custom-call | tf_op jit(solution)/shard_map/gradient_last/pallas_call | solution.py:507
  145.6 0.0 copy-start.4
  145.6 0.0 copy-start.5
  145.6 4.0 %collective-permute-start.3 = (bf16[8,64,128]{2,1,0:T(8,128)(2,1)}, bf16[8,64,128]{2,1,0:T(8,128)(2,1)S(1)}, u32[]{:S(2)}, u32[]{:S(2)}) collective-permute-start(bf16[8,64,128]{2,1,0:T(8,128)(2,1)} %get-tuple-element.28), channel_id=1, source_target_pairs={{0,64},{32,96},{64,0},{96,32},{1,65},{33,97},{65,1},{97,33},{2,66}... | collective-permute-start | bytes 393224 | tf_op jit(solution)/shard_map/ppermute | solution.py:628
  149.6 1.0 collective-permute-start.4
  150.6 0.0 collective-permute-done.rest_1_
  150.6 2.2 %collective-permute-start.5 = (bf16[8,64,128]{2,1,0:T(8,128)(2,1)}, bf16[8,64,128]{2,1,0:T(8,128)(2,1)S(1)}, u32[]{:S(2)}, u32[]{:S(2)}) collective-permute-start(bf16[8,64,128]{2,1,0:T(8,128)(2,1)} %get-tuple-element.30), channel_id=1, source_target_pairs={{0,96},{32,0},{64,32},{96,64},{1,97},{33,1},{65,33},{97,65},{2,98}... | collective-permute-start | bytes 393224 | tf_op jit(solution)/shard_map/ppermute | solution.py:628
  152.8 0.0 copy-done.1
  152.8 0.0 copy-done.3
  152.8 1.3 target.1.base_ref
  154.1 0.0 collective-permute-done.1.rest_2_
  154.1 0.0 collective-permute-done.2.rest_3_
  154.1 0.0 collective-permute-done.3.rest_5_
  154.2 2.2 %collective-permute-done.4.rest_6_ = bf16[8,64,128]{2,1,0:T(8,128)(2,1)S(1)} collective-permute-done((bf16[8,64,128]{2,1,0:T(8,128)(2,1)}, bf16[8,64,128]{2,1,0:T(8,128)(2,1)S(1)}, u32[]{:S(2)}, u32[]{:S(2)}) %collective-permute-start.4) | collective-permute-done | bytes 131104 | tf_op jit(solution)/shard_map/ppermute | solution.py:628
  156.4 0.3 collective-permute-done.5.rest_7_
  156.6 0.0 copy-done.4
  156.7 0.0 copy-done.5
  156.7 1.4 update.1
Async XLA Ops:
  5.9 36.5 %all-to-all-start = ((bf16[32,2,8,16,128]{4,3,2,1,0:T(8,128)(2,1)}), bf16[32,2,8,16,128]{4,3,2,1,0:T(8,128)(2,1)}, u32[]{:S(2)}, u32[]{:S(2)}) async-start(bf16[32,2,8,16,128]{4,3,2,1,0:T(8,128)(2,1)} %coil_forward_0.1), calls=%async_computation | async-start | bytes 4194304 | tf_op jit(solution)/shard_map/all_to_all | solution.py:650
  13.5 7.7 %copy-start.7 = (bf16[1,24,128,512]{3,2,1,0:T(8,128)(2,1)S(1)}, bf16[1,24,128,512]{3,2,1,0:T(8,128)(2,1)}, u32[]{:S(2)}) copy-start(bf16[1,24,128,512]{3,2,1,0:T(8,128)(2,1)} %param.12) | copy-start | bytes 9437188
  42.4 4.2 %copy-start = (bf16[512,512]{1,0:T(8,128)(2,1)S(1)}, bf16[512,512]{1,0:T(8,128)(2,1)}, u32[]{:S(2)}) copy-start(bf16[512,512]{1,0:T(8,128)(2,1)} %constant.11.clone.refs_3_) | copy-start | bytes 1572868
  42.4 4.2 %copy-start.6 = (s32[1,24]{1,0:T(1,128)S(1)}, s32[1,24]{1,0:T(1,128)}, u32[]{:S(2)}) copy-start(s32[1,24]{1,0:T(1,128)} %refs_0_.5) | copy-start | bytes 292
  42.4 33.0 %all-to-all-start.2 = ((bf16[32,2,8,16,128]{4,3,2,1,0:T(8,128)(2,1)}), bf16[32,2,8,16,128]{4,3,2,1,0:T(8,128)(2,1)S(1)}, u32[]{:S(2)}, u32[]{:S(2)}) async-start(bf16[32,2,8,16,128]{4,3,2,1,0:T(8,128)(2,1)} %coil_forward_1.1), calls=%async_computation.2 | async-start | bytes 4194304 | tf_op jit(solution)/shard_map/all_to_all | solution.py:650
  75.4 33.6 %all-to-all-start.1 = ((bf16[32,2,8,16,128]{4,3,2,1,0:T(8,128)(2,1)}), bf16[32,2,8,16,128]{4,3,2,1,0:T(8,128)(2,1)}, u32[]{:S(2)}, u32[]{:S(2)}) async-start(bf16[32,2,8,16,128]{4,3,2,1,0:T(8,128)(2,1)} %grid_tile_0.1), calls=%async_computation.1 | async-start | bytes 4194304 | tf_op jit(solution)/shard_map/all_to_all | solution.py:666
  91.5 21.8 %copy-start.2 = (bf16[512,512]{0,1:T(8,128)(2,1)S(1)}, bf16[512,512]{0,1:T(8,128)(2,1)}, u32[]{:S(2)}) copy-start(bf16[512,512]{0,1:T(8,128)(2,1)} %constant.10.clone) | copy-start | bytes 1572868
  109.1 32.9 %all-to-all-start.3 = ((bf16[32,2,8,16,128]{4,3,2,1,0:T(8,128)(2,1)}), bf16[32,2,8,16,128]{4,3,2,1,0:T(8,128)(2,1)S(1)}, u32[]{:S(2)}, u32[]{:S(2)}) async-start(bf16[32,2,8,16,128]{4,3,2,1,0:T(8,128)(2,1)} %grid_tile_1.1), calls=%async_computation.3 | async-start | bytes 4194304 | tf_op jit(solution)/shard_map/all_to_all | solution.py:666
  121.1 29.5 %collective-permute-start = (bf16[8,64,128]{2,1,0:T(8,128)(2,1)}, bf16[8,64,128]{2,1,0:T(8,128)(2,1)S(1)}, u32[]{:S(2)}, u32[]{:S(2)}) collective-permute-start(bf16[8,64,128]{2,1,0:T(8,128)(2,1)} %get-tuple-element.22), channel_id=1, source_target_pairs={{0,64},{32,96},{64,0},{96,32},{1,65},{33,97},{65,1},{97,33},{2,66}... | collective-permute-start | bytes 393224 | tf_op jit(solution)/shard_map/ppermute | solution.py:628
  125.1 29.0 %collective-permute-start.1 = (bf16[8,64,128]{2,1,0:T(8,128)(2,1)}, bf16[8,64,128]{2,1,0:T(8,128)(2,1)S(1)}, u32[]{:S(2)}, u32[]{:S(2)}) collective-permute-start(bf16[8,64,128]{2,1,0:T(8,128)(2,1)} %get-tuple-element.23), channel_id=1, source_target_pairs={{0,32},{32,64},{64,96},{96,0},{1,33},{33,65},{65,97},{97,1},{2,34}... | collective-permute-start | bytes 393224 | tf_op jit(solution)/shard_map/ppermute | solution.py:628
  126.1 28.0 %collective-permute-start.2 = (bf16[8,64,128]{2,1,0:T(8,128)(2,1)}, bf16[8,64,128]{2,1,0:T(8,128)(2,1)S(1)}, u32[]{:S(2)}, u32[]{:S(2)}) collective-permute-start(bf16[8,64,128]{2,1,0:T(8,128)(2,1)} %get-tuple-element.24), channel_id=1, source_target_pairs={{0,96},{32,0},{64,32},{96,64},{1,97},{33,1},{65,33},{97,65},{2,98}... | collective-permute-start | bytes 393224 | tf_op jit(solution)/shard_map/ppermute | solution.py:628
  142.0 10.8 %copy-start.1 = (f32[2,8,64,128]{3,2,1,0:T(8,128)S(1)}, f32[2,8,64,128]{3,2,1,0:T(8,128)}, u32[]{:S(2)}) copy-start(f32[2,8,64,128]{3,2,1,0:T(8,128)} %rest_8_.1) | copy-start | bytes 1572868
  142.0 10.8 %copy-start.3 = (f32[2,8,64,128]{3,2,1,0:T(8,128)S(1)}, f32[2,8,64,128]{3,2,1,0:T(8,128)}, u32[]{:S(2)}) copy-start(f32[2,8,64,128]{3,2,1,0:T(8,128)} %aux_ref.1) | copy-start | bytes 1572868
  145.6 11.0 %copy-start.4 = (bf16[8,64,128]{2,1,0:T(8,128)(2,1)S(1)}, bf16[8,64,128]{2,1,0:T(8,128)(2,1)}, u32[]{:S(2)}) copy-start(bf16[8,64,128]{2,1,0:T(8,128)(2,1)} %get-tuple-element.21.rest_0_) | copy-start | bytes 393220
  145.6 11.0 %copy-start.5 = (bf16[8,64,128]{2,1,0:T(8,128)(2,1)S(1)}, bf16[8,64,128]{2,1,0:T(8,128)(2,1)}, u32[]{:S(2)}) copy-start(bf16[8,64,128]{2,1,0:T(8,128)(2,1)} %get-tuple-element.27.rest_4_) | copy-start | bytes 393220
  145.6 8.5 %collective-permute-start.3 = (bf16[8,64,128]{2,1,0:T(8,128)(2,1)}, bf16[8,64,128]{2,1,0:T(8,128)(2,1)S(1)}, u32[]{:S(2)}, u32[]{:S(2)}) collective-permute-start(bf16[8,64,128]{2,1,0:T(8,128)(2,1)} %get-tuple-element.28), channel_id=1, source_target_pairs={{0,64},{32,96},{64,0},{96,32},{1,65},{33,97},{65,1},{97,33},{2,66}... | collective-permute-start | bytes 393224 | tf_op jit(solution)/shard_map/ppermute | solution.py:628
  149.6 6.8 %collective-permute-start.4 = (bf16[8,64,128]{2,1,0:T(8,128)(2,1)}, bf16[8,64,128]{2,1,0:T(8,128)(2,1)S(1)}, u32[]{:S(2)}, u32[]{:S(2)}) collective-permute-start(bf16[8,64,128]{2,1,0:T(8,128)(2,1)} %get-tuple-element.29), channel_id=1, source_target_pairs={{0,32},{32,64},{64,96},{96,0},{1,33},{33,65},{65,97},{97,1},{2,34}... | collective-permute-start | bytes 393224 | tf_op jit(solution)/shard_map/ppermute | solution.py:628
  150.6 6.0 %collective-permute-start.5 = (bf16[8,64,128]{2,1,0:T(8,128)(2,1)}, bf16[8,64,128]{2,1,0:T(8,128)(2,1)S(1)}, u32[]{:S(2)}, u32[]{:S(2)}) collective-permute-start(bf16[8,64,128]{2,1,0:T(8,128)(2,1)} %get-tuple-element.30), channel_id=1, source_target_pairs={{0,96},{32,0},{64,32},{96,64},{1,97},{33,1},{65,33},{97,65},{2,98}... | collective-permute-start | bytes 393224 | tf_op jit(solution)/shard_map/ppermute | solution.py:628

commit v8 on v7

--- a/solution.py
+++ b/solution.py
@@ -535,51 +535,67 @@
     return pairs(add), pairs(sub)
 
 
-def target_kernel(position_ref, image_hbm, aux_ref, dual_ref, out_ref, image, sem):
+def spread_halves(first, second):
+    low = lax.broadcasted_iota(jnp.int32, first.shape, 1) < Z // 2
+    return (
+        jnp.where(low, first, pltpu.roll(second, Z // 2, 1)),
+        jnp.where(low, pltpu.roll(first, Z // 2, 1), second),
+    )
+
+
+def target_kernel(position_ref, image_hbm, aux_ref, dual_ref, *rest):
+    early = rest[:NCOIL]
+    own_ref, out_ref, image, sem = rest[NCOIL:]
     share = N // NCOIL
     columns = pl.ds(pl.multiple_of(position_ref[0] * share, share), share)
     copy = pltpu.make_async_copy(image_hbm.at[:, :, columns], image, sem)
     copy.start()
     copy.wait()
     for m in range(KYD // 2):
+        known = []
+        for x in (2 * m, 2 * m + 1):
+            total = early[0][x].astype(F32)
+            for other in early[1:]:
+                total = total + other[x].astype(F32)
+            known.append(spread_halves(total, own_ref[x].astype(F32)))
         for part in range(2):
             rows = haar_rows(
                 *(aux_ref[part, 2 * m + i] - dual_ref[part, 2 * m + i] for i in range(2))
             )
             for i in range(2):
                 current = image[part, 2 * m + i]
-                out_ref[part, 2 * m + i] = current - step_size * penalty * (current - rows[i])
-
-
-def target_step(position, image, auxiliary, scaled_dual):
+                out_ref[part, 2 * m + i] = current - step_size * (
+                    known[i][part] + penalty * (current - rows[i])
+                )
+
+
+def target_step(position, image, auxiliary, scaled_dual, early, own):
     return pl.pallas_call(
         target_kernel,
         out_shape=jax.ShapeDtypeStruct(auxiliary.shape, F32),
-        in_specs=[SMEM, HBM, VMEM, VMEM],
+        in_specs=[SMEM, HBM] + [VMEM] * (NCOIL + 3),
         out_specs=VMEM,
         scratch_shapes=[pltpu.VMEM(auxiliary.shape, F32), DMA],
-        compiler_params=pltpu.CompilerParams(vmem_limit_bytes=6 << 20),
+        compiler_params=pltpu.CompilerParams(vmem_limit_bytes=7 << 20),
         name="target",
-    )(position, image, auxiliary, scaled_dual)
+    )(position, image, auxiliary, scaled_dual, *early, own)
 
 
 def update_kernel(base_ref, *rest):
-    halves = (rest[:NCOIL], rest[NCOIL : 2 * NCOIL])
-    dual_ref, image_hbm, aux_hbm, dual_hbm, image, aux, dual, sems = rest[2 * NCOIL :]
+    late = rest[: NCOIL - 1]
+    dual_ref, image_hbm, aux_hbm, dual_hbm, image, aux, dual, sems = rest[NCOIL - 1 :]
     low = lax.broadcasted_iota(jnp.int32, (N // NCOIL, Z), 1) < Z // 2
     leaving = []
     for m in range(KYD // 2):
         rows = ([], [])
         for x in (2 * m, 2 * m + 1):
-            sums = []
-            for shares in halves:
-                total = shares[0][x].astype(F32)
-                for share in shares[1:]:
-                    total = total + share[x].astype(F32)
-                sums.append(total)
+            total = late[0][x].astype(F32)
+            for other in late[1:]:
+                total = total + other[x].astype(F32)
+            zero = jnp.zeros_like(total)
             gradient = (
-                jnp.where(low, sums[0], pltpu.roll(sums[1], Z // 2, 1)),
-                jnp.where(low, pltpu.roll(sums[0], Z // 2, 1), sums[1]),
+                jnp.where(low, zero, pltpu.roll(total, Z // 2, 1)),
+                jnp.where(low, zero, total),
             )
             for part in range(2):
                 value = base_ref[part, x] - step_size * gradient[part]
@@ -607,17 +623,17 @@
         copy.wait()
 
 
-def update_step(base, shares, scaled_dual):
+def update_step(base, late, scaled_dual):
     shape = hbm(scaled_dual.shape, F32)
     return pl.pallas_call(
         update_kernel,
         out_shape=(shape, shape, shape),
-        in_specs=[VMEM] * (2 * NCOIL + 2),
+        in_specs=[VMEM] * (NCOIL + 1),
         out_specs=(HBM, HBM, HBM),
         scratch_shapes=[pltpu.VMEM(scaled_dual.shape, F32)] * 3 + [DMA((3, KYD // 2))],
         compiler_params=pltpu.CompilerParams(vmem_limit_bytes=8 << 20),
         name="update",
-    )(base, *shares, scaled_dual)
+    )(base, *late, scaled_dual)
 
 
 def over_planes(shares):
@@ -650,7 +666,6 @@
         piece = lax.all_to_all(half, "slab", 0, 0, tiled=True)
         pieces.append(piece)
     position = lax.axis_index("coil").reshape(1)
-    base = target_step(position, image, auxiliary, scaled_dual)
     backs = []
     for chunk in chunks:
         back = grid_tile(
@@ -667,7 +682,8 @@
     *shares, packed = gradient_first(position, y_inverse, in_hbm(backs[0]), sensitivity)
     early = over_planes(shares)
     late = over_planes(gradient_last(position, y_inverse, backs[1], in_hbm(packed)))
-    return update_step(base, early + late, scaled_dual)
+    base = target_step(position, image, auxiliary, scaled_dual, early, late[0])
+    return update_step(base, late[1:], scaled_dual)
 
 
 def solution(mesh):

time: 159 us -> 159 us (level)
  no operation moved by 1% of the time
where the time goes in v8:
time: 159 us; the launch traced here: 158 us
  waiting for transfers between devices  64.8 us (41%)
  Pallas kernels  53 us (33%)
  starting transfers between devices  35 us (22%)
  local copies, waits for them, and re-layouts  3.78 us (2%)
  between operations  1.63 us (1%)
    all_to_all x2, waiting for transfers between devices, body(): piece = lax.all_to_all(half, 'slab', 0, 0, tiled=True)  32.1 us
    all_to_all x2, waiting for transfers between devices, body(): backs.append(lax.all_to_all(back, 'slab', 0, 0, tiled=True))  31.3 us
    pallas_call x2, Pallas kernels, grid_tile(): pl.pallas_call(kernel, out_shape=hbm((TILES, PER, KYD, 16, Z), BF), in_sp...  24.1 us
    ppermute x6, starting transfers between devices, over_planes(): got.append(lax.ppermute(others[k - 1], 'coil', ring))  14.4 us
    pallas_call x2, Pallas kernels, coil_forward(): pl.pallas_call(kernel, out_shape=hbm((TILES, PER, KYD, 16, Z), BF), in_sp...  12.4 us
    all_to_all x2, starting transfers between devices, body(): piece = lax.all_to_all(half, 'slab', 0, 0, tiled=True)  11.7 us
    all_to_all x2, starting transfers between devices, body(): backs.append(lax.all_to_all(back, 'slab', 0, 0, tiled=True))  8.95 us
    pallas_call x1, Pallas kernels, gradient_first(): pl.pallas_call(gradient_first_kernel, out_shape=(hbm(share, BF),) * NCOIL...  7.82 us
  transfers between devices with their start and end apart: 10, of which 6 were waited for; matrix products, arithmetic and copies ran while one was open for 2% of the time, Pallas kernels for 29%

profile of v8, /device:TPU:0, one launch (start us, length us, event | category | flops | bytes accessed | tf_op | source)
XLA Modules:
  0.0 158.2 jit_solution(9913915816730427550)
XLA Ops:
  0.6 5.3 %coil_forward_0.1 = bf16[32,2,8,16,128]{4,3,2,1,0:T(8,128)(2,1)} custom-call(bf16[512,512]{1,0:T(8,128)(2,1)} %constant.20.refs_0_, bf16[4,2,8,256,128]{4,3,2,1,0:T(8,128)(2,1)} %sens_hbm.1, f32[2,8,256,128]{3,2,1,0:T(8,128)} %image_hbm.1), custom_call_target="tpu_custom_call" | custom-call | tf_op jit(solution)/shard_map/coil_forward_0/pallas_call | solution.py:132
  5.9 7.5 %all-to-all-start = ((bf16[32,2,8,16,128]{4,3,2,1,0:T(8,128)(2,1)}), bf16[32,2,8,16,128]{4,3,2,1,0:T(8,128)(2,1)}, u32[]{:S(2)}, u32[]{:S(2)}) async-start(bf16[32,2,8,16,128]{4,3,2,1,0:T(8,128)(2,1)} %coil_forward_0.1), calls=%async_computation | async-start | bytes 4194304 | tf_op jit(solution)/shard_map/all_to_all | solution.py:666
  13.5 0.0 copy-start.7
  13.5 7.0 %coil_forward_1.1 = bf16[32,2,8,16,128]{4,3,2,1,0:T(8,128)(2,1)} custom-call(bf16[512,512]{1,0:T(8,128)(2,1)} %constant.20.refs_0_, bf16[4,2,8,256,128]{4,3,2,1,0:T(8,128)(2,1)} %sens_hbm.1, f32[2,8,256,128]{3,2,1,0:T(8,128)} %image_hbm.1), custom_call_target="tpu_custom_call" | custom-call | tf_op jit(solution)/shard_map/coil_forward_1/pallas_call | solution.py:132
  21.2 0.0 copy-done.7
  21.2 2.9 %copy.14 = bf16[1,24,128,512]{2,3,1,0:T(8,128)(2,1)} copy(bf16[1,24,128,512]{3,2,1,0:T(8,128)(2,1)S(1)} %copy-done.7) | data formatting | bytes 6291456 | tf_op args[2]
  24.1 2.3 %samples_by_coil.1.refs_6_ = bf16[4,24,128,256]{3,2,1,0:T(8,128)(2,1)} custom-call(s32[1]{0:T(128)S(6)} %copy.19.counts_ref.refs_1_, bf16[24,128,8,128]{3,2,1,0:T(8,128)(2,1)} %bitcast.13), custom_call_target="tpu_custom_call" | custom-call | tf_op jit(solution)/shard_map/samples_by_coil/pallas_call | solution.py:190
  26.4 16.0 %all-to-all-done.refs_2_ = bf16[32,2,8,16,128]{4,3,2,1,0:T(8,128)(2,1)} async-done(((bf16[32,2,8,16,128]{4,3,2,1,0:T(8,128)(2,1)}), bf16[32,2,8,16,128]{4,3,2,1,0:T(8,128)(2,1)}, u32[]{:S(2)}, u32[]{:S(2)}) %all-to-all-start) | async-done | bytes 2097184 | tf_op jit(solution)/shard_map/all_to_all | solution.py:666
  42.4 0.0 copy-start
  42.4 0.0 copy-start.6
  42.4 4.1 %all-to-all-start.2 = ((bf16[32,2,8,16,128]{4,3,2,1,0:T(8,128)(2,1)}), bf16[32,2,8,16,128]{4,3,2,1,0:T(8,128)(2,1)S(1)}, u32[]{:S(2)}, u32[]{:S(2)}) async-start(bf16[32,2,8,16,128]{4,3,2,1,0:T(8,128)(2,1)} %coil_forward_1.1), calls=%async_computation.2 | async-start | bytes 4194304 | tf_op jit(solution)/shard_map/all_to_all | solution.py:666
  46.6 0.0 copy-done
  46.6 0.0 copy-done.6
  46.6 12.8 %grid_tile_0.1 = bf16[32,2,8,16,128]{4,3,2,1,0:T(8,128)(2,1)} custom-call(s32[1,24]{1,0:T(1,128)S(1)} %copy-done.6, s32[1]{0:T(128)S(6)} %copy.19.counts_ref.refs_1_, bf16[32,2,8,16,128]{4,3,2,1,0:T(8,128)(2,1)} %all-to-all-done.refs_2_, bf16[512,512]{1,0:T(8,128)(2,1)S(1)} %copy-done, bf16[24,128,512]{2,1,0:T(8,128)(2,1)} %bitcast.9, ...), custom_call_target="tpu_custom_call" | custom-call | tf_op jit(solution)/shard_map/grid_tile_0/pallas_call | solution.py:366
  59.4 16.1 %all-to-all-done.2.refs_2_ = bf16[32,2,8,16,128]{4,3,2,1,0:T(8,128)(2,1)S(1)} async-done(((bf16[32,2,8,16,128]{4,3,2,1,0:T(8,128)(2,1)}), bf16[32,2,8,16,128]{4,3,2,1,0:T(8,128)(2,1)S(1)}, u32[]{:S(2)}, u32[]{:S(2)}) %all-to-all-start.2) | async-done | bytes 2097184 | tf_op jit(solution)/shard_map/all_to_all | solution.py:666
  75.4 4.8 %all-to-all-start.1 = ((bf16[32,2,8,16,128]{4,3,2,1,0:T(8,128)(2,1)}), bf16[32,2,8,16,128]{4,3,2,1,0:T(8,128)(2,1)}, u32[]{:S(2)}, u32[]{:S(2)}) async-start(bf16[32,2,8,16,128]{4,3,2,1,0:T(8,128)(2,1)} %grid_tile_0.1), calls=%async_computation.1 | async-start | bytes 4194304 | tf_op jit(solution)/shard_map/all_to_all | solution.py:681
  80.2 11.3 %grid_tile_1.1 = bf16[32,2,8,16,128]{4,3,2,1,0:T(8,128)(2,1)} custom-call(s32[1,24]{1,0:T(1,128)S(1)} %copy-done.6, s32[1]{0:T(128)S(6)} %copy.19.counts_ref.refs_1_, bf16[32,2,8,16,128]{4,3,2,1,0:T(8,128)(2,1)S(1)} %all-to-all-done.2.refs_2_, bf16[512,512]{1,0:T(8,128)(2,1)S(1)} %copy-done, bf16[24,128,512]{2,1,0:T(8,128)(2,1)} %bitcast.10, ...), custom_call_target="tpu_custom_call" | custom-call | tf_op jit(solution)/shard_map/grid_tile_1/pallas_call | solution.py:366
  91.5 0.0 copy-start.2
  91.5 17.6 %all-to-all-done.1.piece_hbm = bf16[32,2,8,16,128]{4,3,2,1,0:T(8,128)(2,1)} async-done(((bf16[32,2,8,16,128]{4,3,2,1,0:T(8,128)(2,1)}), bf16[32,2,8,16,128]{4,3,2,1,0:T(8,128)(2,1)}, u32[]{:S(2)}, u32[]{:S(2)}) %all-to-all-start.1) | async-done | bytes 2097184 | tf_op jit(solution)/shard_map/all_to_all | solution.py:681
  109.1 4.2 %all-to-all-start.3 = ((bf16[32,2,8,16,128]{4,3,2,1,0:T(8,128)(2,1)}), bf16[32,2,8,16,128]{4,3,2,1,0:T(8,128)(2,1)S(1)}, u32[]{:S(2)}, u32[]{:S(2)}) async-start(bf16[32,2,8,16,128]{4,3,2,1,0:T(8,128)(2,1)} %grid_tile_1.1), calls=%async_computation.3 | async-start | bytes 4194304 | tf_op jit(solution)/shard_map/all_to_all | solution.py:681
  113.3 0.0 copy-done.2
  113.3 7.8 %gradient_first.1 = (bf16[8,64,128]{2,1,0:T(8,128)(2,1)}, bf16[8,64,128]{2,1,0:T(8,128)(2,1)}, bf16[8,64,128]{2,1,0:T(8,128)(2,1)}, bf16[8,64,128]{2,1,0:T(8,128)(2,1)}, bf16[2,2,8,256,128]{4,3,2,1,0:T(8,128)(2,1)}) custom-call(s32[1]{0:T(128)} %bitcast.position_ref, bf16[512,512]{1,0:T(8,128)(2,1)S(1)} %bitcast.7, ...), custom_call_target="tpu_custom_call" | custom-call | tf_op jit(solution)/shard_map/gradient_first/pallas_call | solution.py:454
  121.1 4.0 %collective-permute-start = (bf16[8,64,128]{2,1,0:T(8,128)(2,1)}, bf16[8,64,128]{2,1,0:T(8,128)(2,1)S(1)}, u32[]{:S(2)}, u32[]{:S(2)}) collective-permute-start(bf16[8,64,128]{2,1,0:T(8,128)(2,1)} %get-tuple-element.22), channel_id=1, source_target_pairs={{0,64},{32,96},{64,0},{96,32},{1,65},{33,97},{65,1},{97,33},{2,66}... | collective-permute-start | bytes 393224 | tf_op jit(solution)/shard_map/ppermute | solution.py:644
  125.1 1.0 collective-permute-start.1
  126.1 2.2 %collective-permute-start.2 = (bf16[8,64,128]{2,1,0:T(8,128)(2,1)}, bf16[8,64,128]{2,1,0:T(8,128)(2,1)S(1)}, u32[]{:S(2)}, u32[]{:S(2)}) collective-permute-start(bf16[8,64,128]{2,1,0:T(8,128)(2,1)} %get-tuple-element.24), channel_id=1, source_target_pairs={{0,96},{32,0},{64,32},{96,64},{1,97},{33,1},{65,33},{97,65},{2,98}... | collective-permute-start | bytes 393224 | tf_op jit(solution)/shard_map/ppermute | solution.py:644
  128.3 13.7 %all-to-all-done.3.piece = bf16[32,2,8,16,128]{4,3,2,1,0:T(8,128)(2,1)S(1)} async-done(((bf16[32,2,8,16,128]{4,3,2,1,0:T(8,128)(2,1)}), bf16[32,2,8,16,128]{4,3,2,1,0:T(8,128)(2,1)S(1)}, u32[]{:S(2)}, u32[]{:S(2)}) %all-to-all-start.3) | async-done | bytes 2097184 | tf_op jit(solution)/shard_map/all_to_all | solution.py:681
  142.0 0.0 copy-start.1
  142.0 0.0 copy-start.3
  142.0 0.0 copy-start.4
  142.0 3.6 %gradient_last.1 = (bf16[8,64,128]{2,1,0:T(8,128)(2,1)}, bf16[8,64,128]{2,1,0:T(8,128)(2,1)}, bf16[8,64,128]{2,1,0:T(8,128)(2,1)}, bf16[8,64,128]{2,1,0:T(8,128)(2,1)}) custom-call(s32[1]{0:T(128)} %bitcast.position_ref, bf16[512,512]{1,0:T(8,128)(2,1)S(1)} %bitcast.8, bf16[32,2,8,16,128]{4,3,2,1,0:T(8,128)(2,1)S(1)} %all-to-all-done.3.piece, ...), custom_call_target="tpu_custom_call" | custom-call | tf_op jit(solution)/shard_map/gradient_last/pallas_call | solution.py:507
  145.6 4.0 %collective-permute-start.3 = (bf16[8,64,128]{2,1,0:T(8,128)(2,1)}, bf16[8,64,128]{2,1,0:T(8,128)(2,1)S(1)}, u32[]{:S(2)}, u32[]{:S(2)}) collective-permute-start(bf16[8,64,128]{2,1,0:T(8,128)(2,1)} %get-tuple-element.28), channel_id=1, source_target_pairs={{0,64},{32,96},{64,0},{96,32},{1,65},{33,97},{65,1},{97,33},{2,66}... | collective-permute-start | bytes 393224 | tf_op jit(solution)/shard_map/ppermute | solution.py:644
  149.6 1.0 collective-permute-start.4
  150.6 0.0 collective-permute-done.rest_1_
  150.6 2.2 %collective-permute-start.5 = (bf16[8,64,128]{2,1,0:T(8,128)(2,1)}, bf16[8,64,128]{2,1,0:T(8,128)(2,1)S(1)}, u32[]{:S(2)}, u32[]{:S(2)}) collective-permute-start(bf16[8,64,128]{2,1,0:T(8,128)(2,1)} %get-tuple-element.30), channel_id=1, source_target_pairs={{0,96},{32,0},{64,32},{96,64},{1,97},{33,1},{65,33},{97,65},{2,98}... | collective-permute-start | bytes 393224 | tf_op jit(solution)/shard_map/ppermute | solution.py:644
  152.8 0.0 collective-permute-done.1.rest_2_
  152.8 0.0 collective-permute-done.2.rest_3_
  152.8 0.0 copy-done.1
  152.8 0.0 copy-done.3
  152.8 0.0 copy-done.4
  152.9 0.0 copy-start.5
  152.9 0.9 copy-done.5
  153.8 1.4 target.1.base_ref
  155.2 0.0 collective-permute-done.3.rest_0_
  155.2 1.2 collective-permute-done.4.rest_1_
  156.4 0.3 collective-permute-done.5.rest_2_
  156.6 1.4 update.1
Async XLA Ops:
  5.9 36.5 %all-to-all-start = ((bf16[32,2,8,16,128]{4,3,2,1,0:T(8,128)(2,1)}), bf16[32,2,8,16,128]{4,3,2,1,0:T(8,128)(2,1)}, u32[]{:S(2)}, u32[]{:S(2)}) async-start(bf16[32,2,8,16,128]{4,3,2,1,0:T(8,128)(2,1)} %coil_forward_0.1), calls=%async_computation | async-start | bytes 4194304 | tf_op jit(solution)/shard_map/all_to_all | solution.py:666
  13.5 7.7 %copy-start.7 = (bf16[1,24,128,512]{3,2,1,0:T(8,128)(2,1)S(1)}, bf16[1,24,128,512]{3,2,1,0:T(8,128)(2,1)}, u32[]{:S(2)}) copy-start(bf16[1,24,128,512]{3,2,1,0:T(8,128)(2,1)} %param.12) | copy-start | bytes 9437188
  42.4 4.2 %copy-start = (bf16[512,512]{1,0:T(8,128)(2,1)S(1)}, bf16[512,512]{1,0:T(8,128)(2,1)}, u32[]{:S(2)}) copy-start(bf16[512,512]{1,0:T(8,128)(2,1)} %constant.11.clone.refs_3_) | copy-start | bytes 1572868
  42.4 4.2 %copy-start.6 = (s32[1,24]{1,0:T(1,128)S(1)}, s32[1,24]{1,0:T(1,128)}, u32[]{:S(2)}) copy-start(s32[1,24]{1,0:T(1,128)} %refs_0_.5) | copy-start | bytes 292
  42.4 33.0 %all-to-all-start.2 = ((bf16[32,2,8,16,128]{4,3,2,1,0:T(8,128)(2,1)}), bf16[32,2,8,16,128]{4,3,2,1,0:T(8,128)(2,1)S(1)}, u32[]{:S(2)}, u32[]{:S(2)}) async-start(bf16[32,2,8,16,128]{4,3,2,1,0:T(8,128)(2,1)} %coil_forward_1.1), calls=%async_computation.2 | async-start | bytes 4194304 | tf_op jit(solution)/shard_map/all_to_all | solution.py:666
  75.4 33.6 %all-to-all-start.1 = ((bf16[32,2,8,16,128]{4,3,2,1,0:T(8,128)(2,1)}), bf16[32,2,8,16,128]{4,3,2,1,0:T(8,128)(2,1)}, u32[]{:S(2)}, u32[]{:S(2)}) async-start(bf16[32,2,8,16,128]{4,3,2,1,0:T(8,128)(2,1)} %grid_tile_0.1), calls=%async_computation.1 | async-start | bytes 4194304 | tf_op jit(solution)/shard_map/all_to_all | solution.py:681
  91.5 21.8 %copy-start.2 = (bf16[512,512]{0,1:T(8,128)(2,1)S(1)}, bf16[512,512]{0,1:T(8,128)(2,1)}, u32[]{:S(2)}) copy-start(bf16[512,512]{0,1:T(8,128)(2,1)} %constant.10.clone) | copy-start | bytes 1572868
  109.1 32.9 %all-to-all-start.3 = ((bf16[32,2,8,16,128]{4,3,2,1,0:T(8,128)(2,1)}), bf16[32,2,8,16,128]{4,3,2,1,0:T(8,128)(2,1)S(1)}, u32[]{:S(2)}, u32[]{:S(2)}) async-start(bf16[32,2,8,16,128]{4,3,2,1,0:T(8,128)(2,1)} %grid_tile_1.1), calls=%async_computation.3 | async-start | bytes 4194304 | tf_op jit(solution)/shard_map/all_to_all | solution.py:681
  121.1 29.5 %collective-permute-start = (bf16[8,64,128]{2,1,0:T(8,128)(2,1)}, bf16[8,64,128]{2,1,0:T(8,128)(2,1)S(1)}, u32[]{:S(2)}, u32[]{:S(2)}) collective-permute-start(bf16[8,64,128]{2,1,0:T(8,128)(2,1)} %get-tuple-element.22), channel_id=1, source_target_pairs={{0,64},{32,96},{64,0},{96,32},{1,65},{33,97},{65,1},{97,33},{2,66}... | collective-permute-start | bytes 393224 | tf_op jit(solution)/shard_map/ppermute | solution.py:644
  125.1 27.7 %collective-permute-start.1 = (bf16[8,64,128]{2,1,0:T(8,128)(2,1)}, bf16[8,64,128]{2,1,0:T(8,128)(2,1)S(1)}, u32[]{:S(2)}, u32[]{:S(2)}) collective-permute-start(bf16[8,64,128]{2,1,0:T(8,128)(2,1)} %get-tuple-element.23), channel_id=1, source_target_pairs={{0,32},{32,64},{64,96},{96,0},{1,33},{33,65},{65,97},{97,1},{2,34}... | collective-permute-start | bytes 393224 | tf_op jit(solution)/shard_map/ppermute | solution.py:644
  126.1 26.7 %collective-permute-start.2 = (bf16[8,64,128]{2,1,0:T(8,128)(2,1)}, bf16[8,64,128]{2,1,0:T(8,128)(2,1)S(1)}, u32[]{:S(2)}, u32[]{:S(2)}) collective-permute-start(bf16[8,64,128]{2,1,0:T(8,128)(2,1)} %get-tuple-element.24), channel_id=1, source_target_pairs={{0,96},{32,0},{64,32},{96,64},{1,97},{33,1},{65,33},{97,65},{2,98}... | collective-permute-start | bytes 393224 | tf_op jit(solution)/shard_map/ppermute | solution.py:644
  142.0 10.8 %copy-start.1 = (f32[2,8,64,128]{3,2,1,0:T(8,128)S(1)}, f32[2,8,64,128]{3,2,1,0:T(8,128)}, u32[]{:S(2)}) copy-start(f32[2,8,64,128]{3,2,1,0:T(8,128)} %rest_3_.1) | copy-start | bytes 1572868
  142.0 10.8 %copy-start.3 = (f32[2,8,64,128]{3,2,1,0:T(8,128)S(1)}, f32[2,8,64,128]{3,2,1,0:T(8,128)}, u32[]{:S(2)}) copy-start(f32[2,8,64,128]{3,2,1,0:T(8,128)} %aux_ref.1) | copy-start | bytes 1572868
  142.0 10.8 %copy-start.4 = (bf16[8,64,128]{2,1,0:T(8,128)(2,1)S(1)}, bf16[8,64,128]{2,1,0:T(8,128)(2,1)}, u32[]{:S(2)}) copy-start(bf16[8,64,128]{2,1,0:T(8,128)(2,1)} %get-tuple-element.21.rest_0_) | copy-start | bytes 393220
  145.6 9.6 %collective-permute-start.3 = (bf16[8,64,128]{2,1,0:T(8,128)(2,1)}, bf16[8,64,128]{2,1,0:T(8,128)(2,1)S(1)}, u32[]{:S(2)}, u32[]{:S(2)}) collective-permute-start(bf16[8,64,128]{2,1,0:T(8,128)(2,1)} %get-tuple-element.28), channel_id=1, source_target_pairs={{0,64},{32,96},{64,0},{96,32},{1,65},{33,97},{65,1},{97,33},{2,66}... | collective-permute-start | bytes 393224 | tf_op jit(solution)/shard_map/ppermute | solution.py:644
  149.6 6.8 %collective-permute-start.4 = (bf16[8,64,128]{2,1,0:T(8,128)(2,1)}, bf16[8,64,128]{2,1,0:T(8,128)(2,1)S(1)}, u32[]{:S(2)}, u32[]{:S(2)}) collective-permute-start(bf16[8,64,128]{2,1,0:T(8,128)(2,1)} %get-tuple-element.29), channel_id=1, source_target_pairs={{0,32},{32,64},{64,96},{96,0},{1,33},{33,65},{65,97},{97,1},{2,34}... | collective-permute-start | bytes 393224 | tf_op jit(solution)/shard_map/ppermute | solution.py:644
  150.6 6.0 %collective-permute-start.5 = (bf16[8,64,128]{2,1,0:T(8,128)(2,1)}, bf16[8,64,128]{2,1,0:T(8,128)(2,1)S(1)}, u32[]{:S(2)}, u32[]{:S(2)}) collective-permute-start(bf16[8,64,128]{2,1,0:T(8,128)(2,1)} %get-tuple-element.30), channel_id=1, source_target_pairs={{0,96},{32,0},{64,32},{96,64},{1,97},{33,1},{65,33},{97,65},{2,98}... | collective-permute-start | bytes 393224 | tf_op jit(solution)/shard_map/ppermute | solution.py:644
  152.9 0.9 copy-start.5

commit v9 on v8

--- a/solution.py
+++ b/solution.py
@@ -601,6 +601,10 @@
                 value = base_ref[part, x] - step_size * gradient[part]
                 image[part, x] = value
                 rows[part].append(value)
+        pair = pl.ds(2 * m, 2)
+        copy = pltpu.make_async_copy(image.at[:, pair], image_hbm.at[:, pair], sems.at[0, m])
+        copy.start()
+        leaving.append(copy)
         coeffs = []
         for part in range(2):
             top, bottom = haar_rows(*rows[part])
@@ -614,8 +618,7 @@
                 kept = value * factor
                 aux[part, 2 * m + i] = kept
                 dual[part, 2 * m + i] = value - kept
-        pair = pl.ds(2 * m, 2)
-        for k, (held, place) in enumerate(((image, image_hbm), (aux, aux_hbm), (dual, dual_hbm))):
+        for k, (held, place) in ((1, (aux, aux_hbm)), (2, (dual, dual_hbm))):
             copy = pltpu.make_async_copy(held.at[:, pair], place.at[:, pair], sems.at[k, m])
             copy.start()
             leaving.append(copy)

time: 159 us -> 159 us (level)
  no operation moved by 1% of the time
where the time goes in v9:
time: 159 us; the launch traced here: 158 us
  waiting for transfers between devices  64.8 us (41%)
  Pallas kernels  53 us (33%)
  starting transfers between devices  35 us (22%)
  local copies, waits for them, and re-layouts  3.78 us (2%)
  between operations  1.63 us (1%)
    all_to_all x2, waiting for transfers between devices, body(): piece = lax.all_to_all(half, 'slab', 0, 0, tiled=True)  32.1 us
    all_to_all x2, waiting for transfers between devices, body(): backs.append(lax.all_to_all(back, 'slab', 0, 0, tiled=True))  31.3 us
    pallas_call x2, Pallas kernels, grid_tile(): pl.pallas_call(kernel, out_shape=hbm((TILES, PER, KYD, 16, Z), BF), in_sp...  24.1 us
    ppermute x6, starting transfers between devices, over_planes(): got.append(lax.ppermute(others[k - 1], 'coil', ring))  14.4 us
    pallas_call x2, Pallas kernels, coil_forward(): pl.pallas_call(kernel, out_shape=hbm((TILES, PER, KYD, 16, Z), BF), in_sp...  12.4 us
    all_to_all x2, starting transfers between devices, body(): piece = lax.all_to_all(half, 'slab', 0, 0, tiled=True)  11.7 us
    all_to_all x2, starting transfers between devices, body(): backs.append(lax.all_to_all(back, 'slab', 0, 0, tiled=True))  8.95 us
    pallas_call x1, Pallas kernels, gradient_first(): pl.pallas_call(gradient_first_kernel, out_shape=(hbm(share, BF),) * NCOIL...  7.82 us
  transfers between devices with their start and end apart: 10, of which 6 were waited for; matrix products, arithmetic and copies ran while one was open for 2% of the time, Pallas kernels for 29%

profile of v9, /device:TPU:0, one launch (start us, length us, event | category | flops | bytes accessed | tf_op | source)
XLA Modules:
  0.0 158.2 jit_solution(9913915816730427550)
XLA Ops:
  0.6 5.3 %coil_forward_0.1 = bf16[32,2,8,16,128]{4,3,2,1,0:T(8,128)(2,1)} custom-call(bf16[512,512]{1,0:T(8,128)(2,1)} %constant.20.refs_0_, bf16[4,2,8,256,128]{4,3,2,1,0:T(8,128)(2,1)} %sens_hbm.1, f32[2,8,256,128]{3,2,1,0:T(8,128)} %image_hbm.1), custom_call_target="tpu_custom_call" | custom-call | tf_op jit(solution)/shard_map/coil_forward_0/pallas_call | solution.py:132
  5.9 7.5 %all-to-all-start = ((bf16[32,2,8,16,128]{4,3,2,1,0:T(8,128)(2,1)}), bf16[32,2,8,16,128]{4,3,2,1,0:T(8,128)(2,1)}, u32[]{:S(2)}, u32[]{:S(2)}) async-start(bf16[32,2,8,16,128]{4,3,2,1,0:T(8,128)(2,1)} %coil_forward_0.1), calls=%async_computation | async-start | bytes 4194304 | tf_op jit(solution)/shard_map/all_to_all | solution.py:669
  13.5 0.0 copy-start.7
  13.5 7.0 %coil_forward_1.1 = bf16[32,2,8,16,128]{4,3,2,1,0:T(8,128)(2,1)} custom-call(bf16[512,512]{1,0:T(8,128)(2,1)} %constant.20.refs_0_, bf16[4,2,8,256,128]{4,3,2,1,0:T(8,128)(2,1)} %sens_hbm.1, f32[2,8,256,128]{3,2,1,0:T(8,128)} %image_hbm.1), custom_call_target="tpu_custom_call" | custom-call | tf_op jit(solution)/shard_map/coil_forward_1/pallas_call | solution.py:132
  21.2 0.0 copy-done.7
  21.2 2.9 %copy.14 = bf16[1,24,128,512]{2,3,1,0:T(8,128)(2,1)} copy(bf16[1,24,128,512]{3,2,1,0:T(8,128)(2,1)S(1)} %copy-done.7) | data formatting | bytes 6291456 | tf_op args[2]
  24.1 2.3 %samples_by_coil.1.refs_6_ = bf16[4,24,128,256]{3,2,1,0:T(8,128)(2,1)} custom-call(s32[1]{0:T(128)S(6)} %copy.19.counts_ref.refs_1_, bf16[24,128,8,128]{3,2,1,0:T(8,128)(2,1)} %bitcast.13), custom_call_target="tpu_custom_call" | custom-call | tf_op jit(solution)/shard_map/samples_by_coil/pallas_call | solution.py:190
  26.4 16.0 %all-to-all-done.refs_2_ = bf16[32,2,8,16,128]{4,3,2,1,0:T(8,128)(2,1)} async-done(((bf16[32,2,8,16,128]{4,3,2,1,0:T(8,128)(2,1)}), bf16[32,2,8,16,128]{4,3,2,1,0:T(8,128)(2,1)}, u32[]{:S(2)}, u32[]{:S(2)}) %all-to-all-start) | async-done | bytes 2097184 | tf_op jit(solution)/shard_map/all_to_all | solution.py:669
  42.4 0.0 copy-start
  42.4 0.0 copy-start.6
  42.4 4.1 %all-to-all-start.2 = ((bf16[32,2,8,16,128]{4,3,2,1,0:T(8,128)(2,1)}), bf16[32,2,8,16,128]{4,3,2,1,0:T(8,128)(2,1)S(1)}, u32[]{:S(2)}, u32[]{:S(2)}) async-start(bf16[32,2,8,16,128]{4,3,2,1,0:T(8,128)(2,1)} %coil_forward_1.1), calls=%async_computation.2 | async-start | bytes 4194304 | tf_op jit(solution)/shard_map/all_to_all | solution.py:669
  46.6 0.0 copy-done
  46.6 0.0 copy-done.6
  46.6 12.8 %grid_tile_0.1 = bf16[32,2,8,16,128]{4,3,2,1,0:T(8,128)(2,1)} custom-call(s32[1,24]{1,0:T(1,128)S(1)} %copy-done.6, s32[1]{0:T(128)S(6)} %copy.19.counts_ref.refs_1_, bf16[32,2,8,16,128]{4,3,2,1,0:T(8,128)(2,1)} %all-to-all-done.refs_2_, bf16[512,512]{1,0:T(8,128)(2,1)S(1)} %copy-done, bf16[24,128,512]{2,1,0:T(8,128)(2,1)} %bitcast.9, ...), custom_call_target="tpu_custom_call" | custom-call | tf_op jit(solution)/shard_map/grid_tile_0/pallas_call | solution.py:366
  59.4 16.1 %all-to-all-done.2.refs_2_ = bf16[32,2,8,16,128]{4,3,2,1,0:T(8,128)(2,1)S(1)} async-done(((bf16[32,2,8,16,128]{4,3,2,1,0:T(8,128)(2,1)}), bf16[32,2,8,16,128]{4,3,2,1,0:T(8,128)(2,1)S(1)}, u32[]{:S(2)}, u32[]{:S(2)}) %all-to-all-start.2) | async-done | bytes 2097184 | tf_op jit(solution)/shard_map/all_to_all | solution.py:669
  75.4 4.8 %all-to-all-start.1 = ((bf16[32,2,8,16,128]{4,3,2,1,0:T(8,128)(2,1)}), bf16[32,2,8,16,128]{4,3,2,1,0:T(8,128)(2,1)}, u32[]{:S(2)}, u32[]{:S(2)}) async-start(bf16[32,2,8,16,128]{4,3,2,1,0:T(8,128)(2,1)} %grid_tile_0.1), calls=%async_computation.1 | async-start | bytes 4194304 | tf_op jit(solution)/shard_map/all_to_all | solution.py:684
  80.2 11.3 %grid_tile_1.1 = bf16[32,2,8,16,128]{4,3,2,1,0:T(8,128)(2,1)} custom-call(s32[1,24]{1,0:T(1,128)S(1)} %copy-done.6, s32[1]{0:T(128)S(6)} %copy.19.counts_ref.refs_1_, bf16[32,2,8,16,128]{4,3,2,1,0:T(8,128)(2,1)S(1)} %all-to-all-done.2.refs_2_, bf16[512,512]{1,0:T(8,128)(2,1)S(1)} %copy-done, bf16[24,128,512]{2,1,0:T(8,128)(2,1)} %bitcast.10, ...), custom_call_target="tpu_custom_call" | custom-call | tf_op jit(solution)/shard_map/grid_tile_1/pallas_call | solution.py:366
  91.5 0.0 copy-start.2
  91.5 17.6 %all-to-all-done.1.piece_hbm = bf16[32,2,8,16,128]{4,3,2,1,0:T(8,128)(2,1)} async-done(((bf16[32,2,8,16,128]{4,3,2,1,0:T(8,128)(2,1)}), bf16[32,2,8,16,128]{4,3,2,1,0:T(8,128)(2,1)}, u32[]{:S(2)}, u32[]{:S(2)}) %all-to-all-start.1) | async-done | bytes 2097184 | tf_op jit(solution)/shard_map/all_to_all | solution.py:684
  109.1 4.2 %all-to-all-start.3 = ((bf16[32,2,8,16,128]{4,3,2,1,0:T(8,128)(2,1)}), bf16[32,2,8,16,128]{4,3,2,1,0:T(8,128)(2,1)S(1)}, u32[]{:S(2)}, u32[]{:S(2)}) async-start(bf16[32,2,8,16,128]{4,3,2,1,0:T(8,128)(2,1)} %grid_tile_1.1), calls=%async_computation.3 | async-start | bytes 4194304 | tf_op jit(solution)/shard_map/all_to_all | solution.py:684
  113.3 0.0 copy-done.2
  113.3 7.8 %gradient_first.1 = (bf16[8,64,128]{2,1,0:T(8,128)(2,1)}, bf16[8,64,128]{2,1,0:T(8,128)(2,1)}, bf16[8,64,128]{2,1,0:T(8,128)(2,1)}, bf16[8,64,128]{2,1,0:T(8,128)(2,1)}, bf16[2,2,8,256,128]{4,3,2,1,0:T(8,128)(2,1)}) custom-call(s32[1]{0:T(128)} %bitcast.position_ref, bf16[512,512]{1,0:T(8,128)(2,1)S(1)} %bitcast.7, ...), custom_call_target="tpu_custom_call" | custom-call | tf_op jit(solution)/shard_map/gradient_first/pallas_call | solution.py:454
  121.1 4.0 %collective-permute-start = (bf16[8,64,128]{2,1,0:T(8,128)(2,1)}, bf16[8,64,128]{2,1,0:T(8,128)(2,1)S(1)}, u32[]{:S(2)}, u32[]{:S(2)}) collective-permute-start(bf16[8,64,128]{2,1,0:T(8,128)(2,1)} %get-tuple-element.22), channel_id=1, source_target_pairs={{0,64},{32,96},{64,0},{96,32},{1,65},{33,97},{65,1},{97,33},{2,66}... | collective-permute-start | bytes 393224 | tf_op jit(solution)/shard_map/ppermute | solution.py:647
  125.1 1.0 collective-permute-start.1
  126.1 2.2 %collective-permute-start.2 = (bf16[8,64,128]{2,1,0:T(8,128)(2,1)}, bf16[8,64,128]{2,1,0:T(8,128)(2,1)S(1)}, u32[]{:S(2)}, u32[]{:S(2)}) collective-permute-start(bf16[8,64,128]{2,1,0:T(8,128)(2,1)} %get-tuple-element.24), channel_id=1, source_target_pairs={{0,96},{32,0},{64,32},{96,64},{1,97},{33,1},{65,33},{97,65},{2,98}... | collective-permute-start | bytes 393224 | tf_op jit(solution)/shard_map/ppermute | solution.py:647
  128.3 13.7 %all-to-all-done.3.piece = bf16[32,2,8,16,128]{4,3,2,1,0:T(8,128)(2,1)S(1)} async-done(((bf16[32,2,8,16,128]{4,3,2,1,0:T(8,128)(2,1)}), bf16[32,2,8,16,128]{4,3,2,1,0:T(8,128)(2,1)S(1)}, u32[]{:S(2)}, u32[]{:S(2)}) %all-to-all-start.3) | async-done | bytes 2097184 | tf_op jit(solution)/shard_map/all_to_all | solution.py:684
  142.0 0.0 copy-start.1
  142.0 0.0 copy-start.3
  142.0 0.0 copy-start.4
  142.0 3.6 %gradient_last.1 = (bf16[8,64,128]{2,1,0:T(8,128)(2,1)}, bf16[8,64,128]{2,1,0:T(8,128)(2,1)}, bf16[8,64,128]{2,1,0:T(8,128)(2,1)}, bf16[8,64,128]{2,1,0:T(8,128)(2,1)}) custom-call(s32[1]{0:T(128)} %bitcast.position_ref, bf16[512,512]{1,0:T(8,128)(2,1)S(1)} %bitcast.8, bf16[32,2,8,16,128]{4,3,2,1,0:T(8,128)(2,1)S(1)} %all-to-all-done.3.piece, ...), custom_call_target="tpu_custom_call" | custom-call | tf_op jit(solution)/shard_map/gradient_last/pallas_call | solution.py:507
  145.6 4.0 %collective-permute-start.3 = (bf16[8,64,128]{2,1,0:T(8,128)(2,1)}, bf16[8,64,128]{2,1,0:T(8,128)(2,1)S(1)}, u32[]{:S(2)}, u32[]{:S(2)}) collective-permute-start(bf16[8,64,128]{2,1,0:T(8,128)(2,1)} %get-tuple-element.28), channel_id=1, source_target_pairs={{0,64},{32,96},{64,0},{96,32},{1,65},{33,97},{65,1},{97,33},{2,66}... | collective-permute-start | bytes 393224 | tf_op jit(solution)/shard_map/ppermute | solution.py:647
  149.6 1.0 collective-permute-start.4
  150.6 0.0 collective-permute-done.rest_1_
  150.6 2.2 %collective-permute-start.5 = (bf16[8,64,128]{2,1,0:T(8,128)(2,1)}, bf16[8,64,128]{2,1,0:T(8,128)(2,1)S(1)}, u32[]{:S(2)}, u32[]{:S(2)}) collective-permute-start(bf16[8,64,128]{2,1,0:T(8,128)(2,1)} %get-tuple-element.30), channel_id=1, source_target_pairs={{0,96},{32,0},{64,32},{96,64},{1,97},{33,1},{65,33},{97,65},{2,98}... | collective-permute-start | bytes 393224 | tf_op jit(solution)/shard_map/ppermute | solution.py:647
  152.8 0.0 collective-permute-done.1.rest_2_
  152.8 0.0 collective-permute-done.2.rest_3_
  152.8 0.0 copy-done.1
  152.8 0.0 copy-done.3
  152.8 0.0 copy-done.4
  152.9 0.0 copy-start.5
  152.9 0.9 copy-done.5
  153.8 1.4 target.1.base_ref
  155.2 0.0 collective-permute-done.3.rest_0_
  155.2 1.2 collective-permute-done.4.rest_1_
  156.4 0.3 collective-permute-done.5.rest_2_
  156.6 1.4 update.1
Async XLA Ops:
  5.9 36.5 %all-to-all-start = ((bf16[32,2,8,16,128]{4,3,2,1,0:T(8,128)(2,1)}), bf16[32,2,8,16,128]{4,3,2,1,0:T(8,128)(2,1)}, u32[]{:S(2)}, u32[]{:S(2)}) async-start(bf16[32,2,8,16,128]{4,3,2,1,0:T(8,128)(2,1)} %coil_forward_0.1), calls=%async_computation | async-start | bytes 4194304 | tf_op jit(solution)/shard_map/all_to_all | solution.py:669
  13.5 7.7 %copy-start.7 = (bf16[1,24,128,512]{3,2,1,0:T(8,128)(2,1)S(1)}, bf16[1,24,128,512]{3,2,1,0:T(8,128)(2,1)}, u32[]{:S(2)}) copy-start(bf16[1,24,128,512]{3,2,1,0:T(8,128)(2,1)} %param.12) | copy-start | bytes 9437188
  42.4 4.2 %copy-start = (bf16[512,512]{1,0:T(8,128)(2,1)S(1)}, bf16[512,512]{1,0:T(8,128)(2,1)}, u32[]{:S(2)}) copy-start(bf16[512,512]{1,0:T(8,128)(2,1)} %constant.11.clone.refs_3_) | copy-start | bytes 1572868
  42.4 4.2 %copy-start.6 = (s32[1,24]{1,0:T(1,128)S(1)}, s32[1,24]{1,0:T(1,128)}, u32[]{:S(2)}) copy-start(s32[1,24]{1,0:T(1,128)} %refs_0_.5) | copy-start | bytes 292
  42.4 33.0 %all-to-all-start.2 = ((bf16[32,2,8,16,128]{4,3,2,1,0:T(8,128)(2,1)}), bf16[32,2,8,16,128]{4,3,2,1,0:T(8,128)(2,1)S(1)}, u32[]{:S(2)}, u32[]{:S(2)}) async-start(bf16[32,2,8,16,128]{4,3,2,1,0:T(8,128)(2,1)} %coil_forward_1.1), calls=%async_computation.2 | async-start | bytes 4194304 | tf_op jit(solution)/shard_map/all_to_all | solution.py:669
  75.4 33.6 %all-to-all-start.1 = ((bf16[32,2,8,16,128]{4,3,2,1,0:T(8,128)(2,1)}), bf16[32,2,8,16,128]{4,3,2,1,0:T(8,128)(2,1)}, u32[]{:S(2)}, u32[]{:S(2)}) async-start(bf16[32,2,8,16,128]{4,3,2,1,0:T(8,128)(2,1)} %grid_tile_0.1), calls=%async_computation.1 | async-start | bytes 4194304 | tf_op jit(solution)/shard_map/all_to_all | solution.py:684
  91.5 21.8 %copy-start.2 = (bf16[512,512]{0,1:T(8,128)(2,1)S(1)}, bf16[512,512]{0,1:T(8,128)(2,1)}, u32[]{:S(2)}) copy-start(bf16[512,512]{0,1:T(8,128)(2,1)} %constant.10.clone) | copy-start | bytes 1572868
  109.1 32.9 %all-to-all-start.3 = ((bf16[32,2,8,16,128]{4,3,2,1,0:T(8,128)(2,1)}), bf16[32,2,8,16,128]{4,3,2,1,0:T(8,128)(2,1)S(1)}, u32[]{:S(2)}, u32[]{:S(2)}) async-start(bf16[32,2,8,16,128]{4,3,2,1,0:T(8,128)(2,1)} %grid_tile_1.1), calls=%async_computation.3 | async-start | bytes 4194304 | tf_op jit(solution)/shard_map/all_to_all | solution.py:684
  121.1 29.5 %collective-permute-start = (bf16[8,64,128]{2,1,0:T(8,128)(2,1)}, bf16[8,64,128]{2,1,0:T(8,128)(2,1)S(1)}, u32[]{:S(2)}, u32[]{:S(2)}) collective-permute-start(bf16[8,64,128]{2,1,0:T(8,128)(2,1)} %get-tuple-element.22), channel_id=1, source_target_pairs={{0,64},{32,96},{64,0},{96,32},{1,65},{33,97},{65,1},{97,33},{2,66}... | collective-permute-start | bytes 393224 | tf_op jit(solution)/shard_map/ppermute | solution.py:647
  125.1 27.7 %collective-permute-start.1 = (bf16[8,64,128]{2,1,0:T(8,128)(2,1)}, bf16[8,64,128]{2,1,0:T(8,128)(2,1)S(1)}, u32[]{:S(2)}, u32[]{:S(2)}) collective-permute-start(bf16[8,64,128]{2,1,0:T(8,128)(2,1)} %get-tuple-element.23), channel_id=1, source_target_pairs={{0,32},{32,64},{64,96},{96,0},{1,33},{33,65},{65,97},{97,1},{2,34}... | collective-permute-start | bytes 393224 | tf_op jit(solution)/shard_map/ppermute | solution.py:647
  126.1 26.7 %collective-permute-start.2 = (bf16[8,64,128]{2,1,0:T(8,128)(2,1)}, bf16[8,64,128]{2,1,0:T(8,128)(2,1)S(1)}, u32[]{:S(2)}, u32[]{:S(2)}) collective-permute-start(bf16[8,64,128]{2,1,0:T(8,128)(2,1)} %get-tuple-element.24), channel_id=1, source_target_pairs={{0,96},{32,0},{64,32},{96,64},{1,97},{33,1},{65,33},{97,65},{2,98}... | collective-permute-start | bytes 393224 | tf_op jit(solution)/shard_map/ppermute | solution.py:647
  142.0 10.8 %copy-start.1 = (f32[2,8,64,128]{3,2,1,0:T(8,128)S(1)}, f32[2,8,64,128]{3,2,1,0:T(8,128)}, u32[]{:S(2)}) copy-start(f32[2,8,64,128]{3,2,1,0:T(8,128)} %rest_3_.1) | copy-start | bytes 1572868
  142.0 10.8 %copy-start.3 = (f32[2,8,64,128]{3,2,1,0:T(8,128)S(1)}, f32[2,8,64,128]{3,2,1,0:T(8,128)}, u32[]{:S(2)}) copy-start(f32[2,8,64,128]{3,2,1,0:T(8,128)} %aux_ref.1) | copy-start | bytes 1572868
  142.0 10.8 %copy-start.4 = (bf16[8,64,128]{2,1,0:T(8,128)(2,1)S(1)}, bf16[8,64,128]{2,1,0:T(8,128)(2,1)}, u32[]{:S(2)}) copy-start(bf16[8,64,128]{2,1,0:T(8,128)(2,1)} %get-tuple-element.21.rest_0_) | copy-start | bytes 393220
  145.6 9.6 %collective-permute-start.3 = (bf16[8,64,128]{2,1,0:T(8,128)(2,1)}, bf16[8,64,128]{2,1,0:T(8,128)(2,1)S(1)}, u32[]{:S(2)}, u32[]{:S(2)}) collective-permute-start(bf16[8,64,128]{2,1,0:T(8,128)(2,1)} %get-tuple-element.28), channel_id=1, source_target_pairs={{0,64},{32,96},{64,0},{96,32},{1,65},{33,97},{65,1},{97,33},{2,66}... | collective-permute-start | bytes 393224 | tf_op jit(solution)/shard_map/ppermute | solution.py:647
  149.6 6.8 %collective-permute-start.4 = (bf16[8,64,128]{2,1,0:T(8,128)(2,1)}, bf16[8,64,128]{2,1,0:T(8,128)(2,1)S(1)}, u32[]{:S(2)}, u32[]{:S(2)}) collective-permute-start(bf16[8,64,128]{2,1,0:T(8,128)(2,1)} %get-tuple-element.29), channel_id=1, source_target_pairs={{0,32},{32,64},{64,96},{96,0},{1,33},{33,65},{65,97},{97,1},{2,34}... | collective-permute-start | bytes 393224 | tf_op jit(solution)/shard_map/ppermute | solution.py:647
  150.6 6.0 %collective-permute-start.5 = (bf16[8,64,128]{2,1,0:T(8,128)(2,1)}, bf16[8,64,128]{2,1,0:T(8,128)(2,1)S(1)}, u32[]{:S(2)}, u32[]{:S(2)}) collective-permute-start(bf16[8,64,128]{2,1,0:T(8,128)(2,1)} %get-tuple-element.30), channel_id=1, source_target_pairs={{0,96},{32,0},{64,32},{96,64},{1,97},{33,1},{65,33},{97,65},{2,98}... | collective-permute-start | bytes 393224 | tf_op jit(solution)/shard_map/ppermute | solution.py:647
  152.9 0.9 copy-start.5
